TPU v7x, 32 devices: a whole 2x2x4 slice. The times are simulated.
32 devices in a mesh: groups: 2 (over y), seq: 4 (over z), head: 2 (over x), sub: 2 (over core).
Axes of the slice: x: 2, y: 2, z: 4, core: 2. Of those that a mesh axis runs over, the one named last changes fastest.
Arguments:
- queries: bfloat16 [3072, 8192], P(('groups', 'seq', 'head', 'sub')), parts along dimension 0, may hold values from -128 to 128
- new_keys: bfloat16 [3072, 8192], P(('groups', 'seq', 'head', 'sub')), parts along dimension 0, may hold values from -4 to 4
- new_values: bfloat16 [3072, 8192], P(('groups', 'seq', 'head', 'sub')), parts along dimension 0, may hold values from -6 to 6
- key_cache: bfloat16 [2048, 8192], P(('groups', 'seq'), ('head', 'sub')), parts along dimension 0, may hold values from -6 to 6
- value_cache: bfloat16 [2048, 8192], P(('groups', 'seq'), ('head', 'sub')), parts along dimension 0, may hold values from -6 to 6
- selection: int32 [8, 2], P('groups'), parts along dimension 0, may hold values from 0 to 15, as said below
Outputs:
- attended: bfloat16 [3072, 8192], P(('groups', 'seq', 'head', 'sub')), parts along dimension 0
There are 2 independent parts, one for each index of `groups`. A program takes and returns all parts, laid end to end along the dimension named above; each array names one. Nothing has to cross between parts.
Inputs may be any that keep to these rules, and one draw needn't show every extreme that they name: `selection`: each row names 2 blocks that lie on 2 different indices of seq: the values block // 4 of a row are distinct. Every row names block 15.
All inputs are finite; a program needn't handle non-finite values.
Results may differ from a plain program's by a relative error of at most 0.0033.
Values may be sent and summed in bfloat16 or wider, within the bound.
No kernel may reach another device: no remote copies, remote signals or barrier semaphores. Data moves between devices by JAX's collectives and lax.ppermute only.
A program may use at most 64 MiB of HBM per device.

v0:
```python
import jax
import jax.numpy as jnp
from jax import lax
from jax.sharding import PartitionSpec as P

HD = 128
BLOCK = 64


def split_heads(rows_array, width):
    count = rows_array.shape[0]
    return rows_array.reshape(count, -1, width).transpose(1, 0, 2)


def per_device(queries, new_keys, new_values, key_cache, value_cache, selection):
    q_rows, k_rows, v_rows = (
        lax.all_to_all(queries, ("head", "sub"), split_axis=1, concat_axis=0, tiled=True),
        lax.all_to_all(new_keys, ("head", "sub"), split_axis=1, concat_axis=0, tiled=True),
        lax.all_to_all(new_values, ("head", "sub"), split_axis=1, concat_axis=0, tiled=True),
    )
    width = HD
    scale = float(width) ** (-0.5)
    q_heads = split_heads(q_rows, width)
    k_heads = split_heads(k_rows, width)
    v_heads = split_heads(v_rows, width)
    count = q_rows.shape[0]
    causal = lax.broadcasted_iota(jnp.int32, (count, count), 0) >= lax.broadcasted_iota(
        jnp.int32, (count, count), 1
    )

    def local_scores(pair):
        query_one, key_one = pair
        raw = jnp.dot(query_one, key_one.T, preferred_element_type=jnp.float32) * scale
        return jnp.where(causal, raw, jnp.float32(-1e30))

    me = lax.axis_index("seq")
    blk_dev = key_cache.shape[0] // BLOCK
    owner_of = selection // blk_dev
    matched = owner_of == me
    wanted = jnp.any(matched, axis=1)
    inner = jnp.sum(jnp.where(matched, selection % blk_dev, 0), axis=1)
    cache_k = key_cache.reshape(blk_dev, BLOCK, -1)
    cache_v = value_cache.reshape(blk_dev, BLOCK, -1)
    send_k = jnp.where(wanted[:, None, None], cache_k[inner], jnp.zeros((), jnp.bfloat16))
    send_v = jnp.where(wanted[:, None, None], cache_v[inner], jnp.zeros((), jnp.bfloat16))
    got_k, got_v = (
        lax.all_to_all(send_k, "seq", split_axis=0, concat_axis=0, tiled=True),
        lax.all_to_all(send_v, "seq", split_axis=0, concat_axis=0, tiled=True),
    )
    my_owners = lax.dynamic_index_in_dim(selection, me, 0, keepdims=False) // blk_dev
    fetched_k = split_heads(got_k[my_owners].reshape(-1, got_k.shape[2]), width)
    fetched_v = split_heads(got_v[my_owners].reshape(-1, got_v.shape[2]), width)

    def attend(query_one, value_one, remote_k, remote_v, own_scores):
        remote_scores = jnp.dot(query_one, remote_k.T, preferred_element_type=jnp.float32) * scale
        top = jnp.maximum(
            jnp.max(own_scores, axis=1, keepdims=True),
            jnp.max(remote_scores, axis=1, keepdims=True),
        )
        own_weights = jnp.exp(own_scores - top)
        remote_weights = jnp.exp(remote_scores - top)
        total = jnp.sum(own_weights, axis=1, keepdims=True) + jnp.sum(
            remote_weights, axis=1, keepdims=True
        )
        mixed = jnp.dot(
            own_weights.astype(jnp.bfloat16), value_one, preferred_element_type=jnp.float32
        )
        mixed = mixed + jnp.dot(
            remote_weights.astype(jnp.bfloat16), remote_v, preferred_element_type=jnp.float32
        )
        return (mixed / total).astype(jnp.bfloat16)

    def per_head(items):
        query_one, key_one, value_one, remote_k, remote_v = items
        return attend(query_one, value_one, remote_k, remote_v, local_scores((query_one, key_one)))

    result = lax.map(per_head, (q_heads, k_heads, v_heads, fetched_k, fetched_v))
    joined = result.transpose(1, 0, 2).reshape(count, -1)
    return lax.all_to_all(joined, ("head", "sub"), split_axis=0, concat_axis=1, tiled=True)


def solution(mesh):
    placed = (
        P(("groups", "seq", "head", "sub"), None),
        P(("groups", "seq", "head", "sub"), None),
        P(("groups", "seq", "head", "sub"), None),
        P(("groups", "seq"), ("head", "sub")),
        P(("groups", "seq"), ("head", "sub")),
        P("groups", None),
    )
    return jax.shard_map(
        per_device,
        mesh=mesh,
        in_specs=placed,
        out_specs=P(("groups", "seq", "head", "sub"), None),
        check_vma=False,
    )
```

profile of v0, /device:TPU:0, one launch (start us, length us, event | category | flops | bytes accessed | tf_op | source)
XLA Modules:
  0.0 226.7 jit_solution(10549713549970579454)
XLA Ops:
  0.0 2.8 %copy.40 = bf16[12,4,8,2048]{3,2,0,1:T(8,128)(2,1)} copy(bf16[12,4,8,2048]{3,2,1,0:T(8,128)(2,1)} %bitcast.118) | data formatting | bytes 3145728 | tf_op jit(solution)/shard_map/all_to_all | solution.py:17
  2.8 4.2 %all-to-all-start = ((bf16[96,4,2048]{2,0,1:T(8,128)(2,1)}), bf16[96,4,2048]{2,0,1:T(8,128)(2,1)S(1)}, u32[]{:S(2)}, u32[]{:S(2)}) async-start(bf16[96,4,2048]{2,0,1:T(8,128)(2,1)} %bitcast.109), calls=%async_computation | async-start | bytes 3145728 | tf_op jit(solution)/shard_map/all_to_all | solution.py:17
  7.1 2.7 %copy.39 = bf16[12,4,8,2048]{3,2,0,1:T(8,128)(2,1)} copy(bf16[12,4,8,2048]{3,2,1,0:T(8,128)(2,1)} %bitcast.119) | data formatting | bytes 3145728 | tf_op jit(solution)/shard_map/all_to_all | solution.py:18
  9.8 17.3 %all-to-all-done = bf16[96,4,2048]{2,0,1:T(8,128)(2,1)S(1)} async-done(((bf16[96,4,2048]{2,0,1:T(8,128)(2,1)}), bf16[96,4,2048]{2,0,1:T(8,128)(2,1)S(1)}, u32[]{:S(2)}, u32[]{:S(2)}) %all-to-all-start) | async-done | bytes 1572896 | tf_op jit(solution)/shard_map/all_to_all | solution.py:17
  27.1 4.3 %all-to-all-start.1 = ((bf16[96,4,2048]{2,0,1:T(8,128)(2,1)}), bf16[96,4,2048]{2,0,1:T(8,128)(2,1)}, u32[]{:S(2)}, u32[]{:S(2)}) async-start(bf16[96,4,2048]{2,0,1:T(8,128)(2,1)} %bitcast.108), calls=%async_computation.1 | async-start | bytes 3145728 | tf_op jit(solution)/shard_map/all_to_all | solution.py:18
  31.5 2.7 %copy.38 = bf16[12,4,8,2048]{3,2,0,1:T(8,128)(2,1)} copy(bf16[12,4,8,2048]{3,2,1,0:T(8,128)(2,1)} %bitcast.120) | data formatting | bytes 3145728 | tf_op jit(solution)/shard_map/all_to_all | solution.py:19
  34.2 17.4 %all-to-all-done.1 = bf16[96,4,2048]{2,0,1:T(8,128)(2,1)} async-done(((bf16[96,4,2048]{2,0,1:T(8,128)(2,1)}), bf16[96,4,2048]{2,0,1:T(8,128)(2,1)}, u32[]{:S(2)}, u32[]{:S(2)}) %all-to-all-start.1) | async-done | bytes 1572896 | tf_op jit(solution)/shard_map/all_to_all | solution.py:18
  51.6 4.5 %all-to-all-start.3 = ((bf16[96,4,2048]{2,0,1:T(8,128)(2,1)}), bf16[96,4,2048]{2,0,1:T(8,128)(2,1)}, u32[]{:S(2)}, u32[]{:S(2)}) async-start(bf16[96,4,2048]{2,0,1:T(8,128)(2,1)} %bitcast.107), calls=%async_computation.3 | async-start | bytes 3145728 | tf_op jit(solution)/shard_map/all_to_all | solution.py:19
  56.1 1.6 gather_fusion
  57.7 2.9 %gather_fusion.2 = bf16[4,64,2048]{2,1,0:T(8,128)(2,1)} fusion(bf16[4,64,2048]{2,1,0:T(8,128)(2,1)} %bitcast.121, s32[1024]{0:T(1024)S(1)} %pad_clamp_fusion.1), kind=kCustom, calls=%fused_computation.2 | custom fusion | bytes 2097168 | tf_op jit(solution)/shard_map/gather | solution.py:45
  60.6 3.1 %broadcast_select_fusion = (bf16[4,64,2048]{2,1,0:T(8,128)(2,1)}, bf16[4,64,2048]{2,1,0:T(8,128)(2,1)}) fusion(bf16[4,64,2048]{2,1,0:T(8,128)(2,1)} %gather_fusion.2, pred[4]{0:T(512)(128)(4,1)S(1)} %get-tuple-element.92, bf16[4,64,2048]{2,1,0:T(8,128)(2,1)} %gather_fusion), kind=kLoop, calls=%fused_computation.42 | loop fusion | flops 1048576 | bytes 4194308 | tf_op jit(solution)/shard_map/jit(_where)/select_n | solution.py:45
  63.7 12.5 %all-to-all-done.3 = bf16[96,4,2048]{2,0,1:T(8,128)(2,1)} async-done(((bf16[96,4,2048]{2,0,1:T(8,128)(2,1)}), bf16[96,4,2048]{2,0,1:T(8,128)(2,1)}, u32[]{:S(2)}, u32[]{:S(2)}) %all-to-all-start.3) | async-done | bytes 1572896 | tf_op jit(solution)/shard_map/all_to_all | solution.py:19
  76.2 31.2 %all_to_all.77 = bf16[4,64,2048]{2,1,0:T(8,128)(2,1)} all-to-all(bf16[4,64,2048]{2,1,0:T(8,128)(2,1)} %get-tuple-element.99), channel_id=1, replica_groups=mesh['groups'=2,'seq'=4,'head'=2,'sub'=2] {'seq'}, dimensions={0} | all-to-all | bytes 2097152 | tf_op jit(solution)/shard_map/all_to_all | solution.py:47
  107.3 4.3 %all-to-all-start.4 = ((bf16[4,64,2048]{2,1,0:T(8,128)(2,1)}), bf16[4,64,2048]{2,1,0:T(8,128)(2,1)}, u32[]{:S(2)}, u32[]{:S(2)}) async-start(bf16[4,64,2048]{2,1,0:T(8,128)(2,1)} %get-tuple-element.98), calls=%async_computation.4 | async-start | bytes 2097152 | tf_op jit(solution)/shard_map/all_to_all | solution.py:48
  112.2 1.6 copy.19
  113.8 1.8 copy.31
  115.6 1.6 copy.20
  117.2 1.8 copy.33
  119.4 1.8 gather_fusion.1
  121.3 1.0 copy.21
  122.3 14.1 %all-to-all-done.4 = bf16[4,64,2048]{2,1,0:T(8,128)(2,1)} async-done(((bf16[4,64,2048]{2,1,0:T(8,128)(2,1)}), bf16[4,64,2048]{2,1,0:T(8,128)(2,1)}, u32[]{:S(2)}, u32[]{:S(2)}) %all-to-all-start.4) | async-done | bytes 1048608 | tf_op jit(solution)/shard_map/all_to_all | solution.py:48
  136.4 1.8 gather_fusion.3
  138.5 58.9 %while.11 = (s32[]{:T(128)}, bf16[16,384,128]{2,1,0:T(8,128)(2,1)}, bf16[16,384,128]{2,1,0:T(8,128)(2,1)}, bf16[16,384,128]{2,1,0:T(8,128)(2,1)}, bf16[16,128,12...) while((s32[]{:T(128)}, bf16[16,384,128]{2,1,0:T(8,128)(2,1)}, ...), condition=%wide.region_7.8_spmd.clone, body=%wide.region_2.7_spmd.clone.sunk | while | flops 102284544 | bytes 3337305 | solution.py:77
  138.5 1.2 fusion.55
  139.7 1.1 fusion.56
  142.2 1.2 fusion.55
  143.4 1.1 fusion.56
  145.8 1.2 fusion.55
  147.0 1.1 fusion.56
  148.6 0.9 fusion.60
  149.5 1.2 fusion.55
  150.7 1.1 fusion.56
  153.2 1.2 fusion.55
  154.4 1.1 fusion.56
  156.0 0.9 fusion.60
  156.9 1.2 fusion.55
  158.1 1.1 fusion.56
  160.6 1.2 fusion.55
  161.8 1.1 fusion.56
  163.4 0.9 fusion.60
  164.2 1.2 fusion.55
  165.4 1.1 fusion.56
  167.9 1.2 fusion.55
  169.1 1.1 fusion.56
  170.7 0.9 fusion.60
  171.6 1.2 fusion.55
  172.8 1.1 fusion.56
  175.3 1.2 fusion.55
  176.5 1.1 fusion.56
  178.1 0.9 fusion.60
  179.0 1.2 fusion.55
  180.2 1.1 fusion.56
  182.6 1.2 fusion.55
  183.8 1.1 fusion.56
  186.3 1.2 fusion.55
  187.5 1.1 fusion.56
  190.0 1.2 fusion.55
  191.2 1.1 fusion.56
  193.7 1.2 fusion.55
  194.9 1.1 fusion.56
  197.4 2.4 %copy.24 = bf16[384,16,128]{2,1,0:T(8,128)(2,1)S(1)} copy(bf16[384,16,128]{2,0,1:T(8,128)(2,1)} %bitcast.13) | data formatting | bytes 3145728 | tf_op jit(solution)/shard_map/transpose | solution.py:78
  199.8 2.1 all_to_all.67
  201.8 23.6 %all_to_all.78 = bf16[4,96,2048]{2,1,0:T(8,128)(2,1)S(1)} all-to-all(bf16[4,96,2048]{2,1,0:T(8,128)(2,1)} %all_to_all.67), channel_id=1, replica_groups=mesh['groups'=2,'seq'=4,'head'=2,'sub'=2] {'head','sub'}, dimensions={0} | all-to-all | bytes 3145728 | tf_op jit(solution)/shard_map/all_to_all | solution.py:79
  225.4 1.2 copy.29
  (108 shorter events, 18.7 us)
Async XLA Ops:
  0.0 56.1 %copy-start = (bf16[256,2048]{1,0:T(8,128)(2,1)S(1)}, bf16[256,2048]{1,0:T(8,128)(2,1)}, u32[]{:S(2)}) copy-start(bf16[256,2048]{1,0:T(8,128)(2,1)} %param.11) | copy-start | bytes 3145732
  2.8 24.3 %all-to-all-start = ((bf16[96,4,2048]{2,0,1:T(8,128)(2,1)}), bf16[96,4,2048]{2,0,1:T(8,128)(2,1)S(1)}, u32[]{:S(2)}, u32[]{:S(2)}) async-start(bf16[96,4,2048]{2,0,1:T(8,128)(2,1)} %bitcast.109), calls=%async_computation | async-start | bytes 3145728 | tf_op jit(solution)/shard_map/all_to_all | solution.py:17
  27.1 24.5 %all-to-all-start.1 = ((bf16[96,4,2048]{2,0,1:T(8,128)(2,1)}), bf16[96,4,2048]{2,0,1:T(8,128)(2,1)}, u32[]{:S(2)}, u32[]{:S(2)}) async-start(bf16[96,4,2048]{2,0,1:T(8,128)(2,1)} %bitcast.108), calls=%async_computation.1 | async-start | bytes 3145728 | tf_op jit(solution)/shard_map/all_to_all | solution.py:18
  51.6 4.5 %copy-start.1 = (s32[4,2]{0,1:T(2,128)S(1)}, s32[4,2]{0,1:T(2,128)}, u32[]{:S(2)}) copy-start(s32[4,2]{0,1:T(2,128)} %param.13) | copy-start | bytes 100
  51.6 24.6 %all-to-all-start.3 = ((bf16[96,4,2048]{2,0,1:T(8,128)(2,1)}), bf16[96,4,2048]{2,0,1:T(8,128)(2,1)}, u32[]{:S(2)}, u32[]{:S(2)}) async-start(bf16[96,4,2048]{2,0,1:T(8,128)(2,1)} %bitcast.107), calls=%async_computation.3 | async-start | bytes 3145728 | tf_op jit(solution)/shard_map/all_to_all | solution.py:19
  107.3 29.1 %all-to-all-start.4 = ((bf16[4,64,2048]{2,1,0:T(8,128)(2,1)}), bf16[4,64,2048]{2,1,0:T(8,128)(2,1)}, u32[]{:S(2)}, u32[]{:S(2)}) async-start(bf16[4,64,2048]{2,1,0:T(8,128)(2,1)} %get-tuple-element.98), calls=%async_computation.4 | async-start | bytes 2097152 | tf_op jit(solution)/shard_map/all_to_all | solution.py:48
where the time goes:
time: 229 us; the launch traced here: 227 us
  waiting for transfers between devices  61.3 us (27%)
  matrix products  55.4 us (24%)
  blocking collectives  54.8 us (24%)
  local copies, waits for them, and re-layouts  31.1 us (14%)
  starting transfers between devices  17.3 us (8%)
  other arithmetic  6.25 us (3%)
    all_to_all x1, blocking collectives, per_device(): lax.all_to_all(send_k, 'seq', split_axis=0, concat_axis=0, tiled=True)  31.2 us
    all_to_all x1, blocking collectives, per_device(): lax.all_to_all(joined, ('head', 'sub'), split_axis=0, concat_axis=1, tile...  23.6 us
    dot_general x16, matrix products, local_scores(): jnp.dot(query_one, key_one.T, preferred_element_type=jnp.float32) * scale  19.2 us
    dot_general x16, matrix products, attend(): jnp.dot(query_one, remote_k.T, preferred_element_type=jnp.float32) * scale  17.6 us
    all_to_all x1, waiting for transfers between devices, per_device(): lax.all_to_all(new_keys, ('head', 'sub'), split_axis=1, concat_axis=0, ti...  17.4 us
    all_to_all x1, waiting for transfers between devices, per_device(): lax.all_to_all(queries, ('head', 'sub'), split_axis=1, concat_axis=0, til...  17.3 us
    all_to_all x1, waiting for transfers between devices, per_device(): lax.all_to_all(send_v, 'seq', split_axis=0, concat_axis=0, tiled=True)  14.1 us
    dot_general x16, matrix products, attend(): jnp.dot(remote_weights.astype(jnp.bfloat16), remote_v, preferred_element_...  14 us
  transfers between devices with their start and end apart: 4, of which 4 were waited for; matrix products, arithmetic and copies ran while one was open for 10% of the time, Pallas kernels for 0%

commit v1 on v0

v1 whole, which is shorter than its diff:
```python
import functools

import jax
import jax.numpy as jnp
from jax import lax
from jax.experimental import pallas as pl
from jax.experimental.pallas import tpu as pltpu
from jax.sharding import PartitionSpec as P

HD = 128
BLOCK = 64
LOG2E = 1.4426950408889634
MASKED = -1e30


def softmax_rows(scores, values):
    top = functools.reduce(jnp.maximum, [jnp.max(s, axis=1, keepdims=True) for s in scores])
    weights = [jnp.exp2(s - top) for s in scores]
    total = functools.reduce(jnp.add, [jnp.sum(w, axis=1, keepdims=True) for w in weights])
    mixed = functools.reduce(
        jnp.add,
        [
            jnp.dot(w.astype(jnp.bfloat16), v, preferred_element_type=jnp.float32)
            for w, v in zip(weights, values)
        ],
    )
    return mixed, top, total


def logits(q, k, factor):
    return lax.dot_general(
        q, k, (((1,), (1,)), ((), ())), preferred_element_type=jnp.float32
    ) * factor


def ulysses_kernel(n, topk, per, parts, factor, where_ref, own_ref, *refs):
    qs, ks, vs = refs[:n], refs[n : 2 * n], refs[2 * n : 3 * n]
    cks, cvs = refs[3 * n : 3 * n + topk], refs[3 * n + topk : 3 * n + 2 * topk]
    out_ref, q_all, k_all, v_all = refs[3 * n + 2 * topk :]
    rows = qs[0].shape[0]
    count = rows * n
    for b in range(n):
        at = pl.ds(pl.multiple_of(where_ref[1 + b] * rows, rows), rows)
        q_all[at, :] = qs[b][...]
        k_all[at, :] = ks[b][...]
        v_all[at, :] = vs[b][...]
    step = count // parts
    causal = lax.broadcasted_iota(jnp.int32, (step, step), 0) >= lax.broadcasted_iota(
        jnp.int32, (step, step), 1
    )
    for j in range(per):
        col = slice(j * HD, (j + 1) * HD)
        ck = [r[0, :, col] for r in cks]
        cv = [r[0, :, col] for r in cvs]
        ck = jnp.concatenate(ck, axis=0)
        cv = jnp.concatenate(cv, axis=0)
        for i in range(parts):
            here = slice(i * step, (i + 1) * step)
            q = q_all[here, col]
            scores = [logits(q, ck, factor)]
            values = [cv]
            if i > 0:
                scores.append(logits(q, k_all[: i * step, col], factor))
                values.append(v_all[: i * step, col])
            scores.append(jnp.where(causal, logits(q, k_all[here, col], factor), MASKED))
            values.append(v_all[here, col])
            mixed, top, total = softmax_rows(scores, values)
            out_ref[here, col] = (mixed / total).astype(jnp.bfloat16)


def ulysses(n, subs, queries, new_keys, new_values, key_cache, value_cache, selection):
    rows, features = queries.shape
    width = features // n
    heads = width // HD
    topk = selection.shape[1]
    me = lax.axis_index("seq")
    group = lax.axis_index("head") * subs + lax.axis_index("sub")

    def peer(b):
        return lax.rem(group + b, n)

    def exchange(b, piece):
        return lax.ppermute(piece, ("head", "sub"), [(i, (i + b) % n) for i in range(n)])

    def spread(array):
        pieces = [array]
        for b in range(1, n):
            piece = lax.dynamic_slice_in_dim(array, peer(b) * width, width, axis=1)
            pieces.append(exchange(b, piece))
        return pieces

    blk_dev = key_cache.shape[0] // BLOCK
    owner_of = selection // blk_dev
    inner = jnp.sum(jnp.where(owner_of == me, selection % blk_dev, 0), axis=1)
    mine = lax.dynamic_index_in_dim(selection, me, 0, keepdims=False) // blk_dev
    got = [
        lax.all_to_all(
            cache.reshape(blk_dev, BLOCK, -1)[inner], "seq", split_axis=0, concat_axis=0, tiled=True
        )
        for cache in (key_cache, value_cache)
    ]
    q_pieces, k_pieces, v_pieces = spread(queries), spread(new_keys), spread(new_values)
    from_of = jnp.stack([group] + [lax.rem(group + b, n) for b in range(n, 0, -1)]).astype(jnp.int32)
    per = 2 if heads % 2 == 0 else 1
    cols = per * HD
    own = pl.BlockSpec((rows, cols), lambda h, w, o: (0, w[0] * (heads // per) + h))
    other = pl.BlockSpec((rows, cols), lambda h, w, o: (0, h))
    cached = [
        pl.BlockSpec((1, BLOCK, cols), functools.partial(lambda t, h, w, o: (o[t], 0, h), t))
        for t in range(topk)
    ]
    count = rows * n
    out = pl.pallas_call(
        functools.partial(
            ulysses_kernel, n, topk, per, 2, float(HD) ** (-0.5) * LOG2E
        ),
        out_shape=jax.ShapeDtypeStruct((count, width), jnp.bfloat16),
        grid_spec=pltpu.PrefetchScalarGridSpec(
            num_scalar_prefetch=2,
            grid=(heads // per,),
            in_specs=([own] + [other] * (n - 1)) * 3 + cached * 2,
            out_specs=pl.BlockSpec((count, cols), lambda h, w, o: (0, h)),
            scratch_shapes=[pltpu.VMEM((count, cols), jnp.bfloat16)] * 3,
        ),
        name="attend",
    )(from_of, mine, *q_pieces, *k_pieces, *v_pieces, *([got[0]] * topk), *([got[1]] * topk))
    result = jnp.zeros((rows, features), jnp.bfloat16)
    for b in range(n):
        piece = lax.dynamic_slice_in_dim(out, peer(b) * rows, rows, axis=0)
        if b > 0:
            piece = exchange(b, piece)
        result = lax.dynamic_update_slice_in_dim(
            result, piece, lax.rem(group + n - b, n) * width, axis=1
        )
    return result


def solution(mesh):
    subs = mesh.shape["sub"]
    n = mesh.shape["head"] * subs
    placed = (
        P(("groups", "seq", "head", "sub"), None),
        P(("groups", "seq", "head", "sub"), None),
        P(("groups", "seq", "head", "sub"), None),
        P(("groups", "seq"), ("head", "sub")),
        P(("groups", "seq"), ("head", "sub")),
        P("groups", None),
    )
    return jax.shard_map(
        functools.partial(ulysses, n, subs),
        mesh=mesh,
        in_specs=placed,
        out_specs=P(("groups", "seq", "head", "sub"), None),
        check_vma=False,
    )
```

time: 229 us -> 133 us (0.58)
  matrix products: 55.4 us -> 0 us
  blocking collectives: 54.8 us -> 0 us
  local copies, waits for them, and re-layouts: 31.1 us -> 11.4 us
  waiting for transfers between devices: 61.3 us -> 79.7 us
  Pallas kernels: 0 us -> 15.5 us
  starting transfers between devices: 17.3 us -> 22.8 us
  other arithmetic: 6.25 us -> 1.29 us
    ppermute x0 -> x12, waiting for transfers between devices: none -> 55.6 us  [exchange(): lax.ppermute(piece, ('head', 'sub'), [(i, (i + b) % n) for i in range(n)])]
    dot_general x64 -> x0, matrix products: 55.4 us -> none  [the longest x16 19.2 us: local_scores(): jnp.dot(query_one, key_one.T, preferred_element_type=jnp.float32) * scale]
    all_to_all x2 -> x0, blocking collectives: 54.8 us -> none  [the longest x1 31.2 us: per_device(): lax.all_to_all(send_k, 'seq', split_axis=0, concat_axis=0, tiled=True)]
    all_to_all x4 -> x2, waiting for transfers between devices: 61.3 us -> 24.1 us  [ulysses(): lax.all_to_all(cache.reshape(blk_dev, BLOCK, -1)[inner], 'seq', split_axi...]
    pallas_call x0 -> x1, Pallas kernels: none -> 15.5 us  [ulysses(): pl.pallas_call(functools.partial(ulysses_kernel, n, topk, per, 2, float(H...]
    ppermute x0 -> x12, starting transfers between devices: none -> 12.8 us  [exchange(): lax.ppermute(piece, ('head', 'sub'), [(i, (i + b) % n) for i in range(n)])]
    all_to_all x5 -> x0, local copies, waits for them, and re-layouts: 11.6 us -> none  [the longest x2 3.3 us: per_device(): lax.all_to_all(joined, ('head', 'sub'), split_axis=0, concat_axis=1, tile...]
    all_to_all x4 -> x2, starting transfers between devices: 17.3 us -> 10 us  [ulysses(): lax.all_to_all(cache.reshape(blk_dev, BLOCK, -1)[inner], 'seq', split_axi...]
  transfers between devices with their start and end apart: 4 -> 14, of which waited for: 4 -> 13; matrix products, arithmetic and copies ran while one was open for 10% -> 5% of each run, Pallas kernels for 0% -> 0%
where the time goes in v1:
time: 133 us; the launch traced here: 131 us
  waiting for transfers between devices  79.7 us (60%)
  starting transfers between devices  22.8 us (17%)
  Pallas kernels  15.5 us (12%)
  local copies, waits for them, and re-layouts  11.4 us (9%)
    ppermute x12, waiting for transfers between devices, exchange(): lax.ppermute(piece, ('head', 'sub'), [(i, (i + b) % n) for i in range(n)])  55.6 us
    all_to_all x2, waiting for transfers between devices, ulysses(): lax.all_to_all(cache.reshape(blk_dev, BLOCK, -1)[inner], 'seq', split_axi...  24.1 us
    pallas_call x1, Pallas kernels, ulysses(): pl.pallas_call(functools.partial(ulysses_kernel, n, topk, per, 2, float(H...  15.5 us
    ppermute x12, starting transfers between devices, exchange(): lax.ppermute(piece, ('head', 'sub'), [(i, (i + b) % n) for i in range(n)])  12.8 us
    all_to_all x2, starting transfers between devices, ulysses(): lax.all_to_all(cache.reshape(blk_dev, BLOCK, -1)[inner], 'seq', split_axi...  10 us
    dynamic_slice x3, local copies, waits for them, and re-layouts, spread(): piece = lax.dynamic_slice_in_dim(array, peer(b) * width, width, axis=1)  3.51 us
    gather x2, local copies, waits for them, and re-layouts, ulysses(): cache.reshape(blk_dev, BLOCK, -1)[inner]  3.21 us
    unnamed x24, local copies, waits for them, and re-layouts  2.73 us
  transfers between devices with their start and end apart: 14, of which 13 were waited for; matrix products, arithmetic and copies ran while one was open for 5% of the time, Pallas kernels for 0%

profile of v1, /device:TPU:0, one launch (start us, length us, event | category | flops | bytes accessed | tf_op | source)
XLA Modules:
  0.0 130.9 jit_solution(15508931247285950825)
XLA Ops:
  0.0 0.0 copy-start
  0.0 0.8 fusion.1
  0.8 0.4 copy-done
  1.2 1.6 %gather_fusion.1 = bf16[4,64,2048]{2,1,0:T(8,128)(2,1)} fusion(bf16[4,64,2048]{2,1,0:T(8,128)(2,1)S(1)} %bitcast.11, s32[1024]{0:T(1024)S(1)} %pad_clamp_fusion), kind=kCustom, calls=%fused_computation.1 | custom fusion | bytes 2097168 | tf_op jit(solution)/shard_map/gather | solution.py:98
  2.9 0.0 copy-start.7
  2.9 6.5 %all-to-all-start.1 = ((bf16[4,64,2048]{2,1,0:T(8,128)(2,1)}), bf16[4,64,2048]{2,1,0:T(8,128)(2,1)S(1)}, u32[]{:S(2)}, u32[]{:S(2)}) async-start(bf16[4,64,2048]{2,1,0:T(8,128)(2,1)} %gather_fusion.1), calls=%async_computation.1 | async-start | bytes 2097152 | tf_op jit(solution)/shard_map/all_to_all | solution.py:97
  9.4 0.0 copy-done.7
  9.4 1.6 %gather_fusion = bf16[4,64,2048]{2,1,0:T(8,128)(2,1)} fusion(bf16[4,64,2048]{2,1,0:T(8,128)(2,1)S(1)} %bitcast.12, s32[1024]{0:T(1024)S(1)} %pad_clamp_fusion), kind=kCustom, calls=%fused_computation | custom fusion | bytes 2097168 | tf_op jit(solution)/shard_map/gather | solution.py:98
  10.9 24.1 %all-to-all-done.1.refs_14_.refs_15_ = bf16[4,64,2048]{2,1,0:T(8,128)(2,1)S(1)} async-done(((bf16[4,64,2048]{2,1,0:T(8,128)(2,1)}), bf16[4,64,2048]{2,1,0:T(8,128)(2,1)S(1)}, u32[]{:S(2)}, u32[]{:S(2)}) %all-to-all-start.1) | async-done | bytes 1048608 | tf_op jit(solution)/shard_map/all_to_all | solution.py:97
  35.1 0.0 copy-start.1
  35.1 3.5 %all-to-all-start = ((bf16[4,64,2048]{2,1,0:T(8,128)(2,1)}), bf16[4,64,2048]{2,1,0:T(8,128)(2,1)S(1)}, u32[]{:S(2)}, u32[]{:S(2)}) async-start(bf16[4,64,2048]{2,1,0:T(8,128)(2,1)} %gather_fusion), calls=%async_computation | async-start | bytes 2097152 | tf_op jit(solution)/shard_map/all_to_all | solution.py:97
  38.6 0.0 copy-start.4
  38.6 1.4 %constant_dynamic-slice_fusion.9 = (bf16[96,2048]{1,0:T(8,128)(2,1)S(1)}, bf16[96,2048]{1,0:T(8,128)(2,1)S(1)}, bf16[96,2048]{1,0:T(8,128)(2,1)S(1)}) fusion(bf16[96,8192]{1,0:T(8,128)(2,1)} %refs_0_.1, s32[]{:T(128)S(6)} %select_n.73, s32[]{:T(128)S(6)} %select_n.72, s32[]{:T(128)S(6)} %select_n.71), kind=kLoop, calls=%fused_computation.15 | loop fusion | bytes 2359308 | tf_op jit(solution)/shard_map/dynamic_slice | solution.py:88
  40.1 0.0 copy-done.1
  40.1 0.0 copy-start.5
  40.1 0.3 collective-permute-start.2
  40.4 1.4 %collective-permute-start.1 = (bf16[96,2048]{1,0:T(8,128)(2,1)S(1)}, bf16[96,2048]{1,0:T(8,128)(2,1)S(1)}, u32[]{:S(2)}, u32[]{:S(2)}) collective-permute-start(bf16[96,2048]{1,0:T(8,128)(2,1)S(1)} %get-tuple-element.16), channel_id=1, source_target_pairs={{0,2},{1,3},{2,0},{3,1},{4,6},{5,7},{6,4},{7,5},{8,10},{9,11},{10,... | collective-permute-start | bytes 1179656 | tf_op jit(solution)/shard_map/ppermute | solution.py:83
  41.7 0.2 collective-permute-start
  41.9 0.0 copy-done.4
  41.9 1.0 constant_dynamic-slice_fusion.6
  42.9 0.0 copy-start.11
  42.9 1.6 %collective-permute-start.5 = (bf16[96,2048]{1,0:T(8,128)(2,1)S(1)}, bf16[96,2048]{1,0:T(8,128)(2,1)}, u32[]{:S(2)}, u32[]{:S(2)}) collective-permute-start(bf16[96,2048]{1,0:T(8,128)(2,1)S(1)} %get-tuple-element.12), channel_id=1, source_target_pairs={{0,3},{1,0},{2,1},{3,2},{4,7},{5,4},{6,5},{7,6},{8,11},{9,8},{10,9... | collective-permute-start | bytes 1179656 | tf_op jit(solution)/shard_map/ppermute | solution.py:83
  44.5 0.7 collective-permute-start.4
  45.1 0.0 copy-done.5
  45.2 1.1 constant_dynamic-slice_fusion.3
  46.2 2.8 %collective-permute-done.2.refs_3_ = bf16[96,2048]{1,0:T(8,128)(2,1)S(1)} collective-permute-done((bf16[96,2048]{1,0:T(8,128)(2,1)S(1)}, bf16[96,2048]{1,0:T(8,128)(2,1)S(1)}, u32[]{:S(2)}, u32[]{:S(2)}) %collective-permute-start.2) | collective-permute-done | bytes 393248 | tf_op jit(solution)/shard_map/ppermute | solution.py:83
  49.1 0.0 copy-start.8
  49.1 2.6 %collective-permute-start.3 = (bf16[96,2048]{1,0:T(8,128)(2,1)}, bf16[96,2048]{1,0:T(8,128)(2,1)}, u32[]{:S(2)}, u32[]{:S(2)}) collective-permute-start(bf16[96,2048]{1,0:T(8,128)(2,1)} %get-tuple-element.14), channel_id=1, source_target_pairs={{0,1},{1,2},{2,3},{3,0},{4,5},{5,6},{6,7},{7,4},{8,9},{9,10},{10,1... | collective-permute-start | bytes 1179656 | tf_op jit(solution)/shard_map/ppermute | solution.py:83
  51.7 8.3 %collective-permute-done.1.refs_2_ = bf16[96,2048]{1,0:T(8,128)(2,1)S(1)} collective-permute-done((bf16[96,2048]{1,0:T(8,128)(2,1)S(1)}, bf16[96,2048]{1,0:T(8,128)(2,1)S(1)}, u32[]{:S(2)}, u32[]{:S(2)}) %collective-permute-start.1) | collective-permute-done | bytes 393248 | tf_op jit(solution)/shard_map/ppermute | solution.py:83
  60.0 0.0 copy-start.9
  60.0 0.0 collective-permute-start.8
  60.0 0.1 collective-permute-done.refs_1_
  60.1 1.5 %collective-permute-start.7 = (bf16[96,2048]{1,0:T(8,128)(2,1)}, bf16[96,2048]{1,0:T(8,128)(2,1)}, u32[]{:S(2)}, u32[]{:S(2)}) collective-permute-start(bf16[96,2048]{1,0:T(8,128)(2,1)} %get-tuple-element.10), channel_id=1, source_target_pairs={{0,2},{1,3},{2,0},{3,1},{4,6},{5,7},{6,4},{7,5},{8,10},{9,11},{10,... | collective-permute-start | bytes 1179656 | tf_op jit(solution)/shard_map/ppermute | solution.py:83
  61.6 4.3 %collective-permute-done.5.refs_7_ = bf16[96,2048]{1,0:T(8,128)(2,1)} collective-permute-done((bf16[96,2048]{1,0:T(8,128)(2,1)S(1)}, bf16[96,2048]{1,0:T(8,128)(2,1)}, u32[]{:S(2)}, u32[]{:S(2)}) %collective-permute-start.5) | collective-permute-done | bytes 393248 | tf_op jit(solution)/shard_map/ppermute | solution.py:83
  65.9 2.4 %collective-permute-start.6 = (bf16[96,2048]{1,0:T(8,128)(2,1)}, bf16[96,2048]{1,0:T(8,128)(2,1)}, u32[]{:S(2)}, u32[]{:S(2)}) collective-permute-start(bf16[96,2048]{1,0:T(8,128)(2,1)} %get-tuple-element.11), channel_id=1, source_target_pairs={{0,1},{1,2},{2,3},{3,0},{4,5},{5,6},{6,7},{7,4},{8,9},{9,10},{10,1... | collective-permute-start | bytes 1179656 | tf_op jit(solution)/shard_map/ppermute | solution.py:83
  68.3 0.0 copy-done.11
  68.3 0.2 fusion
  68.5 0.6 stack.23.where_ref
  69.1 0.5 and_select_fusion.2.own_ref
  69.6 7.3 %collective-permute-done.4.refs_6_ = bf16[96,2048]{1,0:T(8,128)(2,1)} collective-permute-done((bf16[96,2048]{1,0:T(8,128)(2,1)}, bf16[96,2048]{1,0:T(8,128)(2,1)}, u32[]{:S(2)}, u32[]{:S(2)}) %collective-permute-start.4) | collective-permute-done | bytes 393248 | tf_op jit(solution)/shard_map/ppermute | solution.py:83
  76.9 0.1 collective-permute-done.3.refs_5_
  77.1 5.8 %collective-permute-done.8.refs_11_ = bf16[96,2048]{1,0:T(8,128)(2,1)} collective-permute-done((bf16[96,2048]{1,0:T(8,128)(2,1)}, bf16[96,2048]{1,0:T(8,128)(2,1)}, u32[]{:S(2)}, u32[]{:S(2)}) %collective-permute-start.8) | collective-permute-done | bytes 393248 | tf_op jit(solution)/shard_map/ppermute | solution.py:83
  82.9 10.9 %collective-permute-done.7.refs_10_ = bf16[96,2048]{1,0:T(8,128)(2,1)} collective-permute-done((bf16[96,2048]{1,0:T(8,128)(2,1)}, bf16[96,2048]{1,0:T(8,128)(2,1)}, u32[]{:S(2)}, u32[]{:S(2)}) %collective-permute-start.7) | collective-permute-done | bytes 393248 | tf_op jit(solution)/shard_map/ppermute | solution.py:83
  93.8 0.1 collective-permute-done.6.refs_9_
  93.9 0.0 all-to-all-done.refs_12_.refs_13_
  93.9 0.0 copy-done.8
  93.9 0.0 copy-done.9
  93.9 0.0 copy-done.10
  93.9 0.0 copy-start.2
  93.9 1.0 copy-done.2
  94.9 15.5 %attend.1 = bf16[384,2048]{1,0:T(8,128)(2,1)} custom-call(s32[5]{0:T(128)} %stack.23.where_ref, s32[2]{0:T(128)} %and_select_fusion.2.own_ref, bf16[96,8192]{1,0:T(8,128)(2,1)} %refs_0_.1, bf16[96,2048]{1,0:T(8,128)(2,1)} %copy-done.10, bf16[96,2048]{1,0:T(8,128)(2,1)} %copy-done.9, bf16[96,2048]{1,0:T(8,128)(2,1)} %copy-done.8, bf16[96,8192]{1,0:T(8,128)(2,1)} %refs_4_.1, ...), custom_call_target="tpu_custom_call" | custom-call | tf_op jit(solution)/shard_map/attend/pallas_call | solution.py:113
  110.4 0.0 copy-start.3
  110.4 0.1 broadcast_in_dim.4
  110.6 1.3 copy-done.3
  111.8 0.2 constant_dynamic-slice_fusion
  112.0 0.1 collective-permute-start.9
  112.0 0.8 collective-permute-start.10
  112.8 1.4 %collective-permute-start.11 = (bf16[96,2048]{1,0:T(8,128)(2,1)S(1)}, bf16[96,2048]{1,0:T(8,128)(2,1)S(1)}, u32[]{:S(2)}, u32[]{:S(2)}) collective-permute-start(bf16[96,2048]{1,0:T(8,128)(2,1)S(1)} %get-tuple-element.5), channel_id=1, source_target_pairs={{0,3},{1,0},{2,1},{3,2},{4,7},{5,4},{6,5},{7,6},{8,11},{9,8},{10,9... | collective-permute-start | bytes 1179656 | tf_op jit(solution)/shard_map/ppermute | solution.py:83
  114.2 8.6 %collective-permute-done.9 = bf16[96,2048]{1,0:T(8,128)(2,1)S(1)} collective-permute-done((bf16[96,2048]{1,0:T(8,128)(2,1)S(1)}, bf16[96,2048]{1,0:T(8,128)(2,1)S(1)}, u32[]{:S(2)}, u32[]{:S(2)}) %collective-permute-start.9) | collective-permute-done | bytes 393248 | tf_op jit(solution)/shard_map/ppermute | solution.py:83
  122.8 1.3 collective-permute-done.10
  124.1 0.0 copy-start.6
  124.2 6.0 %collective-permute-done.11 = bf16[96,2048]{1,0:T(8,128)(2,1)S(1)} collective-permute-done((bf16[96,2048]{1,0:T(8,128)(2,1)S(1)}, bf16[96,2048]{1,0:T(8,128)(2,1)S(1)}, u32[]{:S(2)}, u32[]{:S(2)}) %collective-permute-start.11) | collective-permute-done | bytes 393248 | tf_op jit(solution)/shard_map/ppermute | solution.py:83
  130.1 0.0 copy-done.6
  130.1 0.8 constant_dynamic-update-slice_fusion
  (5 shorter events, 0.1 us)
Async XLA Ops:
  0.0 1.2 copy-start
  2.9 6.5 %copy-start.7 = (bf16[256,2048]{1,0:T(8,128)(2,1)S(1)}, bf16[256,2048]{1,0:T(8,128)(2,1)}, u32[]{:S(2)}) copy-start(bf16[256,2048]{1,0:T(8,128)(2,1)} %param.9) | copy-start | bytes 3145732
  2.9 32.2 %all-to-all-start.1 = ((bf16[4,64,2048]{2,1,0:T(8,128)(2,1)}), bf16[4,64,2048]{2,1,0:T(8,128)(2,1)S(1)}, u32[]{:S(2)}, u32[]{:S(2)}) async-start(bf16[4,64,2048]{2,1,0:T(8,128)(2,1)} %gather_fusion.1), calls=%async_computation.1 | async-start | bytes 2097152 | tf_op jit(solution)/shard_map/all_to_all | solution.py:97
  35.1 5.0 %copy-start.1 = (bf16[4,64,2048]{2,1,0:T(8,128)(2,1)}, bf16[4,64,2048]{2,1,0:T(8,128)(2,1)S(1)}, u32[]{:S(2)}) copy-start(bf16[4,64,2048]{2,1,0:T(8,128)(2,1)S(1)} %all-to-all-done.1.refs_14_.refs_15_) | copy-start | bytes 3145732
  35.1 58.8 %all-to-all-start = ((bf16[4,64,2048]{2,1,0:T(8,128)(2,1)}), bf16[4,64,2048]{2,1,0:T(8,128)(2,1)S(1)}, u32[]{:S(2)}, u32[]{:S(2)}) async-start(bf16[4,64,2048]{2,1,0:T(8,128)(2,1)} %gather_fusion), calls=%async_computation | async-start | bytes 2097152 | tf_op jit(solution)/shard_map/all_to_all | solution.py:97
  38.6 3.2 %copy-start.4 = (bf16[96,8192]{1,0:T(8,128)(2,1)S(1)}, bf16[96,8192]{1,0:T(8,128)(2,1)}, u32[]{:S(2)}) copy-start(bf16[96,8192]{1,0:T(8,128)(2,1)} %refs_4_.1) | copy-start | bytes 4718596
  40.1 5.1 %copy-start.5 = (bf16[96,8192]{1,0:T(8,128)(2,1)S(1)}, bf16[96,8192]{1,0:T(8,128)(2,1)}, u32[]{:S(2)}) copy-start(bf16[96,8192]{1,0:T(8,128)(2,1)} %refs_8_.1) | copy-start | bytes 4718596
  40.1 8.9 %collective-permute-start.2 = (bf16[96,2048]{1,0:T(8,128)(2,1)S(1)}, bf16[96,2048]{1,0:T(8,128)(2,1)S(1)}, u32[]{:S(2)}, u32[]{:S(2)}) collective-permute-start(bf16[96,2048]{1,0:T(8,128)(2,1)S(1)} %get-tuple-element.15), channel_id=1, source_target_pairs={{0,3},{1,0},{2,1},{3,2},{4,7},{5,4},{6,5},{7,6},{8,11},{9,8},{10,9... | collective-permute-start | bytes 1179656 | tf_op jit(solution)/shard_map/ppermute | solution.py:83
  40.4 19.6 %collective-permute-start.1 = (bf16[96,2048]{1,0:T(8,128)(2,1)S(1)}, bf16[96,2048]{1,0:T(8,128)(2,1)S(1)}, u32[]{:S(2)}, u32[]{:S(2)}) collective-permute-start(bf16[96,2048]{1,0:T(8,128)(2,1)S(1)} %get-tuple-element.16), channel_id=1, source_target_pairs={{0,2},{1,3},{2,0},{3,1},{4,6},{5,7},{6,4},{7,5},{8,10},{9,11},{10,... | collective-permute-start | bytes 1179656 | tf_op jit(solution)/shard_map/ppermute | solution.py:83
  41.7 18.4 %collective-permute-start = (bf16[96,2048]{1,0:T(8,128)(2,1)S(1)}, bf16[96,2048]{1,0:T(8,128)(2,1)S(1)}, u32[]{:S(2)}, u32[]{:S(2)}) collective-permute-start(bf16[96,2048]{1,0:T(8,128)(2,1)S(1)} %get-tuple-element.17), channel_id=1, source_target_pairs={{0,1},{1,2},{2,3},{3,0},{4,5},{5,6},{6,7},{7,4},{8,9},{9,10},{10,1... | collective-permute-start | bytes 1179656 | tf_op jit(solution)/shard_map/ppermute | solution.py:83
  42.9 25.4 %copy-start.11 = (s32[4,2]{0,1:T(2,128)S(1)}, s32[4,2]{0,1:T(2,128)}, u32[]{:S(2)}) copy-start(s32[4,2]{0,1:T(2,128)} %param.11) | copy-start | bytes 100
  42.9 23.0 %collective-permute-start.5 = (bf16[96,2048]{1,0:T(8,128)(2,1)S(1)}, bf16[96,2048]{1,0:T(8,128)(2,1)}, u32[]{:S(2)}, u32[]{:S(2)}) collective-permute-start(bf16[96,2048]{1,0:T(8,128)(2,1)S(1)} %get-tuple-element.12), channel_id=1, source_target_pairs={{0,3},{1,0},{2,1},{3,2},{4,7},{5,4},{6,5},{7,6},{8,11},{9,8},{10,9... | collective-permute-start | bytes 1179656 | tf_op jit(solution)/shard_map/ppermute | solution.py:83
  44.5 32.5 %collective-permute-start.4 = (bf16[96,2048]{1,0:T(8,128)(2,1)}, bf16[96,2048]{1,0:T(8,128)(2,1)}, u32[]{:S(2)}, u32[]{:S(2)}) collective-permute-start(bf16[96,2048]{1,0:T(8,128)(2,1)} %get-tuple-element.13), channel_id=1, source_target_pairs={{0,2},{1,3},{2,0},{3,1},{4,6},{5,7},{6,4},{7,5},{8,10},{9,11},{10,... | collective-permute-start | bytes 1179656 | tf_op jit(solution)/shard_map/ppermute | solution.py:83
  49.1 44.8 %copy-start.8 = (bf16[96,2048]{1,0:T(8,128)(2,1)}, bf16[96,2048]{1,0:T(8,128)(2,1)S(1)}, u32[]{:S(2)}) copy-start(bf16[96,2048]{1,0:T(8,128)(2,1)S(1)} %collective-permute-done.2.refs_3_) | copy-start | bytes 1179652
  49.1 28.0 %collective-permute-start.3 = (bf16[96,2048]{1,0:T(8,128)(2,1)}, bf16[96,2048]{1,0:T(8,128)(2,1)}, u32[]{:S(2)}, u32[]{:S(2)}) collective-permute-start(bf16[96,2048]{1,0:T(8,128)(2,1)} %get-tuple-element.14), channel_id=1, source_target_pairs={{0,1},{1,2},{2,3},{3,0},{4,5},{5,6},{6,7},{7,4},{8,9},{9,10},{10,1... | collective-permute-start | bytes 1179656 | tf_op jit(solution)/shard_map/ppermute | solution.py:83
  60.0 33.9 %copy-start.9 = (bf16[96,2048]{1,0:T(8,128)(2,1)}, bf16[96,2048]{1,0:T(8,128)(2,1)S(1)}, u32[]{:S(2)}) copy-start(bf16[96,2048]{1,0:T(8,128)(2,1)S(1)} %collective-permute-done.1.refs_2_) | copy-start | bytes 1179652
  60.0 22.9 %collective-permute-start.8 = (bf16[96,2048]{1,0:T(8,128)(2,1)}, bf16[96,2048]{1,0:T(8,128)(2,1)}, u32[]{:S(2)}, u32[]{:S(2)}) collective-permute-start(bf16[96,2048]{1,0:T(8,128)(2,1)} %get-tuple-element.9), channel_id=1, source_target_pairs={{0,3},{1,0},{2,1},{3,2},{4,7},{5,4},{6,5},{7,6},{8,11},{9,8},{10,9... | collective-permute-start | bytes 1179656 | tf_op jit(solution)/shard_map/ppermute | solution.py:83
  60.1 33.8 %copy-start.10 = (bf16[96,2048]{1,0:T(8,128)(2,1)}, bf16[96,2048]{1,0:T(8,128)(2,1)S(1)}, u32[]{:S(2)}) copy-start(bf16[96,2048]{1,0:T(8,128)(2,1)S(1)} %collective-permute-done.refs_1_) | copy-start | bytes 1179652
  60.1 33.7 %collective-permute-start.7 = (bf16[96,2048]{1,0:T(8,128)(2,1)}, bf16[96,2048]{1,0:T(8,128)(2,1)}, u32[]{:S(2)}, u32[]{:S(2)}) collective-permute-start(bf16[96,2048]{1,0:T(8,128)(2,1)} %get-tuple-element.10), channel_id=1, source_target_pairs={{0,2},{1,3},{2,0},{3,1},{4,6},{5,7},{6,4},{7,5},{8,10},{9,11},{10,... | collective-permute-start | bytes 1179656 | tf_op jit(solution)/shard_map/ppermute | solution.py:83
  65.9 27.9 %collective-permute-start.6 = (bf16[96,2048]{1,0:T(8,128)(2,1)}, bf16[96,2048]{1,0:T(8,128)(2,1)}, u32[]{:S(2)}, u32[]{:S(2)}) collective-permute-start(bf16[96,2048]{1,0:T(8,128)(2,1)} %get-tuple-element.11), channel_id=1, source_target_pairs={{0,1},{1,2},{2,3},{3,0},{4,5},{5,6},{6,7},{7,4},{8,9},{9,10},{10,1... | collective-permute-start | bytes 1179656 | tf_op jit(solution)/shard_map/ppermute | solution.py:83
  93.9 1.0 copy-start.2
  110.4 1.4 %copy-start.3 = (bf16[384,2048]{1,0:T(8,128)(2,1)S(1)}, bf16[384,2048]{1,0:T(8,128)(2,1)}, u32[]{:S(2)}) copy-start(bf16[384,2048]{1,0:T(8,128)(2,1)} %attend.1) | copy-start | bytes 4718596
  112.0 10.8 %collective-permute-start.9 = (bf16[96,2048]{1,0:T(8,128)(2,1)S(1)}, bf16[96,2048]{1,0:T(8,128)(2,1)S(1)}, u32[]{:S(2)}, u32[]{:S(2)}) collective-permute-start(bf16[96,2048]{1,0:T(8,128)(2,1)S(1)} %get-tuple-element.7), channel_id=1, source_target_pairs={{0,1},{1,2},{2,3},{3,0},{4,5},{5,6},{6,7},{7,4},{8,9},{9,10},{10,1... | collective-permute-start | bytes 1179656 | tf_op jit(solution)/shard_map/ppermute | solution.py:83
  112.0 12.1 %collective-permute-start.10 = (bf16[96,2048]{1,0:T(8,128)(2,1)S(1)}, bf16[96,2048]{1,0:T(8,128)(2,1)S(1)}, u32[]{:S(2)}, u32[]{:S(2)}) collective-permute-start(bf16[96,2048]{1,0:T(8,128)(2,1)S(1)} %get-tuple-element.6), channel_id=1, source_target_pairs={{0,2},{1,3},{2,0},{3,1},{4,6},{5,7},{6,4},{7,5},{8,10},{9,11},{10,... | collective-permute-start | bytes 1179656 | tf_op jit(solution)/shard_map/ppermute | solution.py:83
  112.8 17.3 %collective-permute-start.11 = (bf16[96,2048]{1,0:T(8,128)(2,1)S(1)}, bf16[96,2048]{1,0:T(8,128)(2,1)S(1)}, u32[]{:S(2)}, u32[]{:S(2)}) collective-permute-start(bf16[96,2048]{1,0:T(8,128)(2,1)S(1)} %get-tuple-element.5), channel_id=1, source_target_pairs={{0,3},{1,0},{2,1},{3,2},{4,7},{5,4},{6,5},{7,6},{8,11},{9,8},{10,9... | collective-permute-start | bytes 1179656 | tf_op jit(solution)/shard_map/ppermute | solution.py:83
  124.1 6.0 %copy-start.6 = (bf16[96,8192]{1,0:T(8,128)(2,1)}, bf16[96,8192]{1,0:T(8,128)(2,1)S(1)}, u32[]{:S(2)}) copy-start(bf16[96,8192]{1,0:T(8,128)(2,1)S(1)} %constant_dynamic-update-slice_fusion.1) | copy-start | bytes 4718596

commit v2 on v1

--- a/solution.py
+++ b/solution.py
@@ -7,10 +7,12 @@
 from jax.experimental.pallas import tpu as pltpu
 from jax.sharding import PartitionSpec as P
 
+
 HD = 128
 BLOCK = 64
 LOG2E = 1.4426950408889634
 MASKED = -1e30
+VMEM_LIMIT = 16 << 20
 
 
 def softmax_rows(scores, values):
@@ -64,7 +66,7 @@
                 values.append(v_all[: i * step, col])
             scores.append(jnp.where(causal, logits(q, k_all[here, col], factor), MASKED))
             values.append(v_all[here, col])
-            mixed, top, total = softmax_rows(scores, values)
+            mixed, _, total = softmax_rows(scores, values)
             out_ref[here, col] = (mixed / total).astype(jnp.bfloat16)
 
 
@@ -135,6 +137,259 @@
     return result
 
 
+def chip_bias(bias, place, rows):
+    def token(at):
+        return jnp.where(at < rows, place * rows + at, (1 - place) * rows + at - rows)
+
+    q = token(lax.broadcasted_iota(jnp.int32, bias.shape, 0))
+    k = lax.broadcasted_iota(jnp.int32, bias.shape, 1)
+    bias[...] = jnp.where((k >= 2 * rows) | (q >= token(k)), 0.0, MASKED)
+
+
+def soft(scores, values):
+    top = jnp.max(scores, axis=1, keepdims=True)
+    weights = jnp.exp2(scores - top)
+    total = jnp.sum(weights, axis=1, keepdims=True)
+    mixed = jnp.dot(weights.astype(jnp.bfloat16), values, preferred_element_type=jnp.float32)
+    return (mixed * (1.0 / total)).astype(jnp.bfloat16)
+
+
+def group_index():
+    return lax.axis_index("head") * 2 + lax.axis_index("sub")
+
+
+def run_copies(pairs, sems):
+    copies = [pltpu.make_async_copy(a, b, sems.at[i]) for i, (a, b) in enumerate(pairs)]
+    for copy in copies:
+        copy.start()
+    for copy in copies:
+        copy.wait()
+
+
+def held(sel_ref, row, owner, blk_dev):
+    inner = jnp.int32(0)
+    for t in range(sel_ref.shape[0]):
+        picked = sel_ref[t, row]
+        match = lax.div(picked, jnp.int32(blk_dev)) == owner
+        inner = jnp.where(match, lax.rem(picked, jnp.int32(blk_dev)), inner)
+    return inner
+
+
+def pack_kernel(width, wanted, q, k, v, after, *refs):
+    outs, sems = refs[:-1], refs[-1]
+    pairs = []
+    for out, (d, start, size) in zip(outs, wanted):
+        at = (group_index() ^ d) * width + start
+        cols = pl.ds(pl.multiple_of(at, HD), size)
+        for i, array in enumerate((q, k, v)):
+            pairs.append((array.at[:, cols], out.at[:, i * size : (i + 1) * size]))
+    run_copies(pairs, sems)
+
+
+def sends_kernel(n_seq, blk_dev, rows, chunks, sel_ref, kc, vc, after, *refs):
+    outs, bias, sems = refs[:-2], refs[-2], refs[-1]
+    me = lax.axis_index("seq")
+    pairs = []
+    for i, (start, size) in enumerate(chunks):
+        for d in range(n_seq):
+            inner = held(sel_ref, me ^ d, me, blk_dev)
+            at = pl.ds(pl.multiple_of(inner * BLOCK, BLOCK), BLOCK)
+            to = outs[i * n_seq + d]
+            pairs.append((kc.at[at, start : start + size], to.at[:BLOCK]))
+            pairs.append((vc.at[at, start : start + size], to.at[BLOCK:]))
+    copies = [pltpu.make_async_copy(a, b, sems.at[i]) for i, (a, b) in enumerate(pairs)]
+    for copy in copies:
+        copy.start()
+    chip_bias(bias, lax.axis_index("sub"), rows)
+    for copy in copies:
+        copy.wait()
+
+
+def attend_kernel(n, n_seq, per, blk_dev, size, factor, sel_ref, bias, *refs):
+    given, came = refs[:n], refs[n : n + n_seq]
+    outs, kept = refs[n + n_seq : 2 * n + n_seq], refs[2 * n + n_seq]
+    rows = given[0].shape[0]
+    topk = sel_ref.shape[0]
+    seen = topk * BLOCK
+    me = lax.axis_index("seq")
+    for t in range(topk):
+        distance = lax.div(sel_ref[t, me], jnp.int32(blk_dev)) ^ me
+        for d in range(n_seq):
+
+            @pl.when(distance == d)
+            def _():
+                kept[t * BLOCK : (t + 1) * BLOCK] = came[d][:BLOCK]
+                kept[seen + t * BLOCK : seen + (t + 1) * BLOCK] = came[d][BLOCK:]
+
+    def work(early, late):
+        def step(h, carry):
+            for j in range(per):
+                head = (h * per + j) * HD
+                col = pl.ds(pl.multiple_of(head, HD), HD)
+
+                def pick(side, t):
+                    at = pl.ds(pl.multiple_of(t * size + head, HD), HD)
+                    return [given[d][:, at] for d in side]
+
+                kept_k, kept_v = kept[:seen, col], kept[seen:, col]
+                early_k, early_v = pick(early, 1), pick(early, 2)
+                for side, k, v in (
+                    (early, early_k, early_v),
+                    (late, pick(late, 1) + early_k, pick(late, 2) + early_v),
+                ):
+                    q = jnp.concatenate(pick(side, 0), axis=0)
+                    scores = logits(q, jnp.concatenate([kept_k] + k, axis=0), factor)
+                    masked = min(bias.shape[1], scores.shape[1] - seen)
+                    parts = [scores[:, :seen], scores[:, seen : seen + masked] + bias[:, :masked]]
+                    if scores.shape[1] > seen + masked:
+                        parts.append(scores[:, seen + masked :])
+                    mixed = soft(
+                        jnp.concatenate(parts, axis=1), jnp.concatenate([kept_v] + v, axis=0)
+                    )
+                    outs[side[0]][:, col] = mixed[:rows]
+                    outs[side[1]][:, col] = mixed[rows:]
+            return carry
+
+        lax.fori_loop(0, size // HD // per, step, 0)
+
+    @pl.when(lax.axis_index("head") == 0)
+    def _():
+        work((0, 1), (2, 3))
+
+    @pl.when(lax.axis_index("head") == 1)
+    def _():
+        work((2, 3), (0, 1))
+
+
+def assemble_kernel(n, width, start, size, count, *refs):
+    arrays, result, sems = refs[:n], refs[count], refs[-1]
+    pairs = []
+    for d in range(n):
+        to = (group_index() ^ d) * width + start
+        pairs.append((arrays[d], result.at[:, pl.ds(pl.multiple_of(to, HD), size)]))
+    run_copies(pairs, sems)
+
+
+def pipelined(n_seq, chunk_heads, queries, new_keys, new_values, key_cache, value_cache, selection):
+    n = 4
+    rows, features = queries.shape
+    width = features // n
+    heads = width // HD
+    chunks, first = [], 0
+    for count in chunk_heads(heads):
+        chunks.append((first * HD, count * HD))
+        first += count
+    factor = float(HD) ** (-0.5) * LOG2E
+    blk_dev = key_cache.shape[0] // BLOCK
+    anywhere = pl.BlockSpec(memory_space=pl.ANY)
+    resident = pl.BlockSpec(memory_space=pltpu.VMEM)
+    bf16 = jnp.bfloat16
+
+    def call(kernel, scalars, arrays, in_specs, outs, scratch):
+        return pl.pallas_call(
+            kernel,
+            out_shape=[
+                jax.ShapeDtypeStruct(*o) if isinstance(o, tuple) else o for o in outs
+            ],
+            grid_spec=pltpu.PrefetchScalarGridSpec(
+                num_scalar_prefetch=len(scalars),
+                grid=(1,),
+                in_specs=in_specs,
+                out_specs=[
+                    pl.BlockSpec(o[0], lambda *_: (0, 0)) if isinstance(o, tuple) else resident
+                    for o in outs
+                ],
+                scratch_shapes=scratch,
+            ),
+            compiler_params=pltpu.CompilerParams(vmem_limit_bytes=VMEM_LIMIT),
+        )(*scalars, *arrays)
+
+    def exchange(d, x):
+        return lax.ppermute(x, ("head", "sub"), [(i, i ^ d) for i in range(n)])
+
+    def along(d, x):
+        return lax.ppermute(x, "seq", [(i, i ^ d) for i in range(n_seq)])
+
+    def pack(wanted, after):
+        return call(
+            functools.partial(pack_kernel, width, wanted), [],
+            [queries, new_keys, new_values, after], [anywhere] * 4,
+            [pltpu.VMEM((rows, 3 * size), bf16) for _, _, size in wanted],
+            [pltpu.SemaphoreType.DMA((3 * len(wanted),))],
+        )
+
+    last = len(chunks) - 1
+    picks = selection.T
+    packed = [pack([(d, *chunks[0]) for d in range(1, n)], queries)]
+    sends = call(
+        functools.partial(sends_kernel, n_seq, blk_dev, rows, chunks), [picks],
+        [key_cache, value_cache, packed[0][0]], [anywhere] * 3,
+        [
+            pltpu.VMEM((2 * BLOCK, size), bf16)
+            for _, size in chunks
+            for _ in range(n_seq)
+        ]
+        + [pltpu.VMEM((2 * rows, pl.cdiv(2 * rows, HD) * HD), jnp.float32)],
+        [pltpu.SemaphoreType.DMA((2 * n_seq * len(chunks),))],
+    )
+    bias = sends[-1]
+    for i in range(1, len(chunks)):
+        packed.append(pack([(d, *chunks[i]) for d in range(1, n)], sends[1]))
+    owned = pack([(0, *chunk) for chunk in chunks], packed[last][0])
+
+    def attend(i, given, came):
+        size = chunks[i][1]
+        count = size // HD
+        return call(
+            functools.partial(
+                attend_kernel, n, n_seq, 2 if count % 2 == 0 else 1, blk_dev, size, factor
+            ),
+            [picks], [bias, *given, *came], [resident] * (1 + n + n_seq),
+            [pltpu.VMEM((rows, size), bf16)] * n,
+            [pltpu.VMEM((2 * selection.shape[1] * BLOCK, size), bf16)],
+        )
+
+    result = None
+    for i, (start, size) in enumerate(chunks):
+        given = [exchange(d, packed[i][d - 1]) for d in range(1, n)]
+        given = [owned[i]] + given
+        block = sends[i * n_seq : (i + 1) * n_seq]
+        came = [block[0]] + [along(d, block[d]) for d in range(1, n_seq)]
+        outs = attend(i, given, came)
+        pieces = [outs[0]] + [exchange(d, outs[d]) for d in range(1, n)]
+        if result is not None:
+            pieces.append(result)
+        result = pl.pallas_call(
+            functools.partial(assemble_kernel, n, width, start, size, len(pieces)),
+            out_shape=jax.ShapeDtypeStruct((rows, features), bf16),
+            grid_spec=pltpu.PrefetchScalarGridSpec(
+                num_scalar_prefetch=0,
+                grid=(1,),
+                in_specs=[resident] * n + [anywhere] * (len(pieces) - n),
+                out_specs=anywhere,
+                scratch_shapes=[pltpu.SemaphoreType.DMA((n,))],
+            ),
+            input_output_aliases={n: 0} if i > 0 else {},
+            compiler_params=pltpu.CompilerParams(vmem_limit_bytes=VMEM_LIMIT),
+        )(*pieces)
+    return result
+
+
+def uneven(heads):
+    second = max(2, heads * 3 // 8 // 2 * 2)
+    return (heads - second, second)
+
+
+def placed_map(body, mesh, placed):
+    return jax.shard_map(
+        body,
+        mesh=mesh,
+        in_specs=placed,
+        out_specs=P(("groups", "seq", "head", "sub"), None),
+        check_vma=False,
+    )
+
+
 def solution(mesh):
     subs = mesh.shape["sub"]
     n = mesh.shape["head"] * subs
@@ -146,10 +401,14 @@
         P(("groups", "seq"), ("head", "sub")),
         P("groups", None),
     )
-    return jax.shard_map(
-        functools.partial(ulysses, n, subs),
-        mesh=mesh,
-        in_specs=placed,
-        out_specs=P(("groups", "seq", "head", "sub"), None),
-        check_vma=False,
-    )
+    n_seq = mesh.shape["seq"]
+    body = functools.partial(ulysses, n, subs)
+    if (mesh.shape["head"], subs, n_seq) == (2, 2, 4):
+        body = functools.partial(pipelined, n_seq, uneven)
+    if (mesh.shape["head"], subs, n_seq) != (2, 2, 4):
+        return placed_map(body, mesh, placed)
+
+    def step(*args):
+        return body(*args)
+
+    return placed_map(step, mesh, placed)

time: 133 us -> 94.3 us (0.71)
  the two profiles are of different devices: /device:TPU:0 before, /device:TPU:9 now
where the time goes in v2:
time: 94.3 us; the launch traced here: 94.1 us
  waiting for transfers between devices  57.5 us (61%)
  starting transfers between devices  16.7 us (18%)
  Pallas kernels  15.5 us (16%)
  local copies, waits for them, and re-layouts  4.25 us (5%)
    ppermute x6, waiting for transfers between devices, along(): return lax.ppermute(x, 'seq', [(i, i ^ d) for i in range(n_seq)])  48 us
    pallas_call x6, Pallas kernels, call(): pl.pallas_call(kernel, out_shape=[jax.ShapeDtypeStruct(*o) if isinstance(...  13.7 us
    ppermute x12, starting transfers between devices, exchange(): return lax.ppermute(x, ('head', 'sub'), [(i, i ^ d) for i in range(n)])  10.6 us
    ppermute x12, waiting for transfers between devices, exchange(): return lax.ppermute(x, ('head', 'sub'), [(i, i ^ d) for i in range(n)])  9.57 us
    ppermute x6, starting transfers between devices, along(): return lax.ppermute(x, 'seq', [(i, i ^ d) for i in range(n_seq)])  6.11 us
    unnamed x18, local copies, waits for them, and re-layouts  4.25 us
  transfers between devices with their start and end apart: 18, of which 8 were waited for; matrix products, arithmetic and copies ran while one was open for 0% of the time, Pallas kernels for 15%

profile of v2, /device:TPU:9, one launch (start us, length us, event | category | flops | bytes accessed | tf_op | source)
XLA Modules:
  0.0 94.1 jit_solution(12326652506635968972)
XLA Ops:
  0.0 0.0 copy-start
  0.0 1.4 %copy-done = bf16[96,8192]{1,0:T(8,128)(2,1)S(1)} copy-done((bf16[96,8192]{1,0:T(8,128)(2,1)S(1)}, bf16[96,8192]{1,0:T(8,128)(2,1)}, u32[]{:S(2)}) %copy-start) | copy-done | bytes 1572888
  1.4 0.0 copy-start.2
  1.4 1.4 %copy-done.2 = bf16[96,8192]{1,0:T(8,128)(2,1)S(1)} copy-done((bf16[96,8192]{1,0:T(8,128)(2,1)S(1)}, bf16[96,8192]{1,0:T(8,128)(2,1)}, u32[]{:S(2)}) %copy-start.2) | copy-done | bytes 1572888
  2.8 0.0 copy-start.4
  2.8 1.4 %copy-done.4 = bf16[96,8192]{1,0:T(8,128)(2,1)S(1)} copy-done((bf16[96,8192]{1,0:T(8,128)(2,1)S(1)}, bf16[96,8192]{1,0:T(8,128)(2,1)}, u32[]{:S(2)}) %copy-start.4) | copy-done | bytes 1572888
  4.2 0.0 copy-start.6
  4.2 0.0 copy-start.7
  4.2 0.0 copy-start.8
  4.2 0.0 copy-start.3
  4.2 0.0 copy-start.5
  4.2 0.4 shard_map.64
  4.7 0.0 copy-start.1
  4.7 0.7 collective-permute-start.9
  5.4 1.2 %collective-permute-start.10 = (bf16[96,3840]{1,0:T(8,128)(2,1)S(1)}, bf16[96,3840]{1,0:T(8,128)(2,1)S(1)}, u32[]{:S(2)}, u32[]{:S(2)}) collective-permute-start(bf16[96,3840]{1,0:T(8,128)(2,1)S(1)} %get-tuple-element.46), channel_id=1, source_target_pairs={{0,2},{1,3},{2,0},{3,1},{4,6},{5,7},{6,4},{7,5},{8,10},{9,11},{10,... | collective-permute-start | bytes 2211848 | tf_op jit(solution)/shard_map/ppermute | solution.py:308
  6.7 0.0 copy-done.6
  6.7 0.0 copy-done.7
  6.7 0.0 copy-done.8
  6.7 1.2 %shard_map.65 = (bf16[128,1280]{1,0:T(8,128)(2,1)S(1)}, bf16[128,1280]{1,0:T(8,128)(2,1)S(1)}, bf16[128,1280]{1,0:T(8,128)(2,1)S(1)}, bf16[128,1280]{1,0:T(8,128...) custom-call(s32[2,4]{1,0:T(2,128)S(1)} %bitcast.1, ...), custom_call_target="tpu_custom_call" | custom-call | tf_op jit(solution)/shard_map/pallas_call | solution.py:289
  7.8 0.2 collective-permute-start.12
  8.1 1.3 %collective-permute-start.3 = (bf16[128,768]{1,0:T(8,128)(2,1)S(1)}, bf16[128,768]{1,0:T(8,128)(2,1)S(1)}, u32[]{:S(2)}, u32[]{:S(2)}) collective-permute-start(bf16[128,768]{1,0:T(8,128)(2,1)S(1)} %get-tuple-element.38), channel_id=1, source_target_pairs={{0,4},{4,0},{8,12},{12,8},{1,5},{5,1},{9,13},{13,9},{2,6},{6,2},{1... | collective-permute-start | bytes 589832 | tf_op jit(solution)/shard_map/ppermute | solution.py:311
  9.4 1.4 %collective-permute-start.11 = (bf16[96,3840]{1,0:T(8,128)(2,1)S(1)}, bf16[96,3840]{1,0:T(8,128)(2,1)S(1)}, u32[]{:S(2)}, u32[]{:S(2)}) collective-permute-start(bf16[96,3840]{1,0:T(8,128)(2,1)S(1)} %get-tuple-element.47), channel_id=1, source_target_pairs={{0,3},{1,2},{2,1},{3,0},{4,7},{5,6},{6,5},{7,4},{8,11},{9,10},{10,... | collective-permute-start | bytes 2211848 | tf_op jit(solution)/shard_map/ppermute | solution.py:308
  10.8 10.2 %collective-permute-done.3.refs_5_ = bf16[128,768]{1,0:T(8,128)(2,1)S(1)} collective-permute-done((bf16[128,768]{1,0:T(8,128)(2,1)S(1)}, bf16[128,768]{1,0:T(8,128)(2,1)S(1)}, u32[]{:S(2)}, u32[]{:S(2)}) %collective-permute-start.3) | collective-permute-done | bytes 196640 | tf_op jit(solution)/shard_map/ppermute | solution.py:311
  21.0 2.3 %collective-permute-start.13 = (bf16[128,1280]{1,0:T(8,128)(2,1)S(1)}, bf16[128,1280]{1,0:T(8,128)(2,1)S(1)}, u32[]{:S(2)}, u32[]{:S(2)}) collective-permute-start(bf16[128,1280]{1,0:T(8,128)(2,1)S(1)} %get-tuple-element.49), channel_id=1, source_target_pairs={{0,8},{4,12},{8,0},{12,4},{1,9},{5,13},{9,1},{13,5},{2,10},{6,14},... | collective-permute-start | bytes 983048 | tf_op jit(solution)/shard_map/ppermute | solution.py:311
  23.3 0.0 collective-permute-done.12.refs_5_
  23.3 0.0 collective-permute-start.14
  23.3 0.0 copy-done.3
  23.3 0.0 copy-done.5
  23.3 0.0 copy-done.1
  23.3 0.3 shard_map.66
  23.7 21.0 %collective-permute-done.13.refs_6_ = bf16[128,1280]{1,0:T(8,128)(2,1)S(1)} collective-permute-done((bf16[128,1280]{1,0:T(8,128)(2,1)S(1)}, bf16[128,1280]{1,0:T(8,128)(2,1)S(1)}, u32[]{:S(2)}, u32[]{:S(2)}) %collective-permute-start.13) | collective-permute-done | bytes 327712 | tf_op jit(solution)/shard_map/ppermute | solution.py:311
  44.7 0.6 collective-permute-start
  45.3 6.4 %collective-permute-done.14.refs_7_ = bf16[128,1280]{1,0:T(8,128)(2,1)S(1)} collective-permute-done((bf16[128,1280]{1,0:T(8,128)(2,1)S(1)}, bf16[128,1280]{1,0:T(8,128)(2,1)S(1)}, u32[]{:S(2)}, u32[]{:S(2)}) %collective-permute-start.14) | collective-permute-done | bytes 327712 | tf_op jit(solution)/shard_map/ppermute | solution.py:311
  51.7 0.0 collective-permute-start.1
  51.7 0.0 collective-permute-done.9.refs_1_
  51.7 2.1 %collective-permute-start.2 = (bf16[96,2304]{1,0:T(8,128)(2,1)S(1)}, bf16[96,2304]{1,0:T(8,128)(2,1)S(1)}, u32[]{:S(2)}, u32[]{:S(2)}) collective-permute-start(bf16[96,2304]{1,0:T(8,128)(2,1)S(1)} %get-tuple-element.36), channel_id=1, source_target_pairs={{0,3},{1,2},{2,1},{3,0},{4,7},{5,6},{6,5},{7,4},{8,11},{9,10},{10,... | collective-permute-start | bytes 1327112 | tf_op jit(solution)/shard_map/ppermute | solution.py:308
  53.8 0.0 collective-permute-done.10.refs_2_
  53.8 0.0 collective-permute-start.4
  53.8 0.0 collective-permute-done.11.refs_3_
  53.8 2.3 %collective-permute-start.5 = (bf16[128,768]{1,0:T(8,128)(2,1)S(1)}, bf16[128,768]{1,0:T(8,128)(2,1)S(1)}, u32[]{:S(2)}, u32[]{:S(2)}) collective-permute-start(bf16[128,768]{1,0:T(8,128)(2,1)S(1)} %get-tuple-element.40), channel_id=1, source_target_pairs={{0,12},{4,8},{8,4},{12,0},{1,13},{5,9},{9,5},{13,1},{2,14},{6,10},... | collective-permute-start | bytes 589832 | tf_op jit(solution)/shard_map/ppermute | solution.py:311
  56.1 0.2 shard_map.67
  56.3 7.1 %shard_map.69 = (bf16[96,1280]{1,0:T(8,128)(2,1)S(1)}, bf16[96,1280]{1,0:T(8,128)(2,1)S(1)}, bf16[96,1280]{1,0:T(8,128)(2,1)S(1)}, bf16[96,1280]{1,0:T(8,128)(2,1)S(1)}) custom-call(s32[2,4]{1,0:T(2,128)S(1)} %bitcast.2, f32[192,256]{1,0:T(8,128)S(1)} %get-tuple-element.31.bias, bf16[96,3840]{1,0:T(8,128)(2,1)S(1)} %get-tuple-element.45.refs_0_, ...), custom_call_target="tpu_custom_call" | custom-call | tf_op jit(solution)/shard_map/pallas_call | solution.py:289
  63.4 3.5 %collective-permute-done.4.refs_6_ = bf16[128,768]{1,0:T(8,128)(2,1)S(1)} collective-permute-done((bf16[128,768]{1,0:T(8,128)(2,1)S(1)}, bf16[128,768]{1,0:T(8,128)(2,1)S(1)}, u32[]{:S(2)}, u32[]{:S(2)}) %collective-permute-start.4) | collective-permute-done | bytes 196640 | tf_op jit(solution)/shard_map/ppermute | solution.py:311
  67.0 0.2 collective-permute-start.15
  67.2 6.8 %collective-permute-done.5.refs_7_ = bf16[128,768]{1,0:T(8,128)(2,1)S(1)} collective-permute-done((bf16[128,768]{1,0:T(8,128)(2,1)S(1)}, bf16[128,768]{1,0:T(8,128)(2,1)S(1)}, u32[]{:S(2)}, u32[]{:S(2)}) %collective-permute-start.5) | collective-permute-done | bytes 196640 | tf_op jit(solution)/shard_map/ppermute | solution.py:311
  74.0 0.0 collective-permute-start.16
  74.0 0.0 collective-permute-done.refs_1_
  74.0 2.0 %collective-permute-start.17 = (bf16[96,1280]{1,0:T(8,128)(2,1)S(1)}, bf16[96,1280]{1,0:T(8,128)(2,1)S(1)}, u32[]{:S(2)}, u32[]{:S(2)}) collective-permute-start(bf16[96,1280]{1,0:T(8,128)(2,1)S(1)} %get-tuple-element.54), channel_id=1, source_target_pairs={{0,3},{1,2},{2,1},{3,0},{4,7},{5,6},{6,5},{7,4},{8,11},{9,10},{10,... | collective-permute-start | bytes 737288 | tf_op jit(solution)/shard_map/ppermute | solution.py:308
  76.0 0.0 collective-permute-done.1.refs_2_
  76.0 0.0 collective-permute-done.2.refs_3_
  76.0 4.5 %shard_map.68 = (bf16[96,768]{1,0:T(8,128)(2,1)S(1)}, bf16[96,768]{1,0:T(8,128)(2,1)S(1)}, bf16[96,768]{1,0:T(8,128)(2,1)S(1)}, bf16[96,768]{1,0:T(8,128)(2,1)S(1)}) custom-call(s32[2,4]{1,0:T(2,128)S(1)} %bitcast.3, f32[192,256]{1,0:T(8,128)S(1)} %get-tuple-element.31.bias, bf16[96,2304]{1,0:T(8,128)(2,1)S(1)} %get-tuple-element.34.refs_0_, ...), custom_call_target="tpu_custom_call" | custom-call | tf_op jit(solution)/shard_map/pallas_call | solution.py:289
  80.5 0.1 collective-permute-start.6
  80.6 0.3 collective-permute-start.7
  80.8 0.0 collective-permute-done.15.refs_1_
  80.8 1.9 %collective-permute-start.8 = (bf16[96,768]{1,0:T(8,128)(2,1)S(1)}, bf16[96,768]{1,0:T(8,128)(2,1)S(1)}, u32[]{:S(2)}, u32[]{:S(2)}) collective-permute-start(bf16[96,768]{1,0:T(8,128)(2,1)S(1)} %get-tuple-element.44), channel_id=1, source_target_pairs={{0,3},{1,2},{2,1},{3,0},{4,7},{5,6},{6,5},{7,4},{8,11},{9,10},{10,... | collective-permute-start | bytes 442376 | tf_op jit(solution)/shard_map/ppermute | solution.py:308
  82.7 0.0 collective-permute-done.16.refs_2_
  82.7 5.1 %collective-permute-done.17.refs_3_ = bf16[96,1280]{1,0:T(8,128)(2,1)S(1)} collective-permute-done((bf16[96,1280]{1,0:T(8,128)(2,1)S(1)}, bf16[96,1280]{1,0:T(8,128)(2,1)S(1)}, u32[]{:S(2)}, u32[]{:S(2)}) %collective-permute-start.17) | collective-permute-done | bytes 245792 | tf_op jit(solution)/shard_map/ppermute | solution.py:308
  87.8 1.0 %shard_map.70.refs_4_ = bf16[96,8192]{1,0:T(8,128)(2,1)} custom-call(bf16[96,1280]{1,0:T(8,128)(2,1)S(1)} %get-tuple-element.51.refs_0_, bf16[96,1280]{1,0:T(8,128)(2,1)S(1)} %collective-permute-done.15.refs_1_, bf16[96,1280]{1,0:T(8,128)(2,1)S(1)} %collective-permute-done.16.refs_2_, bf16[96,1280]{1,0:T(8,128)(2,1)S(1)} %collective-permute-done.17.refs_3_), custom_call_target="tpu_custom_call" | custom-call | tf_op jit(solution)/shard_map/pallas_call | solution.py:362
  88.7 0.0 collective-permute-done.6.refs_1_
  88.7 0.8 collective-permute-done.7.refs_2_
  89.5 3.7 %collective-permute-done.8.refs_3_ = bf16[96,768]{1,0:T(8,128)(2,1)S(1)} collective-permute-done((bf16[96,768]{1,0:T(8,128)(2,1)S(1)}, bf16[96,768]{1,0:T(8,128)(2,1)S(1)}, u32[]{:S(2)}, u32[]{:S(2)}) %collective-permute-start.8) | collective-permute-done | bytes 147488 | tf_op jit(solution)/shard_map/ppermute | solution.py:308
  93.2 0.8 shard_map.71
Async XLA Ops:
  0.0 1.4 %copy-start = (bf16[96,8192]{1,0:T(8,128)(2,1)S(1)}, bf16[96,8192]{1,0:T(8,128)(2,1)}, u32[]{:S(2)}) copy-start(bf16[96,8192]{1,0:T(8,128)(2,1)} %q.5) | copy-start | bytes 4718596
  1.4 1.4 %copy-start.2 = (bf16[96,8192]{1,0:T(8,128)(2,1)S(1)}, bf16[96,8192]{1,0:T(8,128)(2,1)}, u32[]{:S(2)}) copy-start(bf16[96,8192]{1,0:T(8,128)(2,1)} %k.5) | copy-start | bytes 4718596
  2.8 1.4 %copy-start.4 = (bf16[96,8192]{1,0:T(8,128)(2,1)S(1)}, bf16[96,8192]{1,0:T(8,128)(2,1)}, u32[]{:S(2)}) copy-start(bf16[96,8192]{1,0:T(8,128)(2,1)} %v.5) | copy-start | bytes 4718596
  4.2 2.4 %copy-start.6 = (bf16[256,2048]{1,0:T(8,128)(2,1)S(1)}, bf16[256,2048]{1,0:T(8,128)(2,1)}, u32[]{:S(2)}) copy-start(bf16[256,2048]{1,0:T(8,128)(2,1)} %kc.1) | copy-start | bytes 3145732
  4.2 2.4 %copy-start.7 = (bf16[256,2048]{1,0:T(8,128)(2,1)S(1)}, bf16[256,2048]{1,0:T(8,128)(2,1)}, u32[]{:S(2)}) copy-start(bf16[256,2048]{1,0:T(8,128)(2,1)} %vc.1) | copy-start | bytes 3145732
  4.2 2.4 %copy-start.8 = (s32[4,2]{0,1:T(2,128)S(1)}, s32[4,2]{0,1:T(2,128)}, u32[]{:S(2)}) copy-start(s32[4,2]{0,1:T(2,128)} %param.11) | copy-start | bytes 100
  4.2 19.1 %copy-start.3 = (bf16[96,8192]{1,0:T(8,128)(2,1)S(1)}, bf16[96,8192]{1,0:T(8,128)(2,1)}, u32[]{:S(2)}) copy-start(bf16[96,8192]{1,0:T(8,128)(2,1)} %k.5) | copy-start | bytes 4718596
  4.2 19.1 %copy-start.5 = (bf16[96,8192]{1,0:T(8,128)(2,1)S(1)}, bf16[96,8192]{1,0:T(8,128)(2,1)}, u32[]{:S(2)}) copy-start(bf16[96,8192]{1,0:T(8,128)(2,1)} %v.5) | copy-start | bytes 4718596
  4.7 18.7 %copy-start.1 = (bf16[96,8192]{1,0:T(8,128)(2,1)S(1)}, bf16[96,8192]{1,0:T(8,128)(2,1)}, u32[]{:S(2)}) copy-start(bf16[96,8192]{1,0:T(8,128)(2,1)} %q.5) | copy-start | bytes 4718596
  4.7 47.0 %collective-permute-start.9 = (bf16[96,3840]{1,0:T(8,128)(2,1)S(1)}, bf16[96,3840]{1,0:T(8,128)(2,1)S(1)}, u32[]{:S(2)}, u32[]{:S(2)}) collective-permute-start(bf16[96,3840]{1,0:T(8,128)(2,1)S(1)} %get-tuple-element.30.after), channel_id=1, source_target_pairs={{0,1},{1,0},{2,3},{3,2},{4,5},{5,4},{6,7},{7,6},{8,9},{9,8},{10,11... | collective-permute-start | bytes 2211848 | tf_op jit(solution)/shard_map/ppermute | solution.py:308
  5.4 48.4 %collective-permute-start.10 = (bf16[96,3840]{1,0:T(8,128)(2,1)S(1)}, bf16[96,3840]{1,0:T(8,128)(2,1)S(1)}, u32[]{:S(2)}, u32[]{:S(2)}) collective-permute-start(bf16[96,3840]{1,0:T(8,128)(2,1)S(1)} %get-tuple-element.46), channel_id=1, source_target_pairs={{0,2},{1,3},{2,0},{3,1},{4,6},{5,7},{6,4},{7,5},{8,10},{9,11},{10,... | collective-permute-start | bytes 2211848 | tf_op jit(solution)/shard_map/ppermute | solution.py:308
  7.8 15.5 %collective-permute-start.12 = (bf16[128,1280]{1,0:T(8,128)(2,1)S(1)}, bf16[128,1280]{1,0:T(8,128)(2,1)S(1)}, u32[]{:S(2)}, u32[]{:S(2)}) collective-permute-start(bf16[128,1280]{1,0:T(8,128)(2,1)S(1)} %get-tuple-element.32.after), channel_id=1, source_target_pairs={{0,4},{4,0},{8,12},{12,8},{1,5},{5,1},{9,13},{13,9},{2,6},{6,2},{1... | collective-permute-start | bytes 983048 | tf_op jit(solution)/shard_map/ppermute | solution.py:311
  8.1 13.0 %collective-permute-start.3 = (bf16[128,768]{1,0:T(8,128)(2,1)S(1)}, bf16[128,768]{1,0:T(8,128)(2,1)S(1)}, u32[]{:S(2)}, u32[]{:S(2)}) collective-permute-start(bf16[128,768]{1,0:T(8,128)(2,1)S(1)} %get-tuple-element.38), channel_id=1, source_target_pairs={{0,4},{4,0},{8,12},{12,8},{1,5},{5,1},{9,13},{13,9},{2,6},{6,2},{1... | collective-permute-start | bytes 589832 | tf_op jit(solution)/shard_map/ppermute | solution.py:311
  9.4 44.5 %collective-permute-start.11 = (bf16[96,3840]{1,0:T(8,128)(2,1)S(1)}, bf16[96,3840]{1,0:T(8,128)(2,1)S(1)}, u32[]{:S(2)}, u32[]{:S(2)}) collective-permute-start(bf16[96,3840]{1,0:T(8,128)(2,1)S(1)} %get-tuple-element.47), channel_id=1, source_target_pairs={{0,3},{1,2},{2,1},{3,0},{4,7},{5,6},{6,5},{7,4},{8,11},{9,10},{10,... | collective-permute-start | bytes 2211848 | tf_op jit(solution)/shard_map/ppermute | solution.py:308
  21.0 23.7 %collective-permute-start.13 = (bf16[128,1280]{1,0:T(8,128)(2,1)S(1)}, bf16[128,1280]{1,0:T(8,128)(2,1)S(1)}, u32[]{:S(2)}, u32[]{:S(2)}) collective-permute-start(bf16[128,1280]{1,0:T(8,128)(2,1)S(1)} %get-tuple-element.49), channel_id=1, source_target_pairs={{0,8},{4,12},{8,0},{12,4},{1,9},{5,13},{9,1},{13,5},{2,10},{6,14},... | collective-permute-start | bytes 983048 | tf_op jit(solution)/shard_map/ppermute | solution.py:311
  23.3 28.4 %collective-permute-start.14 = (bf16[128,1280]{1,0:T(8,128)(2,1)S(1)}, bf16[128,1280]{1,0:T(8,128)(2,1)S(1)}, u32[]{:S(2)}, u32[]{:S(2)}) collective-permute-start(bf16[128,1280]{1,0:T(8,128)(2,1)S(1)} %get-tuple-element.50), channel_id=1, source_target_pairs={{0,12},{4,8},{8,4},{12,0},{1,13},{5,9},{9,5},{13,1},{2,14},{6,10},... | collective-permute-start | bytes 983048 | tf_op jit(solution)/shard_map/ppermute | solution.py:311
  44.7 29.3 %collective-permute-start = (bf16[96,2304]{1,0:T(8,128)(2,1)S(1)}, bf16[96,2304]{1,0:T(8,128)(2,1)S(1)}, u32[]{:S(2)}, u32[]{:S(2)}) collective-permute-start(bf16[96,2304]{1,0:T(8,128)(2,1)S(1)} %get-tuple-element.33.after), channel_id=1, source_target_pairs={{0,1},{1,0},{2,3},{3,2},{4,5},{5,4},{6,7},{7,6},{8,9},{9,8},{10,11... | collective-permute-start | bytes 1327112 | tf_op jit(solution)/shard_map/ppermute | solution.py:308
  51.7 24.3 %collective-permute-start.1 = (bf16[96,2304]{1,0:T(8,128)(2,1)S(1)}, bf16[96,2304]{1,0:T(8,128)(2,1)S(1)}, u32[]{:S(2)}, u32[]{:S(2)}) collective-permute-start(bf16[96,2304]{1,0:T(8,128)(2,1)S(1)} %get-tuple-element.35), channel_id=1, source_target_pairs={{0,2},{1,3},{2,0},{3,1},{4,6},{5,7},{6,4},{7,5},{8,10},{9,11},{10,... | collective-permute-start | bytes 1327112 | tf_op jit(solution)/shard_map/ppermute | solution.py:308
  51.7 24.3 %collective-permute-start.2 = (bf16[96,2304]{1,0:T(8,128)(2,1)S(1)}, bf16[96,2304]{1,0:T(8,128)(2,1)S(1)}, u32[]{:S(2)}, u32[]{:S(2)}) collective-permute-start(bf16[96,2304]{1,0:T(8,128)(2,1)S(1)} %get-tuple-element.36), channel_id=1, source_target_pairs={{0,3},{1,2},{2,1},{3,0},{4,7},{5,6},{6,5},{7,4},{8,11},{9,10},{10,... | collective-permute-start | bytes 1327112 | tf_op jit(solution)/shard_map/ppermute | solution.py:308
  53.8 13.2 %collective-permute-start.4 = (bf16[128,768]{1,0:T(8,128)(2,1)S(1)}, bf16[128,768]{1,0:T(8,128)(2,1)S(1)}, u32[]{:S(2)}, u32[]{:S(2)}) collective-permute-start(bf16[128,768]{1,0:T(8,128)(2,1)S(1)} %get-tuple-element.39), channel_id=1, source_target_pairs={{0,8},{4,12},{8,0},{12,4},{1,9},{5,13},{9,1},{13,5},{2,10},{6,14},... | collective-permute-start | bytes 589832 | tf_op jit(solution)/shard_map/ppermute | solution.py:311
  53.8 20.1 %collective-permute-start.5 = (bf16[128,768]{1,0:T(8,128)(2,1)S(1)}, bf16[128,768]{1,0:T(8,128)(2,1)S(1)}, u32[]{:S(2)}, u32[]{:S(2)}) collective-permute-start(bf16[128,768]{1,0:T(8,128)(2,1)S(1)} %get-tuple-element.40), channel_id=1, source_target_pairs={{0,12},{4,8},{8,4},{12,0},{1,13},{5,9},{9,5},{13,1},{2,14},{6,10},... | collective-permute-start | bytes 589832 | tf_op jit(solution)/shard_map/ppermute | solution.py:311
  67.0 13.8 %collective-permute-start.15 = (bf16[96,1280]{1,0:T(8,128)(2,1)S(1)}, bf16[96,1280]{1,0:T(8,128)(2,1)S(1)}, u32[]{:S(2)}, u32[]{:S(2)}) collective-permute-start(bf16[96,1280]{1,0:T(8,128)(2,1)S(1)} %get-tuple-element.52), channel_id=1, source_target_pairs={{0,1},{1,0},{2,3},{3,2},{4,5},{5,4},{6,7},{7,6},{8,9},{9,8},{10,11... | collective-permute-start | bytes 737288 | tf_op jit(solution)/shard_map/ppermute | solution.py:308
  74.0 8.7 %collective-permute-start.16 = (bf16[96,1280]{1,0:T(8,128)(2,1)S(1)}, bf16[96,1280]{1,0:T(8,128)(2,1)S(1)}, u32[]{:S(2)}, u32[]{:S(2)}) collective-permute-start(bf16[96,1280]{1,0:T(8,128)(2,1)S(1)} %get-tuple-element.53), channel_id=1, source_target_pairs={{0,2},{1,3},{2,0},{3,1},{4,6},{5,7},{6,4},{7,5},{8,10},{9,11},{10,... | collective-permute-start | bytes 737288 | tf_op jit(solution)/shard_map/ppermute | solution.py:308
  74.0 13.8 %collective-permute-start.17 = (bf16[96,1280]{1,0:T(8,128)(2,1)S(1)}, bf16[96,1280]{1,0:T(8,128)(2,1)S(1)}, u32[]{:S(2)}, u32[]{:S(2)}) collective-permute-start(bf16[96,1280]{1,0:T(8,128)(2,1)S(1)} %get-tuple-element.54), channel_id=1, source_target_pairs={{0,3},{1,2},{2,1},{3,0},{4,7},{5,6},{6,5},{7,4},{8,11},{9,10},{10,... | collective-permute-start | bytes 737288 | tf_op jit(solution)/shard_map/ppermute | solution.py:308
  80.5 8.3 %collective-permute-start.6 = (bf16[96,768]{1,0:T(8,128)(2,1)S(1)}, bf16[96,768]{1,0:T(8,128)(2,1)S(1)}, u32[]{:S(2)}, u32[]{:S(2)}) collective-permute-start(bf16[96,768]{1,0:T(8,128)(2,1)S(1)} %get-tuple-element.42), channel_id=1, source_target_pairs={{0,1},{1,0},{2,3},{3,2},{4,5},{5,4},{6,7},{7,6},{8,9},{9,8},{10,11... | collective-permute-start | bytes 442376 | tf_op jit(solution)/shard_map/ppermute | solution.py:308
  80.6 8.9 %collective-permute-start.7 = (bf16[96,768]{1,0:T(8,128)(2,1)S(1)}, bf16[96,768]{1,0:T(8,128)(2,1)S(1)}, u32[]{:S(2)}, u32[]{:S(2)}) collective-permute-start(bf16[96,768]{1,0:T(8,128)(2,1)S(1)} %get-tuple-element.43), channel_id=1, source_target_pairs={{0,2},{1,3},{2,0},{3,1},{4,6},{5,7},{6,4},{7,5},{8,10},{9,11},{10,... | collective-permute-start | bytes 442376 | tf_op jit(solution)/shard_map/ppermute | solution.py:308
  80.8 12.4 %collective-permute-start.8 = (bf16[96,768]{1,0:T(8,128)(2,1)S(1)}, bf16[96,768]{1,0:T(8,128)(2,1)S(1)}, u32[]{:S(2)}, u32[]{:S(2)}) collective-permute-start(bf16[96,768]{1,0:T(8,128)(2,1)S(1)} %get-tuple-element.44), channel_id=1, source_target_pairs={{0,3},{1,2},{2,1},{3,0},{4,7},{5,6},{6,5},{7,4},{8,11},{9,10},{10,... | collective-permute-start | bytes 442376 | tf_op jit(solution)/shard_map/ppermute | solution.py:308

commit v3 on v1

--- a/solution.py
+++ b/solution.py
@@ -7,10 +7,12 @@
 from jax.experimental.pallas import tpu as pltpu
 from jax.sharding import PartitionSpec as P
 
+
 HD = 128
 BLOCK = 64
 LOG2E = 1.4426950408889634
 MASKED = -1e30
+VMEM_LIMIT = 16 << 20
 
 
 def softmax_rows(scores, values):
@@ -64,7 +66,7 @@
                 values.append(v_all[: i * step, col])
             scores.append(jnp.where(causal, logits(q, k_all[here, col], factor), MASKED))
             values.append(v_all[here, col])
-            mixed, top, total = softmax_rows(scores, values)
+            mixed, _, total = softmax_rows(scores, values)
             out_ref[here, col] = (mixed / total).astype(jnp.bfloat16)
 
 
@@ -135,6 +137,402 @@
     return result
 
 
+def chip_bias(bias, place, rows):
+    def token(at):
+        return jnp.where(at < rows, place * rows + at, (1 - place) * rows + at - rows)
+
+    q = token(lax.broadcasted_iota(jnp.int32, bias.shape, 0))
+    k = lax.broadcasted_iota(jnp.int32, bias.shape, 1)
+    bias[...] = jnp.where((k >= 2 * rows) | (q >= token(k)), 0.0, MASKED)
+
+
+def biased(scores, seen, bias):
+    masked = min(bias.shape[1], scores.shape[1] - seen)
+    parts = [scores[:, seen : seen + masked] + bias[:, :masked]]
+    if seen > 0:
+        parts.insert(0, scores[:, :seen])
+    if scores.shape[1] > seen + masked:
+        parts.append(scores[:, seen + masked :])
+    return jnp.concatenate(parts, axis=1)
+
+
+def soft(scores, values):
+    top = jnp.max(scores, axis=1, keepdims=True)
+    weights = jnp.exp2(scores - top)
+    total = jnp.sum(weights, axis=1, keepdims=True)
+    mixed = jnp.dot(weights.astype(jnp.bfloat16), values, preferred_element_type=jnp.float32)
+    return mixed, top, total
+
+
+def held(sel_ref, row, owner, blk_dev):
+    inner = jnp.int32(0)
+    for t in range(sel_ref.shape[0]):
+        picked = sel_ref[t, row]
+        match = lax.div(picked, jnp.int32(blk_dev)) == owner
+        inner = jnp.where(match, lax.rem(picked, jnp.int32(blk_dev)), inner)
+    return inner
+
+
+def group_index():
+    return lax.axis_index("head") * 2 + lax.axis_index("sub")
+
+
+def run_copies(pairs, sems):
+    copies = [pltpu.make_async_copy(a, b, sems.at[i]) for i, (a, b) in enumerate(pairs)]
+    for copy in copies:
+        copy.start()
+    for copy in copies:
+        copy.wait()
+
+
+def cross_kernel(width, start, size, q, k, v, after, two, three, sems):
+    def pairs(arrays):
+        result = []
+        for out, d in ((two, 2), (three, 3)):
+            at = (group_index() ^ d) * width + start
+            cols = pl.ds(pl.multiple_of(at, HD), size)
+            for i, array in enumerate(arrays):
+                result.append((array.at[:, cols], out.at[:, i * size : (i + 1) * size]))
+        return result
+
+    @pl.when(lax.axis_index("head") == 0)
+    def _():
+        run_copies(pairs((k, v)), sems)
+
+    @pl.when(lax.axis_index("head") == 1)
+    def _():
+        run_copies(pairs((q, q)), sems)
+
+
+def core_kernel(width, start, size, flip, q, k, v, after, out, sems):
+    pairs = []
+    for i in range(2):
+        at = (2 * i + (lax.axis_index("sub") ^ flip)) * width + start
+        cols = pl.ds(pl.multiple_of(at, HD), size)
+        for t, array in enumerate((q, k, v)):
+            to = (3 * i + t) * size
+            pairs.append((array.at[:, cols], out.at[:, to : to + size]))
+    run_copies(pairs, sems)
+
+
+def sends_kernel(n_seq, blk_dev, rows, chunks, sel_ref, kc, vc, *refs):
+    outs, bias, sems = refs[:-2], refs[-2], refs[-1]
+    me = lax.axis_index("seq")
+    pairs = []
+    for i, (start, size) in enumerate(chunks):
+        for d in range(n_seq):
+            inner = held(sel_ref, me ^ d, me, blk_dev)
+            at = pl.ds(pl.multiple_of(inner * BLOCK, BLOCK), BLOCK)
+            to = outs[i * n_seq + d]
+            pairs.append((kc.at[at, start : start + size], to.at[:BLOCK]))
+            pairs.append((vc.at[at, start : start + size], to.at[BLOCK:]))
+    copies = [pltpu.make_async_copy(a, b, sems.at[i]) for i, (a, b) in enumerate(pairs)]
+    for copy in copies:
+        copy.start()
+    chip_bias(bias, lax.axis_index("sub"), rows)
+    for copy in copies:
+        copy.wait()
+
+
+def collect_kernel(blk_dev, sel_ref, *refs):
+    sources, kept = refs[:-1], refs[-1]
+    me = lax.axis_index("seq")
+    topk = sel_ref.shape[0]
+    for t in range(topk):
+        distance = lax.div(sel_ref[t, me], jnp.int32(blk_dev)) ^ me
+        for d, source in enumerate(sources):
+
+            @pl.when(distance == d)
+            def _():
+                kept[t * BLOCK : (t + 1) * BLOCK] = source[:BLOCK]
+                kept[(topk + t) * BLOCK : (topk + t + 1) * BLOCK] = source[BLOCK:]
+
+
+def lane_put(into, lane, column):
+    lanes = lax.broadcasted_iota(jnp.int32, into.shape, 1)
+    return jnp.where(lanes == lane, column, into)
+
+
+def early_kernel(per, size, factor, bias, own, par, two, three, kept, loc0, loc1, part0, part1):
+    rows = own.shape[0]
+    heads = size // HD
+    locs, parts = (loc0, loc1), (part0, part1)
+    for loc in locs:
+        loc[:, size:] = jnp.zeros((rows, HD), jnp.float32)
+
+    def columns(h, j):
+        head = (h * per + j) * HD
+
+        def pick(t):
+            at = pl.ds(pl.multiple_of(t * size + head, HD), HD)
+            return jnp.concatenate([own[:, at], par[:, at]], axis=0)
+
+        return pl.ds(pl.multiple_of(head, HD), HD), pick
+
+    def put(lane, top, total):
+        for i, loc in enumerate(locs):
+            at = slice(i * rows, (i + 1) * rows)
+            stat = lane_put(loc[:, size:], lane, top[at])
+            loc[:, size:] = lane_put(stat, lane + 1, total[at])
+
+    def first_chip(h, carry):
+        for j in range(per):
+            col, pick = columns(h, j)
+            k = jnp.concatenate([kept[: 2 * BLOCK, col], pick(1)], axis=0)
+            v = jnp.concatenate([kept[2 * BLOCK :, col], pick(2)], axis=0)
+            mixed, top, total = soft(biased(logits(pick(0), k, factor), 2 * BLOCK, bias), v)
+            mixed = mixed * (1.0 / total)
+            loc0[:, col], loc1[:, col] = mixed[:rows], mixed[rows:]
+            q = jnp.concatenate([two[:, col], three[:, col]], axis=0)
+            mixed, top, total = soft(logits(q, k, factor), v)
+            mixed = (mixed * (1.0 / total)).astype(jnp.bfloat16)
+            part0[:, col], part1[:, col] = mixed[:rows], mixed[rows:]
+            put((h * per + j) * 2, top, total)
+        return carry
+
+    def second_chip(h, carry):
+        for j in range(per):
+            col, pick = columns(h, j)
+            mixed, top, total = soft(biased(logits(pick(0), pick(1), factor), 0, bias), pick(2))
+            loc0[:, col], loc1[:, col] = mixed[:rows], mixed[rows:]
+            put((h * per + j) * 2, top, total)
+        return carry
+
+    @pl.when(lax.axis_index("head") == 0)
+    def _():
+        lax.fori_loop(0, heads // per, first_chip, 0)
+        for loc, part in zip(locs, parts):
+            left = loc[:, size:]
+            packed = jnp.zeros_like(left)
+            for t in range(3):
+                piece = left.astype(jnp.bfloat16).astype(jnp.float32)
+                left = left - piece
+                packed = packed + (pltpu.roll(piece, 2 * heads * t, 1) if t > 0 else piece)
+            part[:, size:] = packed.astype(jnp.bfloat16)
+
+    @pl.when(lax.axis_index("head") == 1)
+    def _():
+        lax.fori_loop(0, heads // per, second_chip, 0)
+
+
+def late_kernel(per, size, factor, bias, own, par, two, three, kept, crossed, out0, out1):
+    rows = own.shape[0]
+
+    def run(cache, with_first):
+        def step(h, carry):
+            for j in range(per):
+                head = (h * per + j) * HD
+                col = pl.ds(pl.multiple_of(head, HD), HD)
+
+                def pick(t):
+                    at = pl.ds(pl.multiple_of((3 + t) * size + head, HD), HD)
+                    return [own[:, at], par[:, at]]
+
+                k, v = [cache[: 2 * BLOCK, col]] + pick(1), [cache[2 * BLOCK :, col]] + pick(2)
+                if with_first:
+                    there = pl.ds(pl.multiple_of(size + head, HD), HD)
+                    k += [two[:, col], three[:, col]]
+                    v += [two[:, there], three[:, there]]
+                scores = logits(
+                    jnp.concatenate(pick(0), axis=0), jnp.concatenate(k, axis=0), factor
+                )
+                mixed, _, total = soft(biased(scores, 2 * BLOCK, bias), jnp.concatenate(v, axis=0))
+                mixed = (mixed * (1.0 / total)).astype(jnp.bfloat16)
+                out0[:, col], out1[:, col] = mixed[:rows], mixed[rows:]
+            return carry
+
+        lax.fori_loop(0, size // HD // per, step, 0)
+
+    @pl.when(lax.axis_index("head") == 0)
+    def _():
+        run(crossed, False)
+
+    @pl.when(lax.axis_index("head") == 1)
+    def _():
+        run(kept, True)
+
+
+def finish_kernel(width, start, size, count, *refs):
+    own, got, loc_own, loc_got, far_own, far_got = refs[:6]
+    result, merged_own, merged_got, sems = refs[count:]
+    heads = size // HD
+    c = lax.axis_index("sub")
+
+    def put(array, group, i):
+        to = pl.ds(pl.multiple_of(group * width + start, HD), size)
+        return pltpu.make_async_copy(array, result.at[:, to], sems.at[i])
+
+    copies = [put(own, 2 + c, 0), put(got, 3 - c, 1)]
+    for copy in copies:
+        copy.start()
+    pairs = ((loc_own, far_own, merged_own), (loc_got, far_got, merged_got))
+
+    @pl.when(lax.axis_index("head") == 0)
+    def _():
+        for loc, far, merged in pairs:
+            merged[...] = loc[:, :size].astype(jnp.bfloat16)
+
+    @pl.when(lax.axis_index("head") == 1)
+    def _():
+        for loc, far, merged in pairs:
+            packed = far[:, size:].astype(jnp.float32)
+            there = packed
+            for t in range(1, 3):
+                there = there + pltpu.roll(packed, HD - 2 * heads * t, 1)
+            here = loc[:, size:]
+            for i in range(heads):
+                col = slice(i * HD, (i + 1) * HD)
+                near_top, near_sum = here[:, 2 * i : 2 * i + 1], here[:, 2 * i + 1 : 2 * i + 2]
+                far_top, far_sum = there[:, 2 * i : 2 * i + 1], there[:, 2 * i + 1 : 2 * i + 2]
+                top = jnp.maximum(near_top, far_top)
+                near = jnp.exp2(near_top - top)
+                away = far_sum * jnp.exp2(far_top - top)
+                scale = 1.0 / (near_sum * near + away)
+                mixed = loc[:, col] * (near * scale)
+                mixed = mixed + far[:, col].astype(jnp.float32) * (away * scale)
+                merged[:, col] = mixed.astype(jnp.bfloat16)
+
+    copies += [put(merged_own, c, 2), put(merged_got, 1 - c, 3)]
+    for copy in copies[2:]:
+        copy.start()
+    for copy in copies:
+        copy.wait()
+
+
+def hybrid(n_seq, chunk_heads, queries, new_keys, new_values, key_cache, value_cache, selection):
+    n = 4
+    rows, features = queries.shape
+    width = features // n
+    heads = width // HD
+    chunks, first = [], 0
+    for count in chunk_heads(heads):
+        chunks.append((first * HD, count * HD))
+        first += count
+    factor = float(HD) ** (-0.5) * LOG2E
+    blk_dev = key_cache.shape[0] // BLOCK
+    picks = selection.T
+    anywhere = pl.BlockSpec(memory_space=pl.ANY)
+    in_hbm = pl.BlockSpec(memory_space=pltpu.HBM)
+    resident = pl.BlockSpec(memory_space=pltpu.VMEM)
+    bf16, f32 = jnp.bfloat16, jnp.float32
+
+    def call(kernel, arrays, in_specs, shapes, scratch=(), scalars=(), result=None):
+        return pl.pallas_call(
+            kernel,
+            out_shape=[pltpu.VMEM(*s) for s in shapes] if result is None else result,
+            grid_spec=pltpu.PrefetchScalarGridSpec(
+                num_scalar_prefetch=len(scalars),
+                grid=(1,),
+                in_specs=in_specs,
+                out_specs=[resident] * len(shapes) if result is None else anywhere,
+                scratch_shapes=list(scratch),
+            ),
+            input_output_aliases={6: 0} if len(arrays) == 7 and result is not None else {},
+            compiler_params=pltpu.CompilerParams(vmem_limit_bytes=VMEM_LIMIT),
+        )(*scalars, *arrays)
+
+    def move(x, pairs, axes=("head", "sub")):
+        return lax.ppermute(x, axes, list(pairs))
+
+    def apart(d, sources=range(n)):
+        return [(i, i ^ d) for i in sources]
+
+    arrays = [pltpu.with_memory_space_constraint(x, pltpu.HBM) for x in (queries, new_keys, new_values)]
+    caches = [pltpu.with_memory_space_constraint(x, pltpu.HBM) for x in (key_cache, value_cache)]
+    from_args = [in_hbm] * 3 + [anywhere]
+
+    def cross(i, after):
+        start, size = chunks[i]
+        sent = call(
+            functools.partial(cross_kernel, width, start, size), arrays + [after],
+            from_args, [((rows, 2 * size), bf16)] * 2, [pltpu.SemaphoreType.DMA((4,))],
+        )
+        return sent, [move(sent[d - 2], apart(d)) for d in (2, 3)]
+
+    def cores(i, flip, after):
+        start, size = chunks[i]
+        return call(
+            functools.partial(core_kernel, width, start, size, flip),
+            arrays + [after], from_args, [((rows, 6 * size), bf16)],
+            [pltpu.SemaphoreType.DMA((6,))],
+        )[0]
+
+    sends = call(
+        functools.partial(sends_kernel, n_seq, blk_dev, rows, chunks),
+        caches, [in_hbm] * 2,
+        [((2 * BLOCK, size), bf16) for _, size in chunks for _ in range(n_seq)]
+        + [((2 * rows, pl.cdiv(2 * rows, HD) * HD), f32)],
+        [pltpu.SemaphoreType.DMA((2 * n_seq * len(chunks),))], [picks],
+    )
+    bias = sends[-1]
+    sent, crossing = [sends[1]], []
+    for i in range(len(chunks)):
+        sent, came = cross(i, sent[0])
+        crossing.append(came)
+    own, par, after = [], [], sent[0]
+    for i in range(len(chunks)):
+        after = cores(i, 1, after)
+        par.append(move(after, apart(1)))
+    for i in range(len(chunks)):
+        after = cores(i, 0, after)
+        own.append(after)
+
+    def fetch(i):
+        block = sends[n_seq * i : n_seq * (i + 1)]
+        came = [block[0]]
+        for d in range(1, n_seq):
+            came.append(move(block[d], [(z, z ^ d) for z in range(n_seq)], "seq"))
+        kept = call(
+            functools.partial(collect_kernel, blk_dev), came, [resident] * n_seq,
+            [((4 * BLOCK, chunks[i][1]), bf16)], (), [picks],
+        )[0]
+        return kept, move(kept, apart(2, (2, 3)))
+
+    result = None
+    for i, (start, size) in enumerate(chunks):
+        kept, crossed = fetch(i)
+        per = 2 if size // HD % 2 == 0 else 1
+        given = [bias, own[i], par[i], *crossing[i], kept]
+        loc0, loc1, part0, part1 = call(
+            functools.partial(early_kernel, per, size, factor), given, [resident] * 6,
+            [((rows, size + HD), f32)] * 2 + [((rows, size + HD), bf16)] * 2,
+        )
+        far0 = move(part0, apart(2, (0, 1)))
+        far1 = move(part1, apart(3, (0, 1)))
+        got_loc = move(loc1, apart(1))
+        out0, out1 = call(
+            functools.partial(late_kernel, per, size, factor), given + [crossed],
+            [resident] * 7, [((rows, size), bf16)] * 2,
+        )
+        got = move(out1, apart(1))
+        pieces = [out0, got, loc0, got_loc, far0, far1]
+        specs = [resident] * 6
+        if result is not None:
+            pieces, specs = pieces + [result], specs + [anywhere]
+        result = call(
+            functools.partial(finish_kernel, width, start, size, len(pieces)),
+            pieces, specs, [],
+            [pltpu.VMEM((rows, size), bf16)] * 2 + [pltpu.SemaphoreType.DMA((4,))],
+            (), jax.ShapeDtypeStruct((rows, features), bf16),
+        )
+    return result
+
+
+def uneven(heads):
+    second = max(2, heads * 3 // 8 // 2 * 2)
+    return (heads - second, second)
+
+
+def placed_map(body, mesh, placed):
+    return jax.shard_map(
+        body,
+        mesh=mesh,
+        in_specs=placed,
+        out_specs=P(("groups", "seq", "head", "sub"), None),
+        check_vma=False,
+    )
+
+
 def solution(mesh):
     subs = mesh.shape["sub"]
     n = mesh.shape["head"] * subs
@@ -146,10 +544,14 @@
         P(("groups", "seq"), ("head", "sub")),
         P("groups", None),
     )
-    return jax.shard_map(
-        functools.partial(ulysses, n, subs),
-        mesh=mesh,
-        in_specs=placed,
-        out_specs=P(("groups", "seq", "head", "sub"), None),
-        check_vma=False,
-    )
+    n_seq = mesh.shape["seq"]
+    body = functools.partial(ulysses, n, subs)
+    if (mesh.shape["head"], subs, n_seq) == (2, 2, 4):
+        body = functools.partial(hybrid, n_seq, uneven)
+    if (mesh.shape["head"], subs, n_seq) != (2, 2, 4):
+        return placed_map(body, mesh, placed)
+
+    def step(*args):
+        return body(*args)
+
+    return placed_map(step, mesh, placed)

time: 133 us -> 128 us (0.962)
  Pallas kernels: 15.5 us -> 29.7 us
  local copies, waits for them, and re-layouts: 11.4 us -> 0.68 us
  waiting for transfers between devices: 79.7 us -> 71.4 us
  starting transfers between devices: 22.8 us -> 25.1 us
    all_to_all x2 -> x0, waiting for transfers between devices: 24.1 us -> none  [ulysses(): lax.all_to_all(cache.reshape(blk_dev, BLOCK, -1)[inner], 'seq', split_axi...]
    ppermute x12 -> x22, waiting for transfers between devices: 55.6 us -> 71.4 us  [move(): return lax.ppermute(x, axes, list(pairs))]
    pallas_call x1 -> x15, Pallas kernels: 15.5 us -> 29.7 us  [call(): pl.pallas_call(kernel, out_shape=[pltpu.VMEM(*s) for s in shapes] if resu...]
    ppermute x12 -> x22, starting transfers between devices: 12.8 us -> 25.1 us  [move(): return lax.ppermute(x, axes, list(pairs))]
    all_to_all x2 -> x0, starting transfers between devices: 10 us -> none  [ulysses(): lax.all_to_all(cache.reshape(blk_dev, BLOCK, -1)[inner], 'seq', split_axi...]
    dynamic_slice x5 -> x0, local copies, waits for them, and re-layouts: 3.85 us -> none  [the longest x3 3.51 us: spread(): piece = lax.dynamic_slice_in_dim(array, peer(b) * width, width, axis=1)]
    gather x2 -> x0, local copies, waits for them, and re-layouts: 3.21 us -> none  [ulysses(): cache.reshape(blk_dev, BLOCK, -1)[inner]]
    unnamed x24 -> x4, local copies, waits for them, and re-layouts: 2.73 us -> 0.68 us
  transfers between devices with their start and end apart: 14 -> 22, of which waited for: 13 -> 9; matrix products, arithmetic and copies ran while one was open for 5% -> 0% of each run, Pallas kernels for 0% -> 18%
where the time goes in v3:
time: 128 us; the launch traced here: 127 us
  waiting for transfers between devices  71.4 us (56%)
  Pallas kernels  29.7 us (23%)
  starting transfers between devices  25.1 us (20%)
    ppermute x22, waiting for transfers between devices, move(): return lax.ppermute(x, axes, list(pairs))  71.4 us
    pallas_call x15, Pallas kernels, call(): pl.pallas_call(kernel, out_shape=[pltpu.VMEM(*s) for s in shapes] if resu...  29.7 us
    ppermute x22, starting transfers between devices, move(): return lax.ppermute(x, axes, list(pairs))  25.1 us
  transfers between devices with their start and end apart: 22, of which 9 were waited for; matrix products, arithmetic and copies ran while one was open for 0% of the time, Pallas kernels for 18%

profile of v3, /device:TPU:0, one launch (start us, length us, event | category | flops | bytes accessed | tf_op | source)
XLA Modules:
  0.0 127.2 jit_solution(17127253653155914143)
XLA Ops:
  0.0 0.0 copy-start
  0.0 0.7 copy-done
  0.7 2.4 %shard_map.64 = (bf16[128,1280]{1,0:T(8,128)(2,1)S(1)}, bf16[128,1280]{1,0:T(8,128)(2,1)S(1)}, bf16[128,1280]{1,0:T(8,128)(2,1)S(1)}, bf16[128,1280]{1,0:T(8,128...) custom-call(s32[2,4]{1,0:T(2,128)S(1)} %bitcast.1, ...), custom_call_target="tpu_custom_call" | custom-call | tf_op jit(solution)/shard_map/pallas_call | solution.py:420
  3.1 1.4 %shard_map.65 = (bf16[96,2560]{1,0:T(8,128)(2,1)S(1)}, bf16[96,2560]{1,0:T(8,128)(2,1)S(1)}) custom-call(bf16[96,8192]{1,0:T(8,128)(2,1)} %q.11, bf16[96,8192]{1,0:T(8,128)(2,1)} %k.11, bf16[96,8192]{1,0:T(8,128)(2,1)} %v.11, bf16[128,1280]{1,0:T(8,128)(2,1)S(1)} %get-tuple-element.31.after), custom_call_target="tpu_custom_call" | custom-call | tf_op jit(solution)/shard_map/pallas_call | solution.py:420
  4.5 1.2 shard_map.66
  5.6 1.5 %shard_map.67.after = bf16[96,7680]{1,0:T(8,128)(2,1)S(1)} custom-call(bf16[96,8192]{1,0:T(8,128)(2,1)} %q.11, bf16[96,8192]{1,0:T(8,128)(2,1)} %k.11, bf16[96,8192]{1,0:T(8,128)(2,1)} %v.11, bf16[96,1536]{1,0:T(8,128)(2,1)S(1)} %get-tuple-element.33.after), custom_call_target="tpu_custom_call" | custom-call | tf_op jit(solution)/shard_map/pallas_call | solution.py:420
  7.2 0.6 collective-permute-start.11
  7.7 2.6 %collective-permute-start.3 = (bf16[128,768]{1,0:T(8,128)(2,1)S(1)}, bf16[128,768]{1,0:T(8,128)(2,1)S(1)}, u32[]{:S(2)}, u32[]{:S(2)}) collective-permute-start(bf16[128,768]{1,0:T(8,128)(2,1)S(1)} %get-tuple-element.36), channel_id=1, source_target_pairs={{0,4},{4,0},{8,12},{12,8},{1,5},{5,1},{9,13},{13,9},{2,6},{6,2},{1... | collective-permute-start | bytes 589832 | tf_op jit(solution)/shard_map/ppermute | solution.py:435
  10.4 2.7 %collective-permute-start.15 = (bf16[128,1280]{1,0:T(8,128)(2,1)S(1)}, bf16[128,1280]{1,0:T(8,128)(2,1)S(1)}, u32[]{:S(2)}, u32[]{:S(2)}) collective-permute-start(bf16[128,1280]{1,0:T(8,128)(2,1)S(1)} %get-tuple-element.47), channel_id=1, source_target_pairs={{0,8},{4,12},{8,0},{12,4},{1,9},{5,13},{9,1},{13,5},{2,10},{6,14},... | collective-permute-start | bytes 983048 | tf_op jit(solution)/shard_map/ppermute | solution.py:435
  13.1 0.0 collective-permute-start.16
  13.1 0.7 collective-permute-start.14
  13.9 6.3 %collective-permute-done.3.refs_1_ = bf16[128,768]{1,0:T(8,128)(2,1)S(1)} collective-permute-done((bf16[128,768]{1,0:T(8,128)(2,1)S(1)}, bf16[128,768]{1,0:T(8,128)(2,1)S(1)}, u32[]{:S(2)}, u32[]{:S(2)}) %collective-permute-start.3) | collective-permute-done | bytes 196640 | tf_op jit(solution)/shard_map/ppermute | solution.py:435
  20.1 1.3 %collective-permute-start.4 = (bf16[128,768]{1,0:T(8,128)(2,1)S(1)}, bf16[128,768]{1,0:T(8,128)(2,1)S(1)}, u32[]{:S(2)}, u32[]{:S(2)}) collective-permute-start(bf16[128,768]{1,0:T(8,128)(2,1)S(1)} %get-tuple-element.37), channel_id=1, source_target_pairs={{0,8},{4,12},{8,0},{12,4},{1,9},{5,13},{9,1},{13,5},{2,10},{6,14},... | collective-permute-start | bytes 589832 | tf_op jit(solution)/shard_map/ppermute | solution.py:435
  21.4 29.3 %collective-permute-done.4.refs_2_ = bf16[128,768]{1,0:T(8,128)(2,1)S(1)} collective-permute-done((bf16[128,768]{1,0:T(8,128)(2,1)S(1)}, bf16[128,768]{1,0:T(8,128)(2,1)S(1)}, u32[]{:S(2)}, u32[]{:S(2)}) %collective-permute-start.4) | collective-permute-done | bytes 196640 | tf_op jit(solution)/shard_map/ppermute | solution.py:435
  50.7 0.5 collective-permute-start.13
  51.2 1.3 %shard_map.68.after = bf16[96,4608]{1,0:T(8,128)(2,1)S(1)} custom-call(bf16[96,8192]{1,0:T(8,128)(2,1)} %q.11, bf16[96,8192]{1,0:T(8,128)(2,1)} %k.11, bf16[96,8192]{1,0:T(8,128)(2,1)} %v.11, bf16[96,7680]{1,0:T(8,128)(2,1)S(1)} %shard_map.67.after), custom_call_target="tpu_custom_call" | custom-call | tf_op jit(solution)/shard_map/pallas_call | solution.py:420
  52.5 0.0 copy-start.1
  52.5 0.0 collective-permute-done.15.refs_2_
  52.5 1.2 collective-permute-start
  53.7 0.0 collective-permute-done.16.refs_3_
  53.7 2.4 %collective-permute-start.5 = (bf16[128,768]{1,0:T(8,128)(2,1)S(1)}, bf16[128,768]{1,0:T(8,128)(2,1)S(1)}, u32[]{:S(2)}, u32[]{:S(2)}) collective-permute-start(bf16[128,768]{1,0:T(8,128)(2,1)S(1)} %get-tuple-element.38), channel_id=1, source_target_pairs={{0,12},{4,8},{8,4},{12,0},{1,13},{5,9},{9,5},{13,1},{2,14},{6,10},... | collective-permute-start | bytes 589832 | tf_op jit(solution)/shard_map/ppermute | solution.py:435
  56.1 0.0 collective-permute-done.14.refs_1_
  56.1 0.5 collective-permute-start.12
  56.6 0.6 shard_map.74.kept
  57.3 5.3 %collective-permute-done.5.refs_3_ = bf16[128,768]{1,0:T(8,128)(2,1)S(1)} collective-permute-done((bf16[128,768]{1,0:T(8,128)(2,1)S(1)}, bf16[128,768]{1,0:T(8,128)(2,1)S(1)}, u32[]{:S(2)}, u32[]{:S(2)}) %collective-permute-start.5) | collective-permute-done | bytes 196640 | tf_op jit(solution)/shard_map/ppermute | solution.py:435
  62.5 1.3 %collective-permute-start.17 = (bf16[256,1280]{1,0:T(8,128)(2,1)S(1)}, bf16[256,1280]{1,0:T(8,128)(2,1)S(1)}, u32[]{:S(2)}, u32[]{:S(2)}) collective-permute-start(bf16[256,1280]{1,0:T(8,128)(2,1)S(1)} %shard_map.74.kept), channel_id=1, source_target_pairs={{2,0},{3,1},{6,4},{7,5},{10,8},{11,9},{14,12},{15,13},{18,16},{19,... | collective-permute-start | bytes 1966088 | tf_op jit(solution)/shard_map/ppermute | solution.py:435
  63.8 0.4 collective-permute-done.13.three
  64.2 0.9 collective-permute-start.2
  65.1 0.0 copy-done.1
  65.1 0.6 shard_map.71.kept
  65.7 9.1 %collective-permute-done.12.two = bf16[96,2560]{1,0:T(8,128)(2,1)S(1)} collective-permute-done((bf16[96,2560]{1,0:T(8,128)(2,1)S(1)}, bf16[96,2560]{1,0:T(8,128)(2,1)S(1)}, u32[]{:S(2)}, u32[]{:S(2)}) %collective-permute-start.12) | collective-permute-done | bytes 491552 | tf_op jit(solution)/shard_map/ppermute | solution.py:435
  74.8 1.3 %collective-permute-start.6 = (bf16[256,768]{1,0:T(8,128)(2,1)S(1)}, bf16[256,768]{1,0:T(8,128)(2,1)S(1)}, u32[]{:S(2)}, u32[]{:S(2)}) collective-permute-start(bf16[256,768]{1,0:T(8,128)(2,1)S(1)} %shard_map.71.kept), channel_id=1, source_target_pairs={{2,0},{3,1},{6,4},{7,5},{10,8},{11,9},{14,12},{15,13},{18,16},{19,... | collective-permute-start | bytes 1179656 | tf_op jit(solution)/shard_map/ppermute | solution.py:435
  76.1 0.0 collective-permute-done.11.par
  76.1 2.7 %collective-permute-start.1 = (bf16[96,1536]{1,0:T(8,128)(2,1)S(1)}, bf16[96,1536]{1,0:T(8,128)(2,1)S(1)}, u32[]{:S(2)}, u32[]{:S(2)}) collective-permute-start(bf16[96,1536]{1,0:T(8,128)(2,1)S(1)} %get-tuple-element.33.after), channel_id=1, source_target_pairs={{0,2},{1,3},{2,0},{3,1},{4,6},{5,7},{6,4},{7,5},{8,10},{9,11},{10,... | collective-permute-start | bytes 884744 | tf_op jit(solution)/shard_map/ppermute | solution.py:435
  78.9 1.5 %shard_map.69.after.own = bf16[96,7680]{1,0:T(8,128)(2,1)S(1)} custom-call(bf16[96,8192]{1,0:T(8,128)(2,1)} %q.11, bf16[96,8192]{1,0:T(8,128)(2,1)} %k.11, bf16[96,8192]{1,0:T(8,128)(2,1)} %v.11, bf16[96,4608]{1,0:T(8,128)(2,1)S(1)} %shard_map.68.after), custom_call_target="tpu_custom_call" | custom-call | tf_op jit(solution)/shard_map/pallas_call | solution.py:420
  80.4 6.4 %shard_map.76 = (f32[96,1408]{1,0:T(8,128)S(1)}, f32[96,1408]{1,0:T(8,128)S(1)}, bf16[96,1408]{1,0:T(8,128)(2,1)S(1)}, bf16[96,1408]{1,0:T(8,128)(2,1)S(1)}) custom-call(f32[192,256]{1,0:T(8,128)S(1)} %get-tuple-element.30.bias, bf16[96,7680]{1,0:T(8,128)(2,1)S(1)} %shard_map.69.after.own, bf16[96,7680]{1,0:T(8,128)(2,1)S(1)} %collective-permute-done.11.par, ...), custom_call_target="tpu_custom_call" | custom-call | tf_op jit(solution)/shard_map/pallas_call | solution.py:420
  86.8 8.3 %collective-permute-done.2.three = bf16[96,1536]{1,0:T(8,128)(2,1)S(1)} collective-permute-done((bf16[96,1536]{1,0:T(8,128)(2,1)S(1)}, bf16[96,1536]{1,0:T(8,128)(2,1)S(1)}, u32[]{:S(2)}, u32[]{:S(2)}) %collective-permute-start.2) | collective-permute-done | bytes 294944 | tf_op jit(solution)/shard_map/ppermute | solution.py:435
  95.1 0.1 collective-permute-start.19
  95.2 0.0 collective-permute-done.17.crossed
  95.2 1.5 %collective-permute-start.20 = (bf16[96,1408]{1,0:T(8,128)(2,1)S(1)}, bf16[96,1408]{1,0:T(8,128)(2,1)S(1)}, u32[]{:S(2)}, u32[]{:S(2)}) collective-permute-start(bf16[96,1408]{1,0:T(8,128)(2,1)S(1)} %get-tuple-element.53), channel_id=1, source_target_pairs={{0,2},{1,3},{4,6},{5,7},{8,10},{9,11},{12,14},{13,15},{16,18},{17,... | collective-permute-start | bytes 811016 | tf_op jit(solution)/shard_map/ppermute | solution.py:435
  96.7 3.6 %shard_map.75 = (bf16[96,1280]{1,0:T(8,128)(2,1)S(1)}, bf16[96,1280]{1,0:T(8,128)(2,1)S(1)}) custom-call(f32[192,256]{1,0:T(8,128)S(1)} %get-tuple-element.30.bias, bf16[96,7680]{1,0:T(8,128)(2,1)S(1)} %shard_map.69.after.own, bf16[96,7680]{1,0:T(8,128)(2,1)S(1)} %collective-permute-done.11.par, bf16[96,2560]{1,0:T(8,128)(2,1)S(1)} %collective-permute-done.12.two, ...), custom_call_target="tpu_custom_call" | custom-call | tf_op jit(solution)/shard_map/pallas_call | solution.py:420
  100.3 9.6 %collective-permute-done.1.two = bf16[96,1536]{1,0:T(8,128)(2,1)S(1)} collective-permute-done((bf16[96,1536]{1,0:T(8,128)(2,1)S(1)}, bf16[96,1536]{1,0:T(8,128)(2,1)S(1)}, u32[]{:S(2)}, u32[]{:S(2)}) %collective-permute-start.1) | collective-permute-done | bytes 294944 | tf_op jit(solution)/shard_map/ppermute | solution.py:435
  109.9 0.1 collective-permute-start.18
  109.9 0.0 collective-permute-done.par
  109.9 1.5 %collective-permute-start.21 = (bf16[96,1408]{1,0:T(8,128)(2,1)S(1)}, bf16[96,1408]{1,0:T(8,128)(2,1)S(1)}, u32[]{:S(2)}, u32[]{:S(2)}) collective-permute-start(bf16[96,1408]{1,0:T(8,128)(2,1)S(1)} %get-tuple-element.54), channel_id=1, source_target_pairs={{0,3},{1,2},{4,7},{5,6},{8,11},{9,10},{12,15},{13,14},{16,19},{17,... | collective-permute-start | bytes 811016 | tf_op jit(solution)/shard_map/ppermute | solution.py:435
  111.5 1.3 %shard_map.70.own = bf16[96,4608]{1,0:T(8,128)(2,1)S(1)} custom-call(bf16[96,8192]{1,0:T(8,128)(2,1)} %q.11, bf16[96,8192]{1,0:T(8,128)(2,1)} %k.11, bf16[96,8192]{1,0:T(8,128)(2,1)} %v.11, bf16[96,7680]{1,0:T(8,128)(2,1)S(1)} %shard_map.69.after.own), custom_call_target="tpu_custom_call" | custom-call | tf_op jit(solution)/shard_map/pallas_call | solution.py:420
  112.8 3.9 %shard_map.73 = (f32[96,896]{1,0:T(8,128)S(1)}, f32[96,896]{1,0:T(8,128)S(1)}, bf16[96,896]{1,0:T(8,128)(2,1)S(1)}, bf16[96,896]{1,0:T(8,128)(2,1)S(1)}) custom-call(f32[192,256]{1,0:T(8,128)S(1)} %get-tuple-element.30.bias, bf16[96,4608]{1,0:T(8,128)(2,1)S(1)} %shard_map.70.own, bf16[96,4608]{1,0:T(8,128)(2,1)S(1)} %collective-permute-done.par, ...), custom_call_target="tpu_custom_call" | custom-call | tf_op jit(solution)/shard_map/pallas_call | solution.py:420
  116.7 0.0 collective-permute-done.6.crossed
  116.7 0.3 collective-permute-start.8
  117.0 0.0 collective-permute-done.18.refs_1_
  117.0 1.3 %collective-permute-start.9 = (bf16[96,896]{1,0:T(8,128)(2,1)S(1)}, bf16[96,896]{1,0:T(8,128)(2,1)S(1)}, u32[]{:S(2)}, u32[]{:S(2)}) collective-permute-start(bf16[96,896]{1,0:T(8,128)(2,1)S(1)} %get-tuple-element.43), channel_id=1, source_target_pairs={{0,2},{1,3},{4,6},{5,7},{8,10},{9,11},{12,14},{13,15},{16,18},{17,... | collective-permute-start | bytes 516104 | tf_op jit(solution)/shard_map/ppermute | solution.py:435
  118.3 0.0 collective-permute-done.20.refs_4_
  118.3 1.3 %collective-permute-start.10 = (bf16[96,896]{1,0:T(8,128)(2,1)S(1)}, bf16[96,896]{1,0:T(8,128)(2,1)S(1)}, u32[]{:S(2)}, u32[]{:S(2)}) collective-permute-start(bf16[96,896]{1,0:T(8,128)(2,1)S(1)} %get-tuple-element.44), channel_id=1, source_target_pairs={{0,3},{1,2},{4,7},{5,6},{8,11},{9,10},{12,15},{13,14},{16,19},{17,... | collective-permute-start | bytes 516104 | tf_op jit(solution)/shard_map/ppermute | solution.py:435
  119.6 2.2 %shard_map.72 = (bf16[96,768]{1,0:T(8,128)(2,1)S(1)}, bf16[96,768]{1,0:T(8,128)(2,1)S(1)}) custom-call(f32[192,256]{1,0:T(8,128)S(1)} %get-tuple-element.30.bias, bf16[96,4608]{1,0:T(8,128)(2,1)S(1)} %shard_map.70.own, bf16[96,4608]{1,0:T(8,128)(2,1)S(1)} %collective-permute-done.par, bf16[96,1536]{1,0:T(8,128)(2,1)S(1)} %collective-permute-done.1.two, ...), custom_call_target="tpu_custom_call" | custom-call | tf_op jit(solution)/shard_map/pallas_call | solution.py:420
  121.8 0.0 collective-permute-done.21.refs_5_
  121.8 0.4 collective-permute-start.7
  122.2 0.0 collective-permute-done.19.refs_3_
  122.2 1.0 shard_map.77.refs_6_
  123.2 0.1 collective-permute-done.7.refs_1_
  123.2 0.0 collective-permute-done.9.refs_4_
  123.2 3.1 %collective-permute-done.10.refs_5_ = bf16[96,896]{1,0:T(8,128)(2,1)S(1)} collective-permute-done((bf16[96,896]{1,0:T(8,128)(2,1)S(1)}, bf16[96,896]{1,0:T(8,128)(2,1)S(1)}, u32[]{:S(2)}, u32[]{:S(2)}) %collective-permute-start.10) | collective-permute-done | bytes 172064 | tf_op jit(solution)/shard_map/ppermute | solution.py:435
  126.3 0.0 collective-permute-done.8.refs_3_
  126.3 0.8 shard_map.78
Async XLA Ops:
  0.0 0.7 copy-start
  7.2 68.9 %collective-permute-start.11 = (bf16[96,7680]{1,0:T(8,128)(2,1)S(1)}, bf16[96,7680]{1,0:T(8,128)(2,1)S(1)}, u32[]{:S(2)}, u32[]{:S(2)}) collective-permute-start(bf16[96,7680]{1,0:T(8,128)(2,1)S(1)} %shard_map.67.after), channel_id=1, source_target_pairs={{0,1},{1,0},{2,3},{3,2},{4,5},{5,4},{6,7},{7,6},{8,9},{9,8},{10,11... | collective-permute-start | bytes 4423688 | tf_op jit(solution)/shard_map/ppermute | solution.py:435
  7.7 12.4 %collective-permute-start.3 = (bf16[128,768]{1,0:T(8,128)(2,1)S(1)}, bf16[128,768]{1,0:T(8,128)(2,1)S(1)}, u32[]{:S(2)}, u32[]{:S(2)}) collective-permute-start(bf16[128,768]{1,0:T(8,128)(2,1)S(1)} %get-tuple-element.36), channel_id=1, source_target_pairs={{0,4},{4,0},{8,12},{12,8},{1,5},{5,1},{9,13},{13,9},{2,6},{6,2},{1... | collective-permute-start | bytes 589832 | tf_op jit(solution)/shard_map/ppermute | solution.py:435
  10.4 42.2 %collective-permute-start.15 = (bf16[128,1280]{1,0:T(8,128)(2,1)S(1)}, bf16[128,1280]{1,0:T(8,128)(2,1)S(1)}, u32[]{:S(2)}, u32[]{:S(2)}) collective-permute-start(bf16[128,1280]{1,0:T(8,128)(2,1)S(1)} %get-tuple-element.47), channel_id=1, source_target_pairs={{0,8},{4,12},{8,0},{12,4},{1,9},{5,13},{9,1},{13,5},{2,10},{6,14},... | collective-permute-start | bytes 983048 | tf_op jit(solution)/shard_map/ppermute | solution.py:435
  13.1 40.6 %collective-permute-start.16 = (bf16[128,1280]{1,0:T(8,128)(2,1)S(1)}, bf16[128,1280]{1,0:T(8,128)(2,1)S(1)}, u32[]{:S(2)}, u32[]{:S(2)}) collective-permute-start(bf16[128,1280]{1,0:T(8,128)(2,1)S(1)} %get-tuple-element.48), channel_id=1, source_target_pairs={{0,12},{4,8},{8,4},{12,0},{1,13},{5,9},{9,5},{13,1},{2,14},{6,10},... | collective-permute-start | bytes 983048 | tf_op jit(solution)/shard_map/ppermute | solution.py:435
  13.1 43.0 %collective-permute-start.14 = (bf16[128,1280]{1,0:T(8,128)(2,1)S(1)}, bf16[128,1280]{1,0:T(8,128)(2,1)S(1)}, u32[]{:S(2)}, u32[]{:S(2)}) collective-permute-start(bf16[128,1280]{1,0:T(8,128)(2,1)S(1)} %get-tuple-element.31.after), channel_id=1, source_target_pairs={{0,4},{4,0},{8,12},{12,8},{1,5},{5,1},{9,13},{13,9},{2,6},{6,2},{1... | collective-permute-start | bytes 983048 | tf_op jit(solution)/shard_map/ppermute | solution.py:435
  20.1 30.6 %collective-permute-start.4 = (bf16[128,768]{1,0:T(8,128)(2,1)S(1)}, bf16[128,768]{1,0:T(8,128)(2,1)S(1)}, u32[]{:S(2)}, u32[]{:S(2)}) collective-permute-start(bf16[128,768]{1,0:T(8,128)(2,1)S(1)} %get-tuple-element.37), channel_id=1, source_target_pairs={{0,8},{4,12},{8,0},{12,4},{1,9},{5,13},{9,1},{13,5},{2,10},{6,14},... | collective-permute-start | bytes 589832 | tf_op jit(solution)/shard_map/ppermute | solution.py:435
  50.7 13.5 %collective-permute-start.13 = (bf16[96,2560]{1,0:T(8,128)(2,1)S(1)}, bf16[96,2560]{1,0:T(8,128)(2,1)S(1)}, u32[]{:S(2)}, u32[]{:S(2)}) collective-permute-start(bf16[96,2560]{1,0:T(8,128)(2,1)S(1)} %get-tuple-element.45), channel_id=1, source_target_pairs={{0,3},{1,2},{2,1},{3,0},{4,7},{5,6},{6,5},{7,4},{8,11},{9,10},{10,... | collective-permute-start | bytes 1474568 | tf_op jit(solution)/shard_map/ppermute | solution.py:435
  52.5 12.6 %copy-start.1 = (s32[4,2]{0,1:T(2,128)S(1)}, s32[4,2]{0,1:T(2,128)}, u32[]{:S(2)}) copy-start(s32[4,2]{0,1:T(2,128)} %param.11) | copy-start | bytes 100
  52.5 57.4 %collective-permute-start = (bf16[96,4608]{1,0:T(8,128)(2,1)S(1)}, bf16[96,4608]{1,0:T(8,128)(2,1)S(1)}, u32[]{:S(2)}, u32[]{:S(2)}) collective-permute-start(bf16[96,4608]{1,0:T(8,128)(2,1)S(1)} %shard_map.68.after), channel_id=1, source_target_pairs={{0,1},{1,0},{2,3},{3,2},{4,5},{5,4},{6,7},{7,6},{8,9},{9,8},{10,11... | collective-permute-start | bytes 2654216 | tf_op jit(solution)/shard_map/ppermute | solution.py:435
  53.7 8.8 %collective-permute-start.5 = (bf16[128,768]{1,0:T(8,128)(2,1)S(1)}, bf16[128,768]{1,0:T(8,128)(2,1)S(1)}, u32[]{:S(2)}, u32[]{:S(2)}) collective-permute-start(bf16[128,768]{1,0:T(8,128)(2,1)S(1)} %get-tuple-element.38), channel_id=1, source_target_pairs={{0,12},{4,8},{8,4},{12,0},{1,13},{5,9},{9,5},{13,1},{2,14},{6,10},... | collective-permute-start | bytes 589832 | tf_op jit(solution)/shard_map/ppermute | solution.py:435
  56.1 18.7 %collective-permute-start.12 = (bf16[96,2560]{1,0:T(8,128)(2,1)S(1)}, bf16[96,2560]{1,0:T(8,128)(2,1)S(1)}, u32[]{:S(2)}, u32[]{:S(2)}) collective-permute-start(bf16[96,2560]{1,0:T(8,128)(2,1)S(1)} %get-tuple-element.32.after), channel_id=1, source_target_pairs={{0,2},{1,3},{2,0},{3,1},{4,6},{5,7},{6,4},{7,5},{8,10},{9,11},{10,... | collective-permute-start | bytes 1474568 | tf_op jit(solution)/shard_map/ppermute | solution.py:435
  62.5 32.7 %collective-permute-start.17 = (bf16[256,1280]{1,0:T(8,128)(2,1)S(1)}, bf16[256,1280]{1,0:T(8,128)(2,1)S(1)}, u32[]{:S(2)}, u32[]{:S(2)}) collective-permute-start(bf16[256,1280]{1,0:T(8,128)(2,1)S(1)} %shard_map.74.kept), channel_id=1, source_target_pairs={{2,0},{3,1},{6,4},{7,5},{10,8},{11,9},{14,12},{15,13},{18,16},{19,... | collective-permute-start | bytes 1966088 | tf_op jit(solution)/shard_map/ppermute | solution.py:435
  64.2 30.9 %collective-permute-start.2 = (bf16[96,1536]{1,0:T(8,128)(2,1)S(1)}, bf16[96,1536]{1,0:T(8,128)(2,1)S(1)}, u32[]{:S(2)}, u32[]{:S(2)}) collective-permute-start(bf16[96,1536]{1,0:T(8,128)(2,1)S(1)} %get-tuple-element.34), channel_id=1, source_target_pairs={{0,3},{1,2},{2,1},{3,0},{4,7},{5,6},{6,5},{7,4},{8,11},{9,10},{10,... | collective-permute-start | bytes 884744 | tf_op jit(solution)/shard_map/ppermute | solution.py:435
  74.8 41.9 %collective-permute-start.6 = (bf16[256,768]{1,0:T(8,128)(2,1)S(1)}, bf16[256,768]{1,0:T(8,128)(2,1)S(1)}, u32[]{:S(2)}, u32[]{:S(2)}) collective-permute-start(bf16[256,768]{1,0:T(8,128)(2,1)S(1)} %shard_map.71.kept), channel_id=1, source_target_pairs={{2,0},{3,1},{6,4},{7,5},{10,8},{11,9},{14,12},{15,13},{18,16},{19,... | collective-permute-start | bytes 1179656 | tf_op jit(solution)/shard_map/ppermute | solution.py:435
  76.1 33.8 %collective-permute-start.1 = (bf16[96,1536]{1,0:T(8,128)(2,1)S(1)}, bf16[96,1536]{1,0:T(8,128)(2,1)S(1)}, u32[]{:S(2)}, u32[]{:S(2)}) collective-permute-start(bf16[96,1536]{1,0:T(8,128)(2,1)S(1)} %get-tuple-element.33.after), channel_id=1, source_target_pairs={{0,2},{1,3},{2,0},{3,1},{4,6},{5,7},{6,4},{7,5},{8,10},{9,11},{10,... | collective-permute-start | bytes 884744 | tf_op jit(solution)/shard_map/ppermute | solution.py:435
  95.1 27.1 %collective-permute-start.19 = (f32[96,1408]{1,0:T(8,128)S(1)}, f32[96,1408]{1,0:T(8,128)S(1)}, u32[]{:S(2)}, u32[]{:S(2)}) collective-permute-start(f32[96,1408]{1,0:T(8,128)S(1)} %get-tuple-element.52), channel_id=1, source_target_pairs={{0,1},{1,0},{2,3},{3,2},{4,5},{5,4},{6,7},{7,6},{8,9},{9,8},{10,11... | collective-permute-start | bytes 1622024 | tf_op jit(solution)/shard_map/ppermute | solution.py:435
  95.2 23.1 %collective-permute-start.20 = (bf16[96,1408]{1,0:T(8,128)(2,1)S(1)}, bf16[96,1408]{1,0:T(8,128)(2,1)S(1)}, u32[]{:S(2)}, u32[]{:S(2)}) collective-permute-start(bf16[96,1408]{1,0:T(8,128)(2,1)S(1)} %get-tuple-element.53), channel_id=1, source_target_pairs={{0,2},{1,3},{4,6},{5,7},{8,10},{9,11},{12,14},{13,15},{16,18},{17,... | collective-permute-start | bytes 811016 | tf_op jit(solution)/shard_map/ppermute | solution.py:435
  109.9 7.1 %collective-permute-start.18 = (bf16[96,1280]{1,0:T(8,128)(2,1)S(1)}, bf16[96,1280]{1,0:T(8,128)(2,1)S(1)}, u32[]{:S(2)}, u32[]{:S(2)}) collective-permute-start(bf16[96,1280]{1,0:T(8,128)(2,1)S(1)} %get-tuple-element.50), channel_id=1, source_target_pairs={{0,1},{1,0},{2,3},{3,2},{4,5},{5,4},{6,7},{7,6},{8,9},{9,8},{10,11... | collective-permute-start | bytes 737288 | tf_op jit(solution)/shard_map/ppermute | solution.py:435
  109.9 11.8 %collective-permute-start.21 = (bf16[96,1408]{1,0:T(8,128)(2,1)S(1)}, bf16[96,1408]{1,0:T(8,128)(2,1)S(1)}, u32[]{:S(2)}, u32[]{:S(2)}) collective-permute-start(bf16[96,1408]{1,0:T(8,128)(2,1)S(1)} %get-tuple-element.54), channel_id=1, source_target_pairs={{0,3},{1,2},{4,7},{5,6},{8,11},{9,10},{12,15},{13,14},{16,19},{17,... | collective-permute-start | bytes 811016 | tf_op jit(solution)/shard_map/ppermute | solution.py:435
  116.7 9.6 %collective-permute-start.8 = (f32[96,896]{1,0:T(8,128)S(1)}, f32[96,896]{1,0:T(8,128)S(1)}, u32[]{:S(2)}, u32[]{:S(2)}) collective-permute-start(f32[96,896]{1,0:T(8,128)S(1)} %get-tuple-element.42), channel_id=1, source_target_pairs={{0,1},{1,0},{2,3},{3,2},{4,5},{5,4},{6,7},{7,6},{8,9},{9,8},{10,11... | collective-permute-start | bytes 1032200 | tf_op jit(solution)/shard_map/ppermute | solution.py:435
  117.0 6.2 %collective-permute-start.9 = (bf16[96,896]{1,0:T(8,128)(2,1)S(1)}, bf16[96,896]{1,0:T(8,128)(2,1)S(1)}, u32[]{:S(2)}, u32[]{:S(2)}) collective-permute-start(bf16[96,896]{1,0:T(8,128)(2,1)S(1)} %get-tuple-element.43), channel_id=1, source_target_pairs={{0,2},{1,3},{4,6},{5,7},{8,10},{9,11},{12,14},{13,15},{16,18},{17,... | collective-permute-start | bytes 516104 | tf_op jit(solution)/shard_map/ppermute | solution.py:435
  118.3 8.0 %collective-permute-start.10 = (bf16[96,896]{1,0:T(8,128)(2,1)S(1)}, bf16[96,896]{1,0:T(8,128)(2,1)S(1)}, u32[]{:S(2)}, u32[]{:S(2)}) collective-permute-start(bf16[96,896]{1,0:T(8,128)(2,1)S(1)} %get-tuple-element.44), channel_id=1, source_target_pairs={{0,3},{1,2},{4,7},{5,6},{8,11},{9,10},{12,15},{13,14},{16,19},{17,... | collective-permute-start | bytes 516104 | tf_op jit(solution)/shard_map/ppermute | solution.py:435
  121.8 1.4 %collective-permute-start.7 = (bf16[96,768]{1,0:T(8,128)(2,1)S(1)}, bf16[96,768]{1,0:T(8,128)(2,1)S(1)}, u32[]{:S(2)}, u32[]{:S(2)}) collective-permute-start(bf16[96,768]{1,0:T(8,128)(2,1)S(1)} %get-tuple-element.40), channel_id=1, source_target_pairs={{0,1},{1,0},{2,3},{3,2},{4,5},{5,4},{6,7},{7,6},{8,9},{9,8},{10,11... | collective-permute-start | bytes 442376 | tf_op jit(solution)/shard_map/ppermute | solution.py:435

commit v4 on v3

--- a/solution.py
+++ b/solution.py
@@ -185,10 +185,12 @@
         copy.wait()
 
 
-def cross_kernel(width, start, size, q, k, v, after, two, three, sems):
-    def pairs(arrays):
+def cross_kernel(width, start, size, q, k, v, after, *refs):
+    outs, sems = refs[:-1], refs[-1]
+
+    def pairs(arrays, outs):
         result = []
-        for out, d in ((two, 2), (three, 3)):
+        for out, d in zip(outs, (2, 3)):
             at = (group_index() ^ d) * width + start
             cols = pl.ds(pl.multiple_of(at, HD), size)
             for i, array in enumerate(arrays):
@@ -197,11 +199,11 @@
 
     @pl.when(lax.axis_index("head") == 0)
     def _():
-        run_copies(pairs((k, v)), sems)
+        run_copies(pairs((k, v), outs), sems)
 
     @pl.when(lax.axis_index("head") == 1)
     def _():
-        run_copies(pairs((q, q)), sems)
+        run_copies(pairs((q, q), outs), sems)
 
 
 def core_kernel(width, start, size, flip, q, k, v, after, out, sems):
@@ -253,103 +255,156 @@
     return jnp.where(lanes == lane, column, into)
 
 
-def early_kernel(per, size, factor, bias, own, par, two, three, kept, loc0, loc1, part0, part1):
-    rows = own.shape[0]
+def column(stat, lane):
+    lanes = lax.broadcasted_iota(jnp.int32, stat.shape, 1)
+    return jnp.sum(jnp.where(lanes == lane, stat, 0.0), axis=1, keepdims=True)
+
+
+def resume(scores, values, mixed, top, total):
+    here = jnp.maximum(jnp.max(scores, axis=1, keepdims=True), top)
+    weights = jnp.exp2(scores - here)
+    carry = jnp.exp2(top - here)
+    total = jnp.sum(weights, axis=1, keepdims=True) + total * carry
+    more = jnp.dot(weights.astype(jnp.bfloat16), values, preferred_element_type=jnp.float32)
+    return more + mixed * carry, here, total
+
+
+class Rows:
+    def __init__(self, size, first, second):
+        self.size, self.refs, self.rows = size, (first, second), first.shape[0]
+
+    def clear(self):
+        for ref in self.refs:
+            ref[:, self.size :] = jnp.zeros((self.rows, HD), jnp.float32)
+
+    def put(self, col, mixed):
+        for i, ref in enumerate(self.refs):
+            ref[:, col] = mixed[i * self.rows : (i + 1) * self.rows].astype(ref.dtype)
+
+    def put_stat(self, head, top, total):
+        for i, ref in enumerate(self.refs):
+            at = slice(i * self.rows, (i + 1) * self.rows)
+            stat = lane_put(ref[:, self.size :], 2 * head, top[at])
+            ref[:, self.size :] = lane_put(stat, 2 * head + 1, total[at])
+
+    def get(self, col, head):
+        mixed = jnp.concatenate([ref[:, col] for ref in self.refs], axis=0)
+        stat = jnp.concatenate([ref[:, self.size :] for ref in self.refs], axis=0)
+        return mixed, column(stat, 2 * head), column(stat, 2 * head + 1)
+
+
+def each_head(per, size, work):
+    def step(h, carry):
+        for j in range(per):
+            head = h * per + j
+            work(head, pl.ds(pl.multiple_of(head * HD, HD), HD))
+        return carry
+
+    lax.fori_loop(0, size // HD // per, step, 0)
+
+
+def part_of(refs, size, t, head):
+    at = pl.ds(pl.multiple_of(t * size + head * HD, HD), HD)
+    return [ref[:, at] for ref in refs]
+
+
+def rows_of(refs, size, t, head):
+    return jnp.concatenate(part_of(refs, size, t, head), axis=0)
+
+
+def span_kernel(per, size, factor, bias, own, par, a0, a1, b0, b1):
+    def work(head, col):
+        for base, rows in ((0, first), (3, second)):
+            k, v = (rows_of((own, par), size, base + t, head) for t in (1, 2))
+            scores = logits(rows_of((own, par), size, base, head), k, factor)
+            mixed, top, total = soft(biased(scores, 0, bias), v)
+            rows.put(col, mixed)
+            rows.put_stat(head, top, total)
+
+    first, second = Rows(size, a0, a1), Rows(size, b0, b1)
+    first.clear()
+    second.clear()
+    each_head(per, size, work)
+
+
+def other_kernel(per, size, factor, own, par, two, three, b0, b1, s0, s1):
+    second, result = Rows(size, b0, b1), Rows(size, s0, s1)
+    result.clear()
+
+    def keep(head, col, mixed, top, total):
+        result.put(col, mixed)
+        result.put_stat(head, top, total)
+
+    def on_first(head, col):
+        k, v = (rows_of((own, par), size, t, head) for t in (1, 2))
+        keep(head, col, *soft(logits(rows_of((two, three), size, 0, head), k, factor), v))
+
+    def on_second(head, col):
+        k, v = (rows_of((two, three), size, t, head) for t in (0, 1))
+        scores = logits(rows_of((own, par), size, 3, head), k, factor)
+        keep(head, col, *resume(scores, v, *second.get(col, head)))
+
+    @pl.when(lax.axis_index("head") == 0)
+    def _():
+        each_head(per, size, on_first)
+
+    @pl.when(lax.axis_index("head") == 1)
+    def _():
+        each_head(per, size, on_second)
+
+
+def early_kernel(per, size, factor, own, par, two, three, kept, a0, a1, p0, p1, loc0, loc1, part0, part1):
     heads = size // HD
-    locs, parts = (loc0, loc1), (part0, part1)
-    for loc in locs:
-        loc[:, size:] = jnp.zeros((rows, HD), jnp.float32)
-
-    def columns(h, j):
-        head = (h * per + j) * HD
-
-        def pick(t):
-            at = pl.ds(pl.multiple_of(t * size + head, HD), HD)
-            return jnp.concatenate([own[:, at], par[:, at]], axis=0)
-
-        return pl.ds(pl.multiple_of(head, HD), HD), pick
-
-    def put(lane, top, total):
-        for i, loc in enumerate(locs):
-            at = slice(i * rows, (i + 1) * rows)
-            stat = lane_put(loc[:, size:], lane, top[at])
-            loc[:, size:] = lane_put(stat, lane + 1, total[at])
-
-    def first_chip(h, carry):
-        for j in range(per):
-            col, pick = columns(h, j)
-            k = jnp.concatenate([kept[: 2 * BLOCK, col], pick(1)], axis=0)
-            v = jnp.concatenate([kept[2 * BLOCK :, col], pick(2)], axis=0)
-            mixed, top, total = soft(biased(logits(pick(0), k, factor), 2 * BLOCK, bias), v)
-            mixed = mixed * (1.0 / total)
-            loc0[:, col], loc1[:, col] = mixed[:rows], mixed[rows:]
-            q = jnp.concatenate([two[:, col], three[:, col]], axis=0)
-            mixed, top, total = soft(logits(q, k, factor), v)
-            mixed = (mixed * (1.0 / total)).astype(jnp.bfloat16)
-            part0[:, col], part1[:, col] = mixed[:rows], mixed[rows:]
-            put((h * per + j) * 2, top, total)
-        return carry
-
-    def second_chip(h, carry):
-        for j in range(per):
-            col, pick = columns(h, j)
-            mixed, top, total = soft(biased(logits(pick(0), pick(1), factor), 0, bias), pick(2))
-            loc0[:, col], loc1[:, col] = mixed[:rows], mixed[rows:]
-            put((h * per + j) * 2, top, total)
-        return carry
+    first, partial = Rows(size, a0, a1), Rows(size, p0, p1)
+    loc, part = Rows(size, loc0, loc1), Rows(size, part0, part1)
+
+    def on_first(head, col):
+        k, v = kept[: 2 * BLOCK, col], kept[2 * BLOCK :, col]
+        scores = logits(rows_of((own, par), size, 0, head), k, factor)
+        mixed, top, total = resume(scores, v, *first.get(col, head))
+        loc.put(col, mixed * (1.0 / total))
+        scores = logits(rows_of((two, three), size, 0, head), k, factor)
+        mixed, top, total = resume(scores, v, *partial.get(col, head))
+        part.put(col, mixed * (1.0 / total))
+        loc.put_stat(head, top, total)
 
     @pl.when(lax.axis_index("head") == 0)
     def _():
-        lax.fori_loop(0, heads // per, first_chip, 0)
-        for loc, part in zip(locs, parts):
-            left = loc[:, size:]
+        loc.clear()
+        each_head(per, size, on_first)
+        for source, into in zip(loc.refs, part.refs):
+            left = source[:, size:]
             packed = jnp.zeros_like(left)
             for t in range(3):
                 piece = left.astype(jnp.bfloat16).astype(jnp.float32)
                 left = left - piece
                 packed = packed + (pltpu.roll(piece, 2 * heads * t, 1) if t > 0 else piece)
-            part[:, size:] = packed.astype(jnp.bfloat16)
+            into[:, size:] = packed.astype(jnp.bfloat16)
 
     @pl.when(lax.axis_index("head") == 1)
     def _():
-        lax.fori_loop(0, heads // per, second_chip, 0)
-
-
-def late_kernel(per, size, factor, bias, own, par, two, three, kept, crossed, out0, out1):
-    rows = own.shape[0]
-
-    def run(cache, with_first):
-        def step(h, carry):
-            for j in range(per):
-                head = (h * per + j) * HD
-                col = pl.ds(pl.multiple_of(head, HD), HD)
-
-                def pick(t):
-                    at = pl.ds(pl.multiple_of((3 + t) * size + head, HD), HD)
-                    return [own[:, at], par[:, at]]
-
-                k, v = [cache[: 2 * BLOCK, col]] + pick(1), [cache[2 * BLOCK :, col]] + pick(2)
-                if with_first:
-                    there = pl.ds(pl.multiple_of(size + head, HD), HD)
-                    k += [two[:, col], three[:, col]]
-                    v += [two[:, there], three[:, there]]
-                scores = logits(
-                    jnp.concatenate(pick(0), axis=0), jnp.concatenate(k, axis=0), factor
-                )
-                mixed, _, total = soft(biased(scores, 2 * BLOCK, bias), jnp.concatenate(v, axis=0))
-                mixed = (mixed * (1.0 / total)).astype(jnp.bfloat16)
-                out0[:, col], out1[:, col] = mixed[:rows], mixed[rows:]
-            return carry
-
-        lax.fori_loop(0, size // HD // per, step, 0)
+        for source, into in zip(first.refs, loc.refs):
+            into[...] = source[...]
+
+
+def late_kernel(per, size, factor, own, par, kept, crossed, b0, b1, s0, s1, out0, out1):
+    out = Rows(size, out0, out1)
+
+    def run(cache, second):
+        def work(head, col):
+            scores = logits(rows_of((own, par), size, 3, head), cache[: 2 * BLOCK, col], factor)
+            mixed, _, total = resume(scores, cache[2 * BLOCK :, col], *second.get(col, head))
+            out.put(col, mixed * (1.0 / total))
+
+        each_head(per, size, work)
 
     @pl.when(lax.axis_index("head") == 0)
     def _():
-        run(crossed, False)
+        run(crossed, Rows(size, b0, b1))
 
     @pl.when(lax.axis_index("head") == 1)
     def _():
-        run(kept, True)
+        run(kept, Rows(size, s0, s1))
 
 
 def finish_kernel(width, start, size, count, *refs):
@@ -410,7 +465,7 @@
         first += count
     factor = float(HD) ** (-0.5) * LOG2E
     blk_dev = key_cache.shape[0] // BLOCK
-    picks = selection.T
+    picks = pltpu.with_memory_space_constraint(selection.T, pltpu.HBM)
     anywhere = pl.BlockSpec(memory_space=pl.ANY)
     in_hbm = pl.BlockSpec(memory_space=pltpu.HBM)
     resident = pl.BlockSpec(memory_space=pltpu.VMEM)
@@ -492,17 +547,27 @@
     for i, (start, size) in enumerate(chunks):
         kept, crossed = fetch(i)
         per = 2 if size // HD % 2 == 0 else 1
-        given = [bias, own[i], par[i], *crossing[i], kept]
+        both = [own[i], par[i]]
+        held_f32, held_bf16 = ((rows, size + HD), f32), ((rows, size + HD), bf16)
+        a0, a1, b0, b1 = call(
+            functools.partial(span_kernel, per, size, factor), [bias] + both,
+            [resident] * 3, [held_f32] * 4,
+        )
+        s0, s1 = call(
+            functools.partial(other_kernel, per, size, factor),
+            both + crossing[i] + [b0, b1], [resident] * 6, [held_f32] * 2,
+        )
         loc0, loc1, part0, part1 = call(
-            functools.partial(early_kernel, per, size, factor), given, [resident] * 6,
-            [((rows, size + HD), f32)] * 2 + [((rows, size + HD), bf16)] * 2,
+            functools.partial(early_kernel, per, size, factor),
+            both + crossing[i] + [kept, a0, a1, s0, s1], [resident] * 9,
+            [held_f32] * 2 + [held_bf16] * 2,
         )
         far0 = move(part0, apart(2, (0, 1)))
         far1 = move(part1, apart(3, (0, 1)))
         got_loc = move(loc1, apart(1))
         out0, out1 = call(
-            functools.partial(late_kernel, per, size, factor), given + [crossed],
-            [resident] * 7, [((rows, size), bf16)] * 2,
+            functools.partial(late_kernel, per, size, factor),
+            both + [kept, crossed, b0, b1, s0, s1], [resident] * 8, [((rows, size), bf16)] * 2,
         )
         got = move(out1, apart(1))
         pieces = [out0, got, loc0, got_loc, far0, far1]

time: 128 us -> 131 us (1.023)
  Pallas kernels: 29.7 us -> 38.4 us
  waiting for transfers between devices: 71.4 us -> 66.3 us
    pallas_call x15 -> x19, Pallas kernels: 29.7 us -> 38.4 us  [call(): pl.pallas_call(kernel, out_shape=[pltpu.VMEM(*s) for s in shapes] if resu...]
    ppermute x22, waiting for transfers between devices: 71.4 us -> 66.3 us  [move(): return lax.ppermute(x, axes, list(pairs))]
  transfers between devices with their start and end apart: 22 -> 22, of which waited for: 9 -> 10; matrix products, arithmetic and copies ran while one was open for 0% -> 0% of each run, Pallas kernels for 18% -> 24%
where the time goes in v4:
time: 131 us; the launch traced here: 130 us
  waiting for transfers between devices  66.3 us (51%)
  Pallas kernels  38.4 us (29%)
  starting transfers between devices  25.1 us (19%)
    ppermute x22, waiting for transfers between devices, move(): return lax.ppermute(x, axes, list(pairs))  66.3 us
    pallas_call x19, Pallas kernels, call(): pl.pallas_call(kernel, out_shape=[pltpu.VMEM(*s) for s in shapes] if resu...  38.4 us
    ppermute x22, starting transfers between devices, move(): return lax.ppermute(x, axes, list(pairs))  25.1 us
  transfers between devices with their start and end apart: 22, of which 10 were waited for; matrix products, arithmetic and copies ran while one was open for 0% of the time, Pallas kernels for 24%

profile of v4, /device:TPU:0, one launch (start us, length us, event | category | flops | bytes accessed | tf_op | source)
XLA Modules:
  0.0 130.0 jit_solution(8070731209349475550)
XLA Ops:
  0.0 2.5 %shard_map.64 = (bf16[128,1280]{1,0:T(8,128)(2,1)S(1)}, bf16[128,1280]{1,0:T(8,128)(2,1)S(1)}, bf16[128,1280]{1,0:T(8,128)(2,1)S(1)}, bf16[128,1280]{1,0:T(8,128...) custom-call(s32[2,4]{1,0:T(2,128)} %bitcast.1, ...), custom_call_target="tpu_custom_call" | custom-call | tf_op jit(solution)/shard_map/pallas_call | solution.py:475
  2.6 1.4 %shard_map.65 = (bf16[96,2560]{1,0:T(8,128)(2,1)S(1)}, bf16[96,2560]{1,0:T(8,128)(2,1)S(1)}) custom-call(bf16[96,8192]{1,0:T(8,128)(2,1)} %q.11, bf16[96,8192]{1,0:T(8,128)(2,1)} %k.11, bf16[96,8192]{1,0:T(8,128)(2,1)} %v.11, bf16[128,1280]{1,0:T(8,128)(2,1)S(1)} %get-tuple-element.42.after), custom_call_target="tpu_custom_call" | custom-call | tf_op jit(solution)/shard_map/pallas_call | solution.py:475
  3.9 1.2 shard_map.66
  5.1 1.5 %shard_map.67.after = bf16[96,7680]{1,0:T(8,128)(2,1)S(1)} custom-call(bf16[96,8192]{1,0:T(8,128)(2,1)} %q.11, bf16[96,8192]{1,0:T(8,128)(2,1)} %k.11, bf16[96,8192]{1,0:T(8,128)(2,1)} %v.11, bf16[96,1536]{1,0:T(8,128)(2,1)S(1)} %get-tuple-element.44.after), custom_call_target="tpu_custom_call" | custom-call | tf_op jit(solution)/shard_map/pallas_call | solution.py:475
  6.6 0.6 collective-permute-start.11
  7.2 2.6 %collective-permute-start.1 = (bf16[128,768]{1,0:T(8,128)(2,1)S(1)}, bf16[128,768]{1,0:T(8,128)(2,1)S(1)}, u32[]{:S(2)}, u32[]{:S(2)}) collective-permute-start(bf16[128,768]{1,0:T(8,128)(2,1)S(1)} %get-tuple-element.46), channel_id=1, source_target_pairs={{0,4},{4,0},{8,12},{12,8},{1,5},{5,1},{9,13},{13,9},{2,6},{6,2},{1... | collective-permute-start | bytes 589832 | tf_op jit(solution)/shard_map/ppermute | solution.py:490
  9.8 2.7 %collective-permute-start.13 = (bf16[128,1280]{1,0:T(8,128)(2,1)S(1)}, bf16[128,1280]{1,0:T(8,128)(2,1)S(1)}, u32[]{:S(2)}, u32[]{:S(2)}) collective-permute-start(bf16[128,1280]{1,0:T(8,128)(2,1)S(1)} %get-tuple-element.64), channel_id=1, source_target_pairs={{0,8},{4,12},{8,0},{12,4},{1,9},{5,13},{9,1},{13,5},{2,10},{6,14},... | collective-permute-start | bytes 983048 | tf_op jit(solution)/shard_map/ppermute | solution.py:490
  12.6 0.0 collective-permute-start.14
  12.6 0.7 collective-permute-start.12
  13.3 6.3 %collective-permute-done.1.refs_1_ = bf16[128,768]{1,0:T(8,128)(2,1)S(1)} collective-permute-done((bf16[128,768]{1,0:T(8,128)(2,1)S(1)}, bf16[128,768]{1,0:T(8,128)(2,1)S(1)}, u32[]{:S(2)}, u32[]{:S(2)}) %collective-permute-start.1) | collective-permute-done | bytes 196640 | tf_op jit(solution)/shard_map/ppermute | solution.py:490
  19.6 1.3 collective-permute-start.2
  20.9 29.3 %collective-permute-done.2.refs_2_ = bf16[128,768]{1,0:T(8,128)(2,1)S(1)} collective-permute-done((bf16[128,768]{1,0:T(8,128)(2,1)S(1)}, bf16[128,768]{1,0:T(8,128)(2,1)S(1)}, u32[]{:S(2)}, u32[]{:S(2)}) %collective-permute-start.2) | collective-permute-done | bytes 196640 | tf_op jit(solution)/shard_map/ppermute | solution.py:490
  50.2 0.5 collective-permute-start.17
  50.7 1.3 %shard_map.68.after = bf16[96,4608]{1,0:T(8,128)(2,1)S(1)} custom-call(bf16[96,8192]{1,0:T(8,128)(2,1)} %q.11, bf16[96,8192]{1,0:T(8,128)(2,1)} %k.11, bf16[96,8192]{1,0:T(8,128)(2,1)} %v.11, bf16[96,7680]{1,0:T(8,128)(2,1)S(1)} %shard_map.67.after), custom_call_target="tpu_custom_call" | custom-call | tf_op jit(solution)/shard_map/pallas_call | solution.py:475
  52.0 0.0 collective-permute-done.13.refs_2_
  52.0 1.2 collective-permute-start
  53.2 0.0 collective-permute-done.14.refs_3_
  53.2 2.4 %collective-permute-start.3 = (bf16[128,768]{1,0:T(8,128)(2,1)S(1)}, bf16[128,768]{1,0:T(8,128)(2,1)S(1)}, u32[]{:S(2)}, u32[]{:S(2)}) collective-permute-start(bf16[128,768]{1,0:T(8,128)(2,1)S(1)} %get-tuple-element.48), channel_id=1, source_target_pairs={{0,12},{4,8},{8,4},{12,0},{1,13},{5,9},{9,5},{13,1},{2,14},{6,10},... | collective-permute-start | bytes 589832 | tf_op jit(solution)/shard_map/ppermute | solution.py:490
  55.5 0.0 collective-permute-done.12.refs_1_
  55.6 0.5 collective-permute-start.16
  56.1 0.8 shard_map.76.kept
  56.9 5.1 %collective-permute-done.3.refs_3_ = bf16[128,768]{1,0:T(8,128)(2,1)S(1)} collective-permute-done((bf16[128,768]{1,0:T(8,128)(2,1)S(1)}, bf16[128,768]{1,0:T(8,128)(2,1)S(1)}, u32[]{:S(2)}, u32[]{:S(2)}) %collective-permute-start.3) | collective-permute-done | bytes 196640 | tf_op jit(solution)/shard_map/ppermute | solution.py:490
  62.0 1.3 collective-permute-start.15
  63.3 0.4 collective-permute-done.17.three
  63.6 0.9 collective-permute-start.6
  64.5 0.8 shard_map.71.kept
  65.3 9.0 %collective-permute-done.16.two = bf16[96,2560]{1,0:T(8,128)(2,1)S(1)} collective-permute-done((bf16[96,2560]{1,0:T(8,128)(2,1)S(1)}, bf16[96,2560]{1,0:T(8,128)(2,1)S(1)}, u32[]{:S(2)}, u32[]{:S(2)}) %collective-permute-start.16) | collective-permute-done | bytes 491552 | tf_op jit(solution)/shard_map/ppermute | solution.py:490
  74.3 1.3 collective-permute-start.4
  75.6 0.0 collective-permute-done.11.par
  75.6 2.7 %collective-permute-start.5 = (bf16[96,1536]{1,0:T(8,128)(2,1)S(1)}, bf16[96,1536]{1,0:T(8,128)(2,1)S(1)}, u32[]{:S(2)}, u32[]{:S(2)}) collective-permute-start(bf16[96,1536]{1,0:T(8,128)(2,1)S(1)} %get-tuple-element.44.after), channel_id=1, source_target_pairs={{0,2},{1,3},{2,0},{3,1},{4,6},{5,7},{6,4},{7,5},{8,10},{9,11},{10,... | collective-permute-start | bytes 884744 | tf_op jit(solution)/shard_map/ppermute | solution.py:490
  78.3 1.5 %shard_map.69.after.own = bf16[96,7680]{1,0:T(8,128)(2,1)S(1)} custom-call(bf16[96,8192]{1,0:T(8,128)(2,1)} %q.11, bf16[96,8192]{1,0:T(8,128)(2,1)} %k.11, bf16[96,8192]{1,0:T(8,128)(2,1)} %v.11, bf16[96,4608]{1,0:T(8,128)(2,1)S(1)} %shard_map.68.after), custom_call_target="tpu_custom_call" | custom-call | tf_op jit(solution)/shard_map/pallas_call | solution.py:475
  79.8 4.0 %shard_map.77 = (f32[96,1408]{1,0:T(8,128)S(1)}, f32[96,1408]{1,0:T(8,128)S(1)}, f32[96,1408]{1,0:T(8,128)S(1)}, f32[96,1408]{1,0:T(8,128)S(1)}) custom-call(f32[192,256]{1,0:T(8,128)S(1)} %get-tuple-element.49.bias, bf16[96,7680]{1,0:T(8,128)(2,1)S(1)} %shard_map.69.after.own, bf16[96,7680]{1,0:T(8,128)(2,1)S(1)} %collective-permute-done.11.par), custom_call_target="tpu_custom_call" | custom-call | tf_op jit(solution)/shard_map/pallas_call | solution.py:475
  83.8 3.4 %shard_map.78 = (f32[96,1408]{1,0:T(8,128)S(1)}, f32[96,1408]{1,0:T(8,128)S(1)}) custom-call(bf16[96,7680]{1,0:T(8,128)(2,1)S(1)} %shard_map.69.after.own, bf16[96,7680]{1,0:T(8,128)(2,1)S(1)} %collective-permute-done.11.par, bf16[96,2560]{1,0:T(8,128)(2,1)S(1)} %collective-permute-done.16.two, bf16[96,2560]{1,0:T(8,128)(2,1)S(1)} %collective-permute-done.17.three, ...), custom_call_target="tpu_custom_call" | custom-call | tf_op jit(solution)/shard_map/pallas_call | solution.py:475
  87.2 4.6 %shard_map.80 = (f32[96,1408]{1,0:T(8,128)S(1)}, f32[96,1408]{1,0:T(8,128)S(1)}, bf16[96,1408]{1,0:T(8,128)(2,1)S(1)}, bf16[96,1408]{1,0:T(8,128)(2,1)S(1)}) custom-call(bf16[96,7680]{1,0:T(8,128)(2,1)S(1)} %shard_map.69.after.own, bf16[96,7680]{1,0:T(8,128)(2,1)S(1)} %collective-permute-done.11.par, bf16[96,2560]{1,0:T(8,128)(2,1)S(1)} %collective-permute-done.16.two, ...), custom_call_target="tpu_custom_call" | custom-call | tf_op jit(solution)/shard_map/pallas_call | solution.py:475
  91.9 2.7 %collective-permute-done.6.three = bf16[96,1536]{1,0:T(8,128)(2,1)S(1)} collective-permute-done((bf16[96,1536]{1,0:T(8,128)(2,1)S(1)}, bf16[96,1536]{1,0:T(8,128)(2,1)S(1)}, u32[]{:S(2)}, u32[]{:S(2)}) %collective-permute-start.6) | collective-permute-done | bytes 294944 | tf_op jit(solution)/shard_map/ppermute | solution.py:490
  94.5 0.1 collective-permute-start.19
  94.7 0.0 collective-permute-done.15.crossed
  94.7 1.5 %collective-permute-start.20 = (bf16[96,1408]{1,0:T(8,128)(2,1)S(1)}, bf16[96,1408]{1,0:T(8,128)(2,1)S(1)}, u32[]{:S(2)}, u32[]{:S(2)}) collective-permute-start(bf16[96,1408]{1,0:T(8,128)(2,1)S(1)} %get-tuple-element.77), channel_id=1, source_target_pairs={{0,2},{1,3},{4,6},{5,7},{8,10},{9,11},{12,14},{13,15},{16,18},{17,... | collective-permute-start | bytes 811016 | tf_op jit(solution)/shard_map/ppermute | solution.py:490
  96.1 3.1 %shard_map.79 = (bf16[96,1280]{1,0:T(8,128)(2,1)S(1)}, bf16[96,1280]{1,0:T(8,128)(2,1)S(1)}) custom-call(bf16[96,7680]{1,0:T(8,128)(2,1)S(1)} %shard_map.69.after.own, bf16[96,7680]{1,0:T(8,128)(2,1)S(1)} %collective-permute-done.11.par, bf16[256,1280]{1,0:T(8,128)(2,1)S(1)} %shard_map.76.kept, bf16[256,1280]{1,0:T(8,128)(2,1)S(1)} %collective-permute-done.15.crossed, ...), custom_call_target="tpu_custom_call" | custom-call | tf_op jit(solution)/shard_map/pallas_call | solution.py:475
  99.2 10.1 %collective-permute-done.5.two = bf16[96,1536]{1,0:T(8,128)(2,1)S(1)} collective-permute-done((bf16[96,1536]{1,0:T(8,128)(2,1)S(1)}, bf16[96,1536]{1,0:T(8,128)(2,1)S(1)}, u32[]{:S(2)}, u32[]{:S(2)}) %collective-permute-start.5) | collective-permute-done | bytes 294944 | tf_op jit(solution)/shard_map/ppermute | solution.py:490
  109.3 0.1 collective-permute-start.18
  109.4 0.0 collective-permute-done.par
  109.4 1.5 %collective-permute-start.21 = (bf16[96,1408]{1,0:T(8,128)(2,1)S(1)}, bf16[96,1408]{1,0:T(8,128)(2,1)S(1)}, u32[]{:S(2)}, u32[]{:S(2)}) collective-permute-start(bf16[96,1408]{1,0:T(8,128)(2,1)S(1)} %get-tuple-element.78), channel_id=1, source_target_pairs={{0,3},{1,2},{4,7},{5,6},{8,11},{9,10},{12,15},{13,14},{16,19},{17,... | collective-permute-start | bytes 811016 | tf_op jit(solution)/shard_map/ppermute | solution.py:490
  110.9 1.3 %shard_map.70.own = bf16[96,4608]{1,0:T(8,128)(2,1)S(1)} custom-call(bf16[96,8192]{1,0:T(8,128)(2,1)} %q.11, bf16[96,8192]{1,0:T(8,128)(2,1)} %k.11, bf16[96,8192]{1,0:T(8,128)(2,1)} %v.11, bf16[96,7680]{1,0:T(8,128)(2,1)S(1)} %shard_map.69.after.own), custom_call_target="tpu_custom_call" | custom-call | tf_op jit(solution)/shard_map/pallas_call | solution.py:475
  112.3 2.4 %shard_map.72 = (f32[96,896]{1,0:T(8,128)S(1)}, f32[96,896]{1,0:T(8,128)S(1)}, f32[96,896]{1,0:T(8,128)S(1)}, f32[96,896]{1,0:T(8,128)S(1)}) custom-call(f32[192,256]{1,0:T(8,128)S(1)} %get-tuple-element.49.bias, bf16[96,4608]{1,0:T(8,128)(2,1)S(1)} %shard_map.70.own, bf16[96,4608]{1,0:T(8,128)(2,1)S(1)} %collective-permute-done.par), custom_call_target="tpu_custom_call" | custom-call | tf_op jit(solution)/shard_map/pallas_call | solution.py:475
  114.7 2.1 %shard_map.73 = (f32[96,896]{1,0:T(8,128)S(1)}, f32[96,896]{1,0:T(8,128)S(1)}) custom-call(bf16[96,4608]{1,0:T(8,128)(2,1)S(1)} %shard_map.70.own, bf16[96,4608]{1,0:T(8,128)(2,1)S(1)} %collective-permute-done.par, bf16[96,1536]{1,0:T(8,128)(2,1)S(1)} %collective-permute-done.5.two, bf16[96,1536]{1,0:T(8,128)(2,1)S(1)} %collective-permute-done.6.three, ...), custom_call_target="tpu_custom_call" | custom-call | tf_op jit(solution)/shard_map/pallas_call | solution.py:475
  116.7 2.8 %shard_map.75 = (f32[96,896]{1,0:T(8,128)S(1)}, f32[96,896]{1,0:T(8,128)S(1)}, bf16[96,896]{1,0:T(8,128)(2,1)S(1)}, bf16[96,896]{1,0:T(8,128)(2,1)S(1)}) custom-call(bf16[96,4608]{1,0:T(8,128)(2,1)S(1)} %shard_map.70.own, bf16[96,4608]{1,0:T(8,128)(2,1)S(1)} %collective-permute-done.par, bf16[96,1536]{1,0:T(8,128)(2,1)S(1)} %collective-permute-done.5.two, ...), custom_call_target="tpu_custom_call" | custom-call | tf_op jit(solution)/shard_map/pallas_call | solution.py:475
  119.6 0.0 collective-permute-done.4.crossed
  119.6 0.3 collective-permute-start.8
  119.9 0.0 collective-permute-done.18.refs_1_
  119.9 1.3 collective-permute-start.9
  121.2 0.0 collective-permute-done.20.refs_4_
  121.2 1.3 collective-permute-start.10
  122.5 1.9 %shard_map.74 = (bf16[96,768]{1,0:T(8,128)(2,1)S(1)}, bf16[96,768]{1,0:T(8,128)(2,1)S(1)}) custom-call(bf16[96,4608]{1,0:T(8,128)(2,1)S(1)} %shard_map.70.own, bf16[96,4608]{1,0:T(8,128)(2,1)S(1)} %collective-permute-done.par, bf16[256,768]{1,0:T(8,128)(2,1)S(1)} %shard_map.71.kept, bf16[256,768]{1,0:T(8,128)(2,1)S(1)} %collective-permute-done.4.crossed, ...), custom_call_target="tpu_custom_call" | custom-call | tf_op jit(solution)/shard_map/pallas_call | solution.py:475
  124.4 0.0 collective-permute-done.21.refs_5_
  124.4 0.4 collective-permute-start.7
  124.7 0.0 collective-permute-done.19.refs_3_
  124.7 1.0 shard_map.81.refs_6_
  125.7 0.1 collective-permute-done.7.refs_1_
  125.8 0.1 collective-permute-done.9.refs_4_
  125.9 3.3 %collective-permute-done.10.refs_5_ = bf16[96,896]{1,0:T(8,128)(2,1)S(1)} collective-permute-done((bf16[96,896]{1,0:T(8,128)(2,1)S(1)}, bf16[96,896]{1,0:T(8,128)(2,1)S(1)}, u32[]{:S(2)}, u32[]{:S(2)}) %collective-permute-start.10) | collective-permute-done | bytes 172064 | tf_op jit(solution)/shard_map/ppermute | solution.py:490
  129.2 0.0 collective-permute-done.8.refs_3_
  129.2 0.8 shard_map.82
Async XLA Ops:
  6.6 68.9 %collective-permute-start.11 = (bf16[96,7680]{1,0:T(8,128)(2,1)S(1)}, bf16[96,7680]{1,0:T(8,128)(2,1)S(1)}, u32[]{:S(2)}, u32[]{:S(2)}) collective-permute-start(bf16[96,7680]{1,0:T(8,128)(2,1)S(1)} %shard_map.67.after), channel_id=1, source_target_pairs={{0,1},{1,0},{2,3},{3,2},{4,5},{5,4},{6,7},{7,6},{8,9},{9,8},{10,11... | collective-permute-start | bytes 4423688 | tf_op jit(solution)/shard_map/ppermute | solution.py:490
  7.2 12.4 %collective-permute-start.1 = (bf16[128,768]{1,0:T(8,128)(2,1)S(1)}, bf16[128,768]{1,0:T(8,128)(2,1)S(1)}, u32[]{:S(2)}, u32[]{:S(2)}) collective-permute-start(bf16[128,768]{1,0:T(8,128)(2,1)S(1)} %get-tuple-element.46), channel_id=1, source_target_pairs={{0,4},{4,0},{8,12},{12,8},{1,5},{5,1},{9,13},{13,9},{2,6},{6,2},{1... | collective-permute-start | bytes 589832 | tf_op jit(solution)/shard_map/ppermute | solution.py:490
  9.8 42.2 %collective-permute-start.13 = (bf16[128,1280]{1,0:T(8,128)(2,1)S(1)}, bf16[128,1280]{1,0:T(8,128)(2,1)S(1)}, u32[]{:S(2)}, u32[]{:S(2)}) collective-permute-start(bf16[128,1280]{1,0:T(8,128)(2,1)S(1)} %get-tuple-element.64), channel_id=1, source_target_pairs={{0,8},{4,12},{8,0},{12,4},{1,9},{5,13},{9,1},{13,5},{2,10},{6,14},... | collective-permute-start | bytes 983048 | tf_op jit(solution)/shard_map/ppermute | solution.py:490
  12.6 40.6 %collective-permute-start.14 = (bf16[128,1280]{1,0:T(8,128)(2,1)S(1)}, bf16[128,1280]{1,0:T(8,128)(2,1)S(1)}, u32[]{:S(2)}, u32[]{:S(2)}) collective-permute-start(bf16[128,1280]{1,0:T(8,128)(2,1)S(1)} %get-tuple-element.65), channel_id=1, source_target_pairs={{0,12},{4,8},{8,4},{12,0},{1,13},{5,9},{9,5},{13,1},{2,14},{6,10},... | collective-permute-start | bytes 983048 | tf_op jit(solution)/shard_map/ppermute | solution.py:490
  12.6 43.0 %collective-permute-start.12 = (bf16[128,1280]{1,0:T(8,128)(2,1)S(1)}, bf16[128,1280]{1,0:T(8,128)(2,1)S(1)}, u32[]{:S(2)}, u32[]{:S(2)}) collective-permute-start(bf16[128,1280]{1,0:T(8,128)(2,1)S(1)} %get-tuple-element.42.after), channel_id=1, source_target_pairs={{0,4},{4,0},{8,12},{12,8},{1,5},{5,1},{9,13},{13,9},{2,6},{6,2},{1... | collective-permute-start | bytes 983048 | tf_op jit(solution)/shard_map/ppermute | solution.py:490
  19.6 30.6 %collective-permute-start.2 = (bf16[128,768]{1,0:T(8,128)(2,1)S(1)}, bf16[128,768]{1,0:T(8,128)(2,1)S(1)}, u32[]{:S(2)}, u32[]{:S(2)}) collective-permute-start(bf16[128,768]{1,0:T(8,128)(2,1)S(1)} %get-tuple-element.47), channel_id=1, source_target_pairs={{0,8},{4,12},{8,0},{12,4},{1,9},{5,13},{9,1},{13,5},{2,10},{6,14},... | collective-permute-start | bytes 589832 | tf_op jit(solution)/shard_map/ppermute | solution.py:490
  50.2 13.5 %collective-permute-start.17 = (bf16[96,2560]{1,0:T(8,128)(2,1)S(1)}, bf16[96,2560]{1,0:T(8,128)(2,1)S(1)}, u32[]{:S(2)}, u32[]{:S(2)}) collective-permute-start(bf16[96,2560]{1,0:T(8,128)(2,1)S(1)} %get-tuple-element.68), channel_id=1, source_target_pairs={{0,3},{1,2},{2,1},{3,0},{4,7},{5,6},{6,5},{7,4},{8,11},{9,10},{10,... | collective-permute-start | bytes 1474568 | tf_op jit(solution)/shard_map/ppermute | solution.py:490
  52.0 57.4 %collective-permute-start = (bf16[96,4608]{1,0:T(8,128)(2,1)S(1)}, bf16[96,4608]{1,0:T(8,128)(2,1)S(1)}, u32[]{:S(2)}, u32[]{:S(2)}) collective-permute-start(bf16[96,4608]{1,0:T(8,128)(2,1)S(1)} %shard_map.68.after), channel_id=1, source_target_pairs={{0,1},{1,0},{2,3},{3,2},{4,5},{5,4},{6,7},{7,6},{8,9},{9,8},{10,11... | collective-permute-start | bytes 2654216 | tf_op jit(solution)/shard_map/ppermute | solution.py:490
  53.2 8.8 %collective-permute-start.3 = (bf16[128,768]{1,0:T(8,128)(2,1)S(1)}, bf16[128,768]{1,0:T(8,128)(2,1)S(1)}, u32[]{:S(2)}, u32[]{:S(2)}) collective-permute-start(bf16[128,768]{1,0:T(8,128)(2,1)S(1)} %get-tuple-element.48), channel_id=1, source_target_pairs={{0,12},{4,8},{8,4},{12,0},{1,13},{5,9},{9,5},{13,1},{2,14},{6,10},... | collective-permute-start | bytes 589832 | tf_op jit(solution)/shard_map/ppermute | solution.py:490
  55.6 18.7 %collective-permute-start.16 = (bf16[96,2560]{1,0:T(8,128)(2,1)S(1)}, bf16[96,2560]{1,0:T(8,128)(2,1)S(1)}, u32[]{:S(2)}, u32[]{:S(2)}) collective-permute-start(bf16[96,2560]{1,0:T(8,128)(2,1)S(1)} %get-tuple-element.43.after), channel_id=1, source_target_pairs={{0,2},{1,3},{2,0},{3,1},{4,6},{5,7},{6,4},{7,5},{8,10},{9,11},{10,... | collective-permute-start | bytes 1474568 | tf_op jit(solution)/shard_map/ppermute | solution.py:490
  62.0 32.7 %collective-permute-start.15 = (bf16[256,1280]{1,0:T(8,128)(2,1)S(1)}, bf16[256,1280]{1,0:T(8,128)(2,1)S(1)}, u32[]{:S(2)}, u32[]{:S(2)}) collective-permute-start(bf16[256,1280]{1,0:T(8,128)(2,1)S(1)} %shard_map.76.kept), channel_id=1, source_target_pairs={{2,0},{3,1},{6,4},{7,5},{10,8},{11,9},{14,12},{15,13},{18,16},{19,... | collective-permute-start | bytes 1966088 | tf_op jit(solution)/shard_map/ppermute | solution.py:490
  63.6 30.9 %collective-permute-start.6 = (bf16[96,1536]{1,0:T(8,128)(2,1)S(1)}, bf16[96,1536]{1,0:T(8,128)(2,1)S(1)}, u32[]{:S(2)}, u32[]{:S(2)}) collective-permute-start(bf16[96,1536]{1,0:T(8,128)(2,1)S(1)} %get-tuple-element.52), channel_id=1, source_target_pairs={{0,3},{1,2},{2,1},{3,0},{4,7},{5,6},{6,5},{7,4},{8,11},{9,10},{10,... | collective-permute-start | bytes 884744 | tf_op jit(solution)/shard_map/ppermute | solution.py:490
  74.3 45.3 %collective-permute-start.4 = (bf16[256,768]{1,0:T(8,128)(2,1)S(1)}, bf16[256,768]{1,0:T(8,128)(2,1)S(1)}, u32[]{:S(2)}, u32[]{:S(2)}) collective-permute-start(bf16[256,768]{1,0:T(8,128)(2,1)S(1)} %shard_map.71.kept), channel_id=1, source_target_pairs={{2,0},{3,1},{6,4},{7,5},{10,8},{11,9},{14,12},{15,13},{18,16},{19,... | collective-permute-start | bytes 1179656 | tf_op jit(solution)/shard_map/ppermute | solution.py:490
  75.6 33.8 %collective-permute-start.5 = (bf16[96,1536]{1,0:T(8,128)(2,1)S(1)}, bf16[96,1536]{1,0:T(8,128)(2,1)S(1)}, u32[]{:S(2)}, u32[]{:S(2)}) collective-permute-start(bf16[96,1536]{1,0:T(8,128)(2,1)S(1)} %get-tuple-element.44.after), channel_id=1, source_target_pairs={{0,2},{1,3},{2,0},{3,1},{4,6},{5,7},{6,4},{7,5},{8,10},{9,11},{10,... | collective-permute-start | bytes 884744 | tf_op jit(solution)/shard_map/ppermute | solution.py:490
  94.5 30.2 %collective-permute-start.19 = (f32[96,1408]{1,0:T(8,128)S(1)}, f32[96,1408]{1,0:T(8,128)S(1)}, u32[]{:S(2)}, u32[]{:S(2)}) collective-permute-start(f32[96,1408]{1,0:T(8,128)S(1)} %get-tuple-element.76), channel_id=1, source_target_pairs={{0,1},{1,0},{2,3},{3,2},{4,5},{5,4},{6,7},{7,6},{8,9},{9,8},{10,11... | collective-permute-start | bytes 1622024 | tf_op jit(solution)/shard_map/ppermute | solution.py:490
  94.7 26.5 %collective-permute-start.20 = (bf16[96,1408]{1,0:T(8,128)(2,1)S(1)}, bf16[96,1408]{1,0:T(8,128)(2,1)S(1)}, u32[]{:S(2)}, u32[]{:S(2)}) collective-permute-start(bf16[96,1408]{1,0:T(8,128)(2,1)S(1)} %get-tuple-element.77), channel_id=1, source_target_pairs={{0,2},{1,3},{4,6},{5,7},{8,10},{9,11},{12,14},{13,15},{16,18},{17,... | collective-permute-start | bytes 811016 | tf_op jit(solution)/shard_map/ppermute | solution.py:490
  109.3 10.5 %collective-permute-start.18 = (bf16[96,1280]{1,0:T(8,128)(2,1)S(1)}, bf16[96,1280]{1,0:T(8,128)(2,1)S(1)}, u32[]{:S(2)}, u32[]{:S(2)}) collective-permute-start(bf16[96,1280]{1,0:T(8,128)(2,1)S(1)} %get-tuple-element.72), channel_id=1, source_target_pairs={{0,1},{1,0},{2,3},{3,2},{4,5},{5,4},{6,7},{7,6},{8,9},{9,8},{10,11... | collective-permute-start | bytes 737288 | tf_op jit(solution)/shard_map/ppermute | solution.py:490
  109.4 15.0 %collective-permute-start.21 = (bf16[96,1408]{1,0:T(8,128)(2,1)S(1)}, bf16[96,1408]{1,0:T(8,128)(2,1)S(1)}, u32[]{:S(2)}, u32[]{:S(2)}) collective-permute-start(bf16[96,1408]{1,0:T(8,128)(2,1)S(1)} %get-tuple-element.78), channel_id=1, source_target_pairs={{0,3},{1,2},{4,7},{5,6},{8,11},{9,10},{12,15},{13,14},{16,19},{17,... | collective-permute-start | bytes 811016 | tf_op jit(solution)/shard_map/ppermute | solution.py:490
  119.6 9.6 %collective-permute-start.8 = (f32[96,896]{1,0:T(8,128)S(1)}, f32[96,896]{1,0:T(8,128)S(1)}, u32[]{:S(2)}, u32[]{:S(2)}) collective-permute-start(f32[96,896]{1,0:T(8,128)S(1)} %get-tuple-element.60), channel_id=1, source_target_pairs={{0,1},{1,0},{2,3},{3,2},{4,5},{5,4},{6,7},{7,6},{8,9},{9,8},{10,11... | collective-permute-start | bytes 1032200 | tf_op jit(solution)/shard_map/ppermute | solution.py:490
  119.9 6.0 %collective-permute-start.9 = (bf16[96,896]{1,0:T(8,128)(2,1)S(1)}, bf16[96,896]{1,0:T(8,128)(2,1)S(1)}, u32[]{:S(2)}, u32[]{:S(2)}) collective-permute-start(bf16[96,896]{1,0:T(8,128)(2,1)S(1)} %get-tuple-element.61), channel_id=1, source_target_pairs={{0,2},{1,3},{4,6},{5,7},{8,10},{9,11},{12,14},{13,15},{16,18},{17,... | collective-permute-start | bytes 516104 | tf_op jit(solution)/shard_map/ppermute | solution.py:490
  121.2 8.0 %collective-permute-start.10 = (bf16[96,896]{1,0:T(8,128)(2,1)S(1)}, bf16[96,896]{1,0:T(8,128)(2,1)S(1)}, u32[]{:S(2)}, u32[]{:S(2)}) collective-permute-start(bf16[96,896]{1,0:T(8,128)(2,1)S(1)} %get-tuple-element.62), channel_id=1, source_target_pairs={{0,3},{1,2},{4,7},{5,6},{8,11},{9,10},{12,15},{13,14},{16,19},{17,... | collective-permute-start | bytes 516104 | tf_op jit(solution)/shard_map/ppermute | solution.py:490
  124.4 1.4 %collective-permute-start.7 = (bf16[96,768]{1,0:T(8,128)(2,1)S(1)}, bf16[96,768]{1,0:T(8,128)(2,1)S(1)}, u32[]{:S(2)}, u32[]{:S(2)}) collective-permute-start(bf16[96,768]{1,0:T(8,128)(2,1)S(1)} %get-tuple-element.56), channel_id=1, source_target_pairs={{0,1},{1,0},{2,3},{3,2},{4,5},{5,4},{6,7},{7,6},{8,9},{9,8},{10,11... | collective-permute-start | bytes 442376 | tf_op jit(solution)/shard_map/ppermute | solution.py:490

commit v5 on v4

--- a/solution.py
+++ b/solution.py
@@ -185,25 +185,25 @@
         copy.wait()
 
 
-def cross_kernel(width, start, size, q, k, v, after, *refs):
-    outs, sems = refs[:-1], refs[-1]
-
-    def pairs(arrays, outs):
+def cross_kernel(width, chunk, asked, q, k, v, after, two, three, sems):
+    def pairs(wanted):
         result = []
-        for out, d in zip(outs, (2, 3)):
-            at = (group_index() ^ d) * width + start
-            cols = pl.ds(pl.multiple_of(at, HD), size)
-            for i, array in enumerate(arrays):
-                result.append((array.at[:, cols], out.at[:, i * size : (i + 1) * size]))
+        for out, d in ((two, 2), (three, 3)):
+            to = 0
+            for array, (start, size) in wanted:
+                at = (group_index() ^ d) * width + start
+                cols = pl.ds(pl.multiple_of(at, HD), size)
+                result.append((array.at[:, cols], out.at[:, to : to + size]))
+                to += size
         return result
 
     @pl.when(lax.axis_index("head") == 0)
     def _():
-        run_copies(pairs((k, v), outs), sems)
+        run_copies(pairs([(k, chunk), (v, chunk)]), sems)
 
     @pl.when(lax.axis_index("head") == 1)
     def _():
-        run_copies(pairs((q, q), outs), sems)
+        run_copies(pairs([(q, other) for other in asked]), sems)
 
 
 def core_kernel(width, start, size, flip, q, k, v, after, out, sems):
@@ -327,7 +327,7 @@
     each_head(per, size, work)
 
 
-def other_kernel(per, size, factor, own, par, two, three, b0, b1, s0, s1):
+def other_kernel(per, size, asked_at, factor, own, par, two, three, q_two, q_three, b0, b1, s0, s1):
     second, result = Rows(size, b0, b1), Rows(size, s0, s1)
     result.clear()
 
@@ -337,7 +337,8 @@
 
     def on_first(head, col):
         k, v = (rows_of((own, par), size, t, head) for t in (1, 2))
-        keep(head, col, *soft(logits(rows_of((two, three), size, 0, head), k, factor), v))
+        q = rows_of((q_two, q_three), asked_at, 1, head)
+        keep(head, col, *soft(logits(q, k, factor), v))
 
     def on_second(head, col):
         k, v = (rows_of((two, three), size, t, head) for t in (0, 1))
@@ -353,7 +354,7 @@
         each_head(per, size, on_second)
 
 
-def early_kernel(per, size, factor, own, par, two, three, kept, a0, a1, p0, p1, loc0, loc1, part0, part1):
+def early_kernel(per, size, asked_at, factor, own, par, q_two, q_three, kept, a0, a1, p0, p1, loc0, loc1, part0, part1):
     heads = size // HD
     first, partial = Rows(size, a0, a1), Rows(size, p0, p1)
     loc, part = Rows(size, loc0, loc1), Rows(size, part0, part1)
@@ -363,7 +364,7 @@
         scores = logits(rows_of((own, par), size, 0, head), k, factor)
         mixed, top, total = resume(scores, v, *first.get(col, head))
         loc.put(col, mixed * (1.0 / total))
-        scores = logits(rows_of((two, three), size, 0, head), k, factor)
+        scores = logits(rows_of((q_two, q_three), asked_at, 1, head), k, factor)
         mixed, top, total = resume(scores, v, *partial.get(col, head))
         part.put(col, mixed * (1.0 / total))
         loc.put_stat(head, top, total)
@@ -497,12 +498,14 @@
     from_args = [in_hbm] * 3 + [anywhere]
 
     def cross(i, after):
-        start, size = chunks[i]
+        size = chunks[i][1]
         sent = call(
-            functools.partial(cross_kernel, width, start, size), arrays + [after],
-            from_args, [((rows, 2 * size), bf16)] * 2, [pltpu.SemaphoreType.DMA((4,))],
-        )
-        return sent, [move(sent[d - 2], apart(d)) for d in (2, 3)]
+            functools.partial(cross_kernel, width, chunks[i], chunks if i == 0 else ()),
+            arrays + [after], from_args, [((rows, 2 * size), bf16)] * 2,
+            [pltpu.SemaphoreType.DMA((4,))],
+        )
+        sources = range(n) if i == 0 else (0, 1)
+        return sent, [move(sent[d - 2], apart(d, sources)) for d in (2, 3)]
 
     def cores(i, flip, after):
         start, size = chunks[i]
@@ -554,12 +557,12 @@
             [resident] * 3, [held_f32] * 4,
         )
         s0, s1 = call(
-            functools.partial(other_kernel, per, size, factor),
-            both + crossing[i] + [b0, b1], [resident] * 6, [held_f32] * 2,
+            functools.partial(other_kernel, per, size, start, factor),
+            both + crossing[i] + crossing[0] + [b0, b1], [resident] * 8, [held_f32] * 2,
         )
         loc0, loc1, part0, part1 = call(
-            functools.partial(early_kernel, per, size, factor),
-            both + crossing[i] + [kept, a0, a1, s0, s1], [resident] * 9,
+            functools.partial(early_kernel, per, size, start, factor),
+            both + crossing[0] + [kept, a0, a1, s0, s1], [resident] * 9,
             [held_f32] * 2 + [held_bf16] * 2,
         )
         far0 = move(part0, apart(2, (0, 1)))

time: 131 us -> 119 us (0.908)
  waiting for transfers between devices: 66.3 us -> 51.6 us
  starting transfers between devices: 25.1 us -> 28.1 us
    ppermute x22, waiting for transfers between devices: 66.3 us -> 51.6 us  [move(): return lax.ppermute(x, axes, list(pairs))]
    ppermute x22, starting transfers between devices: 25.1 us -> 28.1 us  [move(): return lax.ppermute(x, axes, list(pairs))]
  transfers between devices with their start and end apart: 22 -> 22, of which waited for: 10 -> 8; matrix products, arithmetic and copies ran while one was open for 0% -> 0% of each run, Pallas kernels for 24% -> 26%
where the time goes in v5:
time: 119 us; the launch traced here: 118 us
  waiting for transfers between devices  51.6 us (43%)
  Pallas kernels  38.4 us (32%)
  starting transfers between devices  28.1 us (24%)
    ppermute x22, waiting for transfers between devices, move(): return lax.ppermute(x, axes, list(pairs))  51.6 us
    pallas_call x19, Pallas kernels, call(): pl.pallas_call(kernel, out_shape=[pltpu.VMEM(*s) for s in shapes] if resu...  38.4 us
    ppermute x22, starting transfers between devices, move(): return lax.ppermute(x, axes, list(pairs))  28.1 us
  transfers between devices with their start and end apart: 22, of which 8 were waited for; matrix products, arithmetic and copies ran while one was open for 0% of the time, Pallas kernels for 26%

profile of v5, /device:TPU:0, one launch (start us, length us, event | category | flops | bytes accessed | tf_op | source)
XLA Modules:
  0.0 118.3 jit_solution(17675924214901943523)
XLA Ops:
  0.0 2.5 %shard_map.64 = (bf16[128,1280]{1,0:T(8,128)(2,1)S(1)}, bf16[128,1280]{1,0:T(8,128)(2,1)S(1)}, bf16[128,1280]{1,0:T(8,128)(2,1)S(1)}, bf16[128,1280]{1,0:T(8,128...) custom-call(s32[2,4]{1,0:T(2,128)} %bitcast.1, ...), custom_call_target="tpu_custom_call" | custom-call | tf_op jit(solution)/shard_map/pallas_call | solution.py:476
  2.6 1.4 %shard_map.65 = (bf16[96,2560]{1,0:T(8,128)(2,1)S(1)}, bf16[96,2560]{1,0:T(8,128)(2,1)S(1)}) custom-call(bf16[96,8192]{1,0:T(8,128)(2,1)} %q.11, bf16[96,8192]{1,0:T(8,128)(2,1)} %k.11, bf16[96,8192]{1,0:T(8,128)(2,1)} %v.11, bf16[128,1280]{1,0:T(8,128)(2,1)S(1)} %get-tuple-element.42.after), custom_call_target="tpu_custom_call" | custom-call | tf_op jit(solution)/shard_map/pallas_call | solution.py:476
  3.9 1.2 shard_map.66
  5.1 1.5 %shard_map.67.after = bf16[96,7680]{1,0:T(8,128)(2,1)S(1)} custom-call(bf16[96,8192]{1,0:T(8,128)(2,1)} %q.11, bf16[96,8192]{1,0:T(8,128)(2,1)} %k.11, bf16[96,8192]{1,0:T(8,128)(2,1)} %v.11, bf16[96,1536]{1,0:T(8,128)(2,1)S(1)} %get-tuple-element.44.after), custom_call_target="tpu_custom_call" | custom-call | tf_op jit(solution)/shard_map/pallas_call | solution.py:476
  6.6 0.6 collective-permute-start.13
  7.2 2.6 %collective-permute-start.1 = (bf16[128,768]{1,0:T(8,128)(2,1)S(1)}, bf16[128,768]{1,0:T(8,128)(2,1)S(1)}, u32[]{:S(2)}, u32[]{:S(2)}) collective-permute-start(bf16[128,768]{1,0:T(8,128)(2,1)S(1)} %get-tuple-element.46), channel_id=1, source_target_pairs={{0,4},{4,0},{8,12},{12,8},{1,5},{5,1},{9,13},{13,9},{2,6},{6,2},{1... | collective-permute-start | bytes 589832 | tf_op jit(solution)/shard_map/ppermute | solution.py:491
  9.8 2.7 %collective-permute-start.15 = (bf16[128,1280]{1,0:T(8,128)(2,1)S(1)}, bf16[128,1280]{1,0:T(8,128)(2,1)S(1)}, u32[]{:S(2)}, u32[]{:S(2)}) collective-permute-start(bf16[128,1280]{1,0:T(8,128)(2,1)S(1)} %get-tuple-element.65), channel_id=1, source_target_pairs={{0,8},{4,12},{8,0},{12,4},{1,9},{5,13},{9,1},{13,5},{2,10},{6,14},... | collective-permute-start | bytes 983048 | tf_op jit(solution)/shard_map/ppermute | solution.py:491
  12.6 0.0 collective-permute-start.16
  12.6 0.7 collective-permute-start.14
  13.3 6.3 %collective-permute-done.1.refs_1_ = bf16[128,768]{1,0:T(8,128)(2,1)S(1)} collective-permute-done((bf16[128,768]{1,0:T(8,128)(2,1)S(1)}, bf16[128,768]{1,0:T(8,128)(2,1)S(1)}, u32[]{:S(2)}, u32[]{:S(2)}) %collective-permute-start.1) | collective-permute-done | bytes 196640 | tf_op jit(solution)/shard_map/ppermute | solution.py:491
  19.6 1.3 %collective-permute-start.2 = (bf16[128,768]{1,0:T(8,128)(2,1)S(1)}, bf16[128,768]{1,0:T(8,128)(2,1)S(1)}, u32[]{:S(2)}, u32[]{:S(2)}) collective-permute-start(bf16[128,768]{1,0:T(8,128)(2,1)S(1)} %get-tuple-element.47), channel_id=1, source_target_pairs={{0,8},{4,12},{8,0},{12,4},{1,9},{5,13},{9,1},{13,5},{2,10},{6,14},... | collective-permute-start | bytes 589832 | tf_op jit(solution)/shard_map/ppermute | solution.py:491
  20.9 29.3 %collective-permute-done.2.refs_2_ = bf16[128,768]{1,0:T(8,128)(2,1)S(1)} collective-permute-done((bf16[128,768]{1,0:T(8,128)(2,1)S(1)}, bf16[128,768]{1,0:T(8,128)(2,1)S(1)}, u32[]{:S(2)}, u32[]{:S(2)}) %collective-permute-start.2) | collective-permute-done | bytes 196640 | tf_op jit(solution)/shard_map/ppermute | solution.py:491
  50.2 0.0 collective-permute-start.8
  50.2 1.3 %shard_map.68.after = bf16[96,4608]{1,0:T(8,128)(2,1)S(1)} custom-call(bf16[96,8192]{1,0:T(8,128)(2,1)} %q.11, bf16[96,8192]{1,0:T(8,128)(2,1)} %k.11, bf16[96,8192]{1,0:T(8,128)(2,1)} %v.11, bf16[96,7680]{1,0:T(8,128)(2,1)S(1)} %shard_map.67.after), custom_call_target="tpu_custom_call" | custom-call | tf_op jit(solution)/shard_map/pallas_call | solution.py:476
  51.5 0.0 collective-permute-done.15.refs_2_
  51.5 0.5 collective-permute-start
  52.0 0.0 collective-permute-done.16.refs_3_
  52.0 2.4 %collective-permute-start.3 = (bf16[128,768]{1,0:T(8,128)(2,1)S(1)}, bf16[128,768]{1,0:T(8,128)(2,1)S(1)}, u32[]{:S(2)}, u32[]{:S(2)}) collective-permute-start(bf16[128,768]{1,0:T(8,128)(2,1)S(1)} %get-tuple-element.48), channel_id=1, source_target_pairs={{0,12},{4,8},{8,4},{12,0},{1,13},{5,9},{9,5},{13,1},{2,14},{6,10},... | collective-permute-start | bytes 589832 | tf_op jit(solution)/shard_map/ppermute | solution.py:491
  54.3 0.0 collective-permute-done.14.refs_1_
  54.3 1.7 %collective-permute-start.7 = (bf16[96,2560]{1,0:T(8,128)(2,1)S(1)}, bf16[96,2560]{1,0:T(8,128)(2,1)S(1)}, u32[]{:S(2)}, u32[]{:S(2)}) collective-permute-start(bf16[96,2560]{1,0:T(8,128)(2,1)S(1)} %get-tuple-element.43.after), channel_id=1, source_target_pairs={{0,2},{1,3},{2,0},{3,1},{4,6},{5,7},{6,4},{7,5},{8,10},{9,11},{10,... | collective-permute-start | bytes 1474568 | tf_op jit(solution)/shard_map/ppermute | solution.py:491
  56.1 0.8 shard_map.76.kept
  56.9 3.9 %collective-permute-done.3.refs_3_ = bf16[128,768]{1,0:T(8,128)(2,1)S(1)} collective-permute-done((bf16[128,768]{1,0:T(8,128)(2,1)S(1)}, bf16[128,768]{1,0:T(8,128)(2,1)S(1)}, u32[]{:S(2)}, u32[]{:S(2)}) %collective-permute-start.3) | collective-permute-done | bytes 196640 | tf_op jit(solution)/shard_map/ppermute | solution.py:491
  60.8 1.3 %collective-permute-start.17 = (bf16[256,1280]{1,0:T(8,128)(2,1)S(1)}, bf16[256,1280]{1,0:T(8,128)(2,1)S(1)}, u32[]{:S(2)}, u32[]{:S(2)}) collective-permute-start(bf16[256,1280]{1,0:T(8,128)(2,1)S(1)} %shard_map.76.kept), channel_id=1, source_target_pairs={{2,0},{3,1},{6,4},{7,5},{10,8},{11,9},{14,12},{15,13},{18,16},{19,... | collective-permute-start | bytes 1966088 | tf_op jit(solution)/shard_map/ppermute | solution.py:491
  62.1 1.6 %collective-permute-done.8.q_three.three = bf16[96,2560]{1,0:T(8,128)(2,1)S(1)} collective-permute-done((bf16[96,2560]{1,0:T(8,128)(2,1)S(1)}, bf16[96,2560]{1,0:T(8,128)(2,1)S(1)}, u32[]{:S(2)}, u32[]{:S(2)}) %collective-permute-start.8) | collective-permute-done | bytes 491552 | tf_op jit(solution)/shard_map/ppermute | solution.py:491
  63.7 1.9 %collective-permute-start.6 = (bf16[96,1536]{1,0:T(8,128)(2,1)S(1)}, bf16[96,1536]{1,0:T(8,128)(2,1)S(1)}, u32[]{:S(2)}, u32[]{:S(2)}) collective-permute-start(bf16[96,1536]{1,0:T(8,128)(2,1)S(1)} %get-tuple-element.52), channel_id=1, source_target_pairs={{0,3},{1,2},{4,7},{5,6},{8,11},{9,10},{12,15},{13,14},{16,19},{17,... | collective-permute-start | bytes 884744 | tf_op jit(solution)/shard_map/ppermute | solution.py:491
  65.6 0.8 shard_map.71.kept
  66.4 7.0 %collective-permute-done.7.q_two.two = bf16[96,2560]{1,0:T(8,128)(2,1)S(1)} collective-permute-done((bf16[96,2560]{1,0:T(8,128)(2,1)S(1)}, bf16[96,2560]{1,0:T(8,128)(2,1)S(1)}, u32[]{:S(2)}, u32[]{:S(2)}) %collective-permute-start.7) | collective-permute-done | bytes 491552 | tf_op jit(solution)/shard_map/ppermute | solution.py:491
  73.4 1.3 %collective-permute-start.4 = (bf16[256,768]{1,0:T(8,128)(2,1)S(1)}, bf16[256,768]{1,0:T(8,128)(2,1)S(1)}, u32[]{:S(2)}, u32[]{:S(2)}) collective-permute-start(bf16[256,768]{1,0:T(8,128)(2,1)S(1)} %shard_map.71.kept), channel_id=1, source_target_pairs={{2,0},{3,1},{6,4},{7,5},{10,8},{11,9},{14,12},{15,13},{18,16},{19,... | collective-permute-start | bytes 1179656 | tf_op jit(solution)/shard_map/ppermute | solution.py:491
  74.6 0.0 collective-permute-done.13.par
  74.7 4.6 %collective-permute-start.5 = (bf16[96,1536]{1,0:T(8,128)(2,1)S(1)}, bf16[96,1536]{1,0:T(8,128)(2,1)S(1)}, u32[]{:S(2)}, u32[]{:S(2)}) collective-permute-start(bf16[96,1536]{1,0:T(8,128)(2,1)S(1)} %get-tuple-element.44.after), channel_id=1, source_target_pairs={{0,2},{1,3},{4,6},{5,7},{8,10},{9,11},{12,14},{13,15},{16,18},{17,... | collective-permute-start | bytes 884744 | tf_op jit(solution)/shard_map/ppermute | solution.py:491
  79.2 1.5 %shard_map.69.after.own = bf16[96,7680]{1,0:T(8,128)(2,1)S(1)} custom-call(bf16[96,8192]{1,0:T(8,128)(2,1)} %q.11, bf16[96,8192]{1,0:T(8,128)(2,1)} %k.11, bf16[96,8192]{1,0:T(8,128)(2,1)} %v.11, bf16[96,4608]{1,0:T(8,128)(2,1)S(1)} %shard_map.68.after), custom_call_target="tpu_custom_call" | custom-call | tf_op jit(solution)/shard_map/pallas_call | solution.py:476
  80.8 4.0 %shard_map.77 = (f32[96,1408]{1,0:T(8,128)S(1)}, f32[96,1408]{1,0:T(8,128)S(1)}, f32[96,1408]{1,0:T(8,128)S(1)}, f32[96,1408]{1,0:T(8,128)S(1)}) custom-call(f32[192,256]{1,0:T(8,128)S(1)} %get-tuple-element.49.bias, bf16[96,7680]{1,0:T(8,128)(2,1)S(1)} %shard_map.69.after.own, bf16[96,7680]{1,0:T(8,128)(2,1)S(1)} %collective-permute-done.13.par), custom_call_target="tpu_custom_call" | custom-call | tf_op jit(solution)/shard_map/pallas_call | solution.py:476
  84.7 3.4 %shard_map.78 = (f32[96,1408]{1,0:T(8,128)S(1)}, f32[96,1408]{1,0:T(8,128)S(1)}) custom-call(bf16[96,7680]{1,0:T(8,128)(2,1)S(1)} %shard_map.69.after.own, bf16[96,7680]{1,0:T(8,128)(2,1)S(1)} %collective-permute-done.13.par, bf16[96,2560]{1,0:T(8,128)(2,1)S(1)} %collective-permute-done.7.q_two.two, ...), custom_call_target="tpu_custom_call" | custom-call | tf_op jit(solution)/shard_map/pallas_call | solution.py:476
  88.2 4.6 %shard_map.80 = (f32[96,1408]{1,0:T(8,128)S(1)}, f32[96,1408]{1,0:T(8,128)S(1)}, bf16[96,1408]{1,0:T(8,128)(2,1)S(1)}, bf16[96,1408]{1,0:T(8,128)(2,1)S(1)}) custom-call(bf16[96,7680]{1,0:T(8,128)(2,1)S(1)} %shard_map.69.after.own, bf16[96,7680]{1,0:T(8,128)(2,1)S(1)} %collective-permute-done.13.par, bf16[96,2560]{1,0:T(8,128)(2,1)S(1)} %collective-permute-done.7.q_two.two, ...), custom_call_target="tpu_custom_call" | custom-call | tf_op jit(solution)/shard_map/pallas_call | solution.py:476
  92.8 0.0 collective-permute-done.6.three
  92.8 0.5 collective-permute-start.19
  93.3 0.0 collective-permute-done.17.crossed
  93.3 1.3 %collective-permute-start.20 = (bf16[96,1408]{1,0:T(8,128)(2,1)S(1)}, bf16[96,1408]{1,0:T(8,128)(2,1)S(1)}, u32[]{:S(2)}, u32[]{:S(2)}) collective-permute-start(bf16[96,1408]{1,0:T(8,128)(2,1)S(1)} %get-tuple-element.77), channel_id=1, source_target_pairs={{0,2},{1,3},{4,6},{5,7},{8,10},{9,11},{12,14},{13,15},{16,18},{17,... | collective-permute-start | bytes 811016 | tf_op jit(solution)/shard_map/ppermute | solution.py:491
  94.6 3.1 %shard_map.79 = (bf16[96,1280]{1,0:T(8,128)(2,1)S(1)}, bf16[96,1280]{1,0:T(8,128)(2,1)S(1)}) custom-call(bf16[96,7680]{1,0:T(8,128)(2,1)S(1)} %shard_map.69.after.own, bf16[96,7680]{1,0:T(8,128)(2,1)S(1)} %collective-permute-done.13.par, bf16[256,1280]{1,0:T(8,128)(2,1)S(1)} %shard_map.76.kept, bf16[256,1280]{1,0:T(8,128)(2,1)S(1)} %collective-permute-done.17.crossed, ...), custom_call_target="tpu_custom_call" | custom-call | tf_op jit(solution)/shard_map/pallas_call | solution.py:476
  97.8 0.0 collective-permute-done.5.two
  97.8 0.1 collective-permute-start.18
  97.9 0.0 collective-permute-done.par
  97.9 1.3 %collective-permute-start.21 = (bf16[96,1408]{1,0:T(8,128)(2,1)S(1)}, bf16[96,1408]{1,0:T(8,128)(2,1)S(1)}, u32[]{:S(2)}, u32[]{:S(2)}) collective-permute-start(bf16[96,1408]{1,0:T(8,128)(2,1)S(1)} %get-tuple-element.78), channel_id=1, source_target_pairs={{0,3},{1,2},{4,7},{5,6},{8,11},{9,10},{12,15},{13,14},{16,19},{17,... | collective-permute-start | bytes 811016 | tf_op jit(solution)/shard_map/ppermute | solution.py:491
  99.2 1.3 %shard_map.70.own = bf16[96,4608]{1,0:T(8,128)(2,1)S(1)} custom-call(bf16[96,8192]{1,0:T(8,128)(2,1)} %q.11, bf16[96,8192]{1,0:T(8,128)(2,1)} %k.11, bf16[96,8192]{1,0:T(8,128)(2,1)} %v.11, bf16[96,7680]{1,0:T(8,128)(2,1)S(1)} %shard_map.69.after.own), custom_call_target="tpu_custom_call" | custom-call | tf_op jit(solution)/shard_map/pallas_call | solution.py:476
  100.6 2.4 %shard_map.72 = (f32[96,896]{1,0:T(8,128)S(1)}, f32[96,896]{1,0:T(8,128)S(1)}, f32[96,896]{1,0:T(8,128)S(1)}, f32[96,896]{1,0:T(8,128)S(1)}) custom-call(f32[192,256]{1,0:T(8,128)S(1)} %get-tuple-element.49.bias, bf16[96,4608]{1,0:T(8,128)(2,1)S(1)} %shard_map.70.own, bf16[96,4608]{1,0:T(8,128)(2,1)S(1)} %collective-permute-done.par), custom_call_target="tpu_custom_call" | custom-call | tf_op jit(solution)/shard_map/pallas_call | solution.py:476
  102.9 2.1 %shard_map.73 = (f32[96,896]{1,0:T(8,128)S(1)}, f32[96,896]{1,0:T(8,128)S(1)}) custom-call(bf16[96,4608]{1,0:T(8,128)(2,1)S(1)} %shard_map.70.own, bf16[96,4608]{1,0:T(8,128)(2,1)S(1)} %collective-permute-done.par, bf16[96,1536]{1,0:T(8,128)(2,1)S(1)} %collective-permute-done.5.two, bf16[96,1536]{1,0:T(8,128)(2,1)S(1)} %collective-permute-done.6.three, ...), custom_call_target="tpu_custom_call" | custom-call | tf_op jit(solution)/shard_map/pallas_call | solution.py:476
  105.0 2.8 %shard_map.75 = (f32[96,896]{1,0:T(8,128)S(1)}, f32[96,896]{1,0:T(8,128)S(1)}, bf16[96,896]{1,0:T(8,128)(2,1)S(1)}, bf16[96,896]{1,0:T(8,128)(2,1)S(1)}) custom-call(bf16[96,4608]{1,0:T(8,128)(2,1)S(1)} %shard_map.70.own, bf16[96,4608]{1,0:T(8,128)(2,1)S(1)} %collective-permute-done.par, bf16[96,2560]{1,0:T(8,128)(2,1)S(1)} %collective-permute-done.7.q_two.two, ...), custom_call_target="tpu_custom_call" | custom-call | tf_op jit(solution)/shard_map/pallas_call | solution.py:476
  107.9 0.0 collective-permute-done.4.crossed
  107.9 0.5 collective-permute-start.10
  108.4 0.0 collective-permute-done.18.refs_1_
  108.4 1.3 %collective-permute-start.11 = (bf16[96,896]{1,0:T(8,128)(2,1)S(1)}, bf16[96,896]{1,0:T(8,128)(2,1)S(1)}, u32[]{:S(2)}, u32[]{:S(2)}) collective-permute-start(bf16[96,896]{1,0:T(8,128)(2,1)S(1)} %get-tuple-element.62), channel_id=1, source_target_pairs={{0,2},{1,3},{4,6},{5,7},{8,10},{9,11},{12,14},{13,15},{16,18},{17,... | collective-permute-start | bytes 516104 | tf_op jit(solution)/shard_map/ppermute | solution.py:491
  109.7 0.0 collective-permute-done.20.refs_4_
  109.7 1.3 %collective-permute-start.12 = (bf16[96,896]{1,0:T(8,128)(2,1)S(1)}, bf16[96,896]{1,0:T(8,128)(2,1)S(1)}, u32[]{:S(2)}, u32[]{:S(2)}) collective-permute-start(bf16[96,896]{1,0:T(8,128)(2,1)S(1)} %get-tuple-element.63), channel_id=1, source_target_pairs={{0,3},{1,2},{4,7},{5,6},{8,11},{9,10},{12,15},{13,14},{16,19},{17,... | collective-permute-start | bytes 516104 | tf_op jit(solution)/shard_map/ppermute | solution.py:491
  111.0 1.9 %shard_map.74 = (bf16[96,768]{1,0:T(8,128)(2,1)S(1)}, bf16[96,768]{1,0:T(8,128)(2,1)S(1)}) custom-call(bf16[96,4608]{1,0:T(8,128)(2,1)S(1)} %shard_map.70.own, bf16[96,4608]{1,0:T(8,128)(2,1)S(1)} %collective-permute-done.par, bf16[256,768]{1,0:T(8,128)(2,1)S(1)} %shard_map.71.kept, bf16[256,768]{1,0:T(8,128)(2,1)S(1)} %collective-permute-done.4.crossed, ...), custom_call_target="tpu_custom_call" | custom-call | tf_op jit(solution)/shard_map/pallas_call | solution.py:476
  112.9 0.0 collective-permute-done.21.refs_5_
  112.9 0.1 collective-permute-start.9
  113.0 0.0 collective-permute-done.19.refs_3_
  113.0 1.0 shard_map.81.refs_6_
  114.0 0.3 collective-permute-done.9.refs_1_
  114.3 0.1 collective-permute-done.11.refs_4_
  114.4 3.1 %collective-permute-done.12.refs_5_ = bf16[96,896]{1,0:T(8,128)(2,1)S(1)} collective-permute-done((bf16[96,896]{1,0:T(8,128)(2,1)S(1)}, bf16[96,896]{1,0:T(8,128)(2,1)S(1)}, u32[]{:S(2)}, u32[]{:S(2)}) %collective-permute-start.12) | collective-permute-done | bytes 172064 | tf_op jit(solution)/shard_map/ppermute | solution.py:491
  117.5 0.0 collective-permute-done.10.refs_3_
  117.5 0.8 shard_map.82
Async XLA Ops:
  6.6 68.0 %collective-permute-start.13 = (bf16[96,7680]{1,0:T(8,128)(2,1)S(1)}, bf16[96,7680]{1,0:T(8,128)(2,1)S(1)}, u32[]{:S(2)}, u32[]{:S(2)}) collective-permute-start(bf16[96,7680]{1,0:T(8,128)(2,1)S(1)} %shard_map.67.after), channel_id=1, source_target_pairs={{0,1},{1,0},{2,3},{3,2},{4,5},{5,4},{6,7},{7,6},{8,9},{9,8},{10,11... | collective-permute-start | bytes 4423688 | tf_op jit(solution)/shard_map/ppermute | solution.py:491
  7.2 12.4 %collective-permute-start.1 = (bf16[128,768]{1,0:T(8,128)(2,1)S(1)}, bf16[128,768]{1,0:T(8,128)(2,1)S(1)}, u32[]{:S(2)}, u32[]{:S(2)}) collective-permute-start(bf16[128,768]{1,0:T(8,128)(2,1)S(1)} %get-tuple-element.46), channel_id=1, source_target_pairs={{0,4},{4,0},{8,12},{12,8},{1,5},{5,1},{9,13},{13,9},{2,6},{6,2},{1... | collective-permute-start | bytes 589832 | tf_op jit(solution)/shard_map/ppermute | solution.py:491
  9.8 41.7 %collective-permute-start.15 = (bf16[128,1280]{1,0:T(8,128)(2,1)S(1)}, bf16[128,1280]{1,0:T(8,128)(2,1)S(1)}, u32[]{:S(2)}, u32[]{:S(2)}) collective-permute-start(bf16[128,1280]{1,0:T(8,128)(2,1)S(1)} %get-tuple-element.65), channel_id=1, source_target_pairs={{0,8},{4,12},{8,0},{12,4},{1,9},{5,13},{9,1},{13,5},{2,10},{6,14},... | collective-permute-start | bytes 983048 | tf_op jit(solution)/shard_map/ppermute | solution.py:491
  12.6 39.4 %collective-permute-start.16 = (bf16[128,1280]{1,0:T(8,128)(2,1)S(1)}, bf16[128,1280]{1,0:T(8,128)(2,1)S(1)}, u32[]{:S(2)}, u32[]{:S(2)}) collective-permute-start(bf16[128,1280]{1,0:T(8,128)(2,1)S(1)} %get-tuple-element.66), channel_id=1, source_target_pairs={{0,12},{4,8},{8,4},{12,0},{1,13},{5,9},{9,5},{13,1},{2,14},{6,10},... | collective-permute-start | bytes 983048 | tf_op jit(solution)/shard_map/ppermute | solution.py:491
  12.6 41.8 %collective-permute-start.14 = (bf16[128,1280]{1,0:T(8,128)(2,1)S(1)}, bf16[128,1280]{1,0:T(8,128)(2,1)S(1)}, u32[]{:S(2)}, u32[]{:S(2)}) collective-permute-start(bf16[128,1280]{1,0:T(8,128)(2,1)S(1)} %get-tuple-element.42.after), channel_id=1, source_target_pairs={{0,4},{4,0},{8,12},{12,8},{1,5},{5,1},{9,13},{13,9},{2,6},{6,2},{1... | collective-permute-start | bytes 983048 | tf_op jit(solution)/shard_map/ppermute | solution.py:491
  19.6 30.6 %collective-permute-start.2 = (bf16[128,768]{1,0:T(8,128)(2,1)S(1)}, bf16[128,768]{1,0:T(8,128)(2,1)S(1)}, u32[]{:S(2)}, u32[]{:S(2)}) collective-permute-start(bf16[128,768]{1,0:T(8,128)(2,1)S(1)} %get-tuple-element.47), channel_id=1, source_target_pairs={{0,8},{4,12},{8,0},{12,4},{1,9},{5,13},{9,1},{13,5},{2,10},{6,14},... | collective-permute-start | bytes 589832 | tf_op jit(solution)/shard_map/ppermute | solution.py:491
  50.2 13.5 %collective-permute-start.8 = (bf16[96,2560]{1,0:T(8,128)(2,1)S(1)}, bf16[96,2560]{1,0:T(8,128)(2,1)S(1)}, u32[]{:S(2)}, u32[]{:S(2)}) collective-permute-start(bf16[96,2560]{1,0:T(8,128)(2,1)S(1)} %get-tuple-element.53), channel_id=1, source_target_pairs={{0,3},{1,2},{2,1},{3,0},{4,7},{5,6},{6,5},{7,4},{8,11},{9,10},{10,... | collective-permute-start | bytes 1474568 | tf_op jit(solution)/shard_map/ppermute | solution.py:491
  51.5 46.4 %collective-permute-start = (bf16[96,4608]{1,0:T(8,128)(2,1)S(1)}, bf16[96,4608]{1,0:T(8,128)(2,1)S(1)}, u32[]{:S(2)}, u32[]{:S(2)}) collective-permute-start(bf16[96,4608]{1,0:T(8,128)(2,1)S(1)} %shard_map.68.after), channel_id=1, source_target_pairs={{0,1},{1,0},{2,3},{3,2},{4,5},{5,4},{6,7},{7,6},{8,9},{9,8},{10,11... | collective-permute-start | bytes 2654216 | tf_op jit(solution)/shard_map/ppermute | solution.py:491
  52.0 8.8 %collective-permute-start.3 = (bf16[128,768]{1,0:T(8,128)(2,1)S(1)}, bf16[128,768]{1,0:T(8,128)(2,1)S(1)}, u32[]{:S(2)}, u32[]{:S(2)}) collective-permute-start(bf16[128,768]{1,0:T(8,128)(2,1)S(1)} %get-tuple-element.48), channel_id=1, source_target_pairs={{0,12},{4,8},{8,4},{12,0},{1,13},{5,9},{9,5},{13,1},{2,14},{6,10},... | collective-permute-start | bytes 589832 | tf_op jit(solution)/shard_map/ppermute | solution.py:491
  54.3 19.0 %collective-permute-start.7 = (bf16[96,2560]{1,0:T(8,128)(2,1)S(1)}, bf16[96,2560]{1,0:T(8,128)(2,1)S(1)}, u32[]{:S(2)}, u32[]{:S(2)}) collective-permute-start(bf16[96,2560]{1,0:T(8,128)(2,1)S(1)} %get-tuple-element.43.after), channel_id=1, source_target_pairs={{0,2},{1,3},{2,0},{3,1},{4,6},{5,7},{6,4},{7,5},{8,10},{9,11},{10,... | collective-permute-start | bytes 1474568 | tf_op jit(solution)/shard_map/ppermute | solution.py:491
  60.8 32.6 %collective-permute-start.17 = (bf16[256,1280]{1,0:T(8,128)(2,1)S(1)}, bf16[256,1280]{1,0:T(8,128)(2,1)S(1)}, u32[]{:S(2)}, u32[]{:S(2)}) collective-permute-start(bf16[256,1280]{1,0:T(8,128)(2,1)S(1)} %shard_map.76.kept), channel_id=1, source_target_pairs={{2,0},{3,1},{6,4},{7,5},{10,8},{11,9},{14,12},{15,13},{18,16},{19,... | collective-permute-start | bytes 1966088 | tf_op jit(solution)/shard_map/ppermute | solution.py:491
  63.7 29.1 %collective-permute-start.6 = (bf16[96,1536]{1,0:T(8,128)(2,1)S(1)}, bf16[96,1536]{1,0:T(8,128)(2,1)S(1)}, u32[]{:S(2)}, u32[]{:S(2)}) collective-permute-start(bf16[96,1536]{1,0:T(8,128)(2,1)S(1)} %get-tuple-element.52), channel_id=1, source_target_pairs={{0,3},{1,2},{4,7},{5,6},{8,11},{9,10},{12,15},{13,14},{16,19},{17,... | collective-permute-start | bytes 884744 | tf_op jit(solution)/shard_map/ppermute | solution.py:491
  73.4 34.5 %collective-permute-start.4 = (bf16[256,768]{1,0:T(8,128)(2,1)S(1)}, bf16[256,768]{1,0:T(8,128)(2,1)S(1)}, u32[]{:S(2)}, u32[]{:S(2)}) collective-permute-start(bf16[256,768]{1,0:T(8,128)(2,1)S(1)} %shard_map.71.kept), channel_id=1, source_target_pairs={{2,0},{3,1},{6,4},{7,5},{10,8},{11,9},{14,12},{15,13},{18,16},{19,... | collective-permute-start | bytes 1179656 | tf_op jit(solution)/shard_map/ppermute | solution.py:491
  74.7 23.1 %collective-permute-start.5 = (bf16[96,1536]{1,0:T(8,128)(2,1)S(1)}, bf16[96,1536]{1,0:T(8,128)(2,1)S(1)}, u32[]{:S(2)}, u32[]{:S(2)}) collective-permute-start(bf16[96,1536]{1,0:T(8,128)(2,1)S(1)} %get-tuple-element.44.after), channel_id=1, source_target_pairs={{0,2},{1,3},{4,6},{5,7},{8,10},{9,11},{12,14},{13,15},{16,18},{17,... | collective-permute-start | bytes 884744 | tf_op jit(solution)/shard_map/ppermute | solution.py:491
  92.8 20.2 %collective-permute-start.19 = (f32[96,1408]{1,0:T(8,128)S(1)}, f32[96,1408]{1,0:T(8,128)S(1)}, u32[]{:S(2)}, u32[]{:S(2)}) collective-permute-start(f32[96,1408]{1,0:T(8,128)S(1)} %get-tuple-element.76), channel_id=1, source_target_pairs={{0,1},{1,0},{2,3},{3,2},{4,5},{5,4},{6,7},{7,6},{8,9},{9,8},{10,11... | collective-permute-start | bytes 1622024 | tf_op jit(solution)/shard_map/ppermute | solution.py:491
  93.3 16.3 %collective-permute-start.20 = (bf16[96,1408]{1,0:T(8,128)(2,1)S(1)}, bf16[96,1408]{1,0:T(8,128)(2,1)S(1)}, u32[]{:S(2)}, u32[]{:S(2)}) collective-permute-start(bf16[96,1408]{1,0:T(8,128)(2,1)S(1)} %get-tuple-element.77), channel_id=1, source_target_pairs={{0,2},{1,3},{4,6},{5,7},{8,10},{9,11},{12,14},{13,15},{16,18},{17,... | collective-permute-start | bytes 811016 | tf_op jit(solution)/shard_map/ppermute | solution.py:491
  97.8 10.6 %collective-permute-start.18 = (bf16[96,1280]{1,0:T(8,128)(2,1)S(1)}, bf16[96,1280]{1,0:T(8,128)(2,1)S(1)}, u32[]{:S(2)}, u32[]{:S(2)}) collective-permute-start(bf16[96,1280]{1,0:T(8,128)(2,1)S(1)} %get-tuple-element.72), channel_id=1, source_target_pairs={{0,1},{1,0},{2,3},{3,2},{4,5},{5,4},{6,7},{7,6},{8,9},{9,8},{10,11... | collective-permute-start | bytes 737288 | tf_op jit(solution)/shard_map/ppermute | solution.py:491
  97.9 14.9 %collective-permute-start.21 = (bf16[96,1408]{1,0:T(8,128)(2,1)S(1)}, bf16[96,1408]{1,0:T(8,128)(2,1)S(1)}, u32[]{:S(2)}, u32[]{:S(2)}) collective-permute-start(bf16[96,1408]{1,0:T(8,128)(2,1)S(1)} %get-tuple-element.78), channel_id=1, source_target_pairs={{0,3},{1,2},{4,7},{5,6},{8,11},{9,10},{12,15},{13,14},{16,19},{17,... | collective-permute-start | bytes 811016 | tf_op jit(solution)/shard_map/ppermute | solution.py:491
  107.9 9.6 %collective-permute-start.10 = (f32[96,896]{1,0:T(8,128)S(1)}, f32[96,896]{1,0:T(8,128)S(1)}, u32[]{:S(2)}, u32[]{:S(2)}) collective-permute-start(f32[96,896]{1,0:T(8,128)S(1)} %get-tuple-element.61), channel_id=1, source_target_pairs={{0,1},{1,0},{2,3},{3,2},{4,5},{5,4},{6,7},{7,6},{8,9},{9,8},{10,11... | collective-permute-start | bytes 1032200 | tf_op jit(solution)/shard_map/ppermute | solution.py:491
  108.4 6.0 %collective-permute-start.11 = (bf16[96,896]{1,0:T(8,128)(2,1)S(1)}, bf16[96,896]{1,0:T(8,128)(2,1)S(1)}, u32[]{:S(2)}, u32[]{:S(2)}) collective-permute-start(bf16[96,896]{1,0:T(8,128)(2,1)S(1)} %get-tuple-element.62), channel_id=1, source_target_pairs={{0,2},{1,3},{4,6},{5,7},{8,10},{9,11},{12,14},{13,15},{16,18},{17,... | collective-permute-start | bytes 516104 | tf_op jit(solution)/shard_map/ppermute | solution.py:491
  109.7 7.8 %collective-permute-start.12 = (bf16[96,896]{1,0:T(8,128)(2,1)S(1)}, bf16[96,896]{1,0:T(8,128)(2,1)S(1)}, u32[]{:S(2)}, u32[]{:S(2)}) collective-permute-start(bf16[96,896]{1,0:T(8,128)(2,1)S(1)} %get-tuple-element.63), channel_id=1, source_target_pairs={{0,3},{1,2},{4,7},{5,6},{8,11},{9,10},{12,15},{13,14},{16,19},{17,... | collective-permute-start | bytes 516104 | tf_op jit(solution)/shard_map/ppermute | solution.py:491
  112.9 1.4 %collective-permute-start.9 = (bf16[96,768]{1,0:T(8,128)(2,1)S(1)}, bf16[96,768]{1,0:T(8,128)(2,1)S(1)}, u32[]{:S(2)}, u32[]{:S(2)}) collective-permute-start(bf16[96,768]{1,0:T(8,128)(2,1)S(1)} %get-tuple-element.57), channel_id=1, source_target_pairs={{0,1},{1,0},{2,3},{3,2},{4,5},{5,4},{6,7},{7,6},{8,9},{9,8},{10,11... | collective-permute-start | bytes 442376 | tf_op jit(solution)/shard_map/ppermute | solution.py:491

commit v6 on v5

--- a/solution.py
+++ b/solution.py
@@ -255,14 +255,14 @@
     return jnp.where(lanes == lane, column, into)
 
 
-def column(stat, lane):
-    lanes = lax.broadcasted_iota(jnp.int32, stat.shape, 1)
-    return jnp.sum(jnp.where(lanes == lane, stat, 0.0), axis=1, keepdims=True)
+def spread(x, width):
+    whole, rest = divmod(width, x.shape[1])
+    return jnp.concatenate([x] * whole + ([x[:, :rest]] if rest else []), axis=1)
 
 
 def resume(scores, values, mixed, top, total):
     here = jnp.maximum(jnp.max(scores, axis=1, keepdims=True), top)
-    weights = jnp.exp2(scores - here)
+    weights = jnp.exp2(scores - spread(here, scores.shape[1]))
     carry = jnp.exp2(top - here)
     total = jnp.sum(weights, axis=1, keepdims=True) + total * carry
     more = jnp.dot(weights.astype(jnp.bfloat16), values, preferred_element_type=jnp.float32)
@@ -270,8 +270,8 @@
 
 
 class Rows:
-    def __init__(self, size, first, second):
-        self.size, self.refs, self.rows = size, (first, second), first.shape[0]
+    def __init__(self, size, first, second, wide=None):
+        self.size, self.refs, self.rows, self.wide = size, (first, second), first.shape[0], wide
 
     def clear(self):
         for ref in self.refs:
@@ -281,23 +281,32 @@
         for i, ref in enumerate(self.refs):
             ref[:, col] = mixed[i * self.rows : (i + 1) * self.rows].astype(ref.dtype)
 
-    def put_stat(self, head, top, total):
+    def put_lanes(self, stats):
         for i, ref in enumerate(self.refs):
             at = slice(i * self.rows, (i + 1) * self.rows)
-            stat = lane_put(ref[:, self.size :], 2 * head, top[at])
-            ref[:, self.size :] = lane_put(stat, 2 * head + 1, total[at])
+            lanes = ref[:, self.size :]
+            for head, top, total in stats:
+                lanes = lane_put(lane_put(lanes, 2 * head, top[at]), 2 * head + 1, total[at])
+            ref[:, self.size :] = lanes
+
+    def put_wide(self, head, top, total):
+        shape = (2 * self.rows, HD)
+        self.wide[2 * head] = jnp.broadcast_to(top, shape)
+        self.wide[2 * head + 1] = jnp.broadcast_to(total, shape)
 
     def get(self, col, head):
         mixed = jnp.concatenate([ref[:, col] for ref in self.refs], axis=0)
-        stat = jnp.concatenate([ref[:, self.size :] for ref in self.refs], axis=0)
-        return mixed, column(stat, 2 * head), column(stat, 2 * head + 1)
-
-
-def each_head(per, size, work):
+        return mixed, self.wide[2 * head], self.wide[2 * head + 1]
+
+
+def each_head(per, size, work, after=None):
     def step(h, carry):
+        stats = []
         for j in range(per):
             head = h * per + j
-            work(head, pl.ds(pl.multiple_of(head * HD, HD), HD))
+            stats.append(work(head, pl.ds(pl.multiple_of(head * HD, HD), HD)))
+        if after is not None:
+            after(stats)
         return carry
 
     lax.fori_loop(0, size // HD // per, step, 0)
@@ -312,28 +321,29 @@
     return jnp.concatenate(part_of(refs, size, t, head), axis=0)
 
 
-def span_kernel(per, size, factor, bias, own, par, a0, a1, b0, b1):
+def span_kernel(per, size, factor, bias, own, par, a0, a1, aw, b0, b1, bw):
     def work(head, col):
         for base, rows in ((0, first), (3, second)):
             k, v = (rows_of((own, par), size, base + t, head) for t in (1, 2))
             scores = logits(rows_of((own, par), size, base, head), k, factor)
             mixed, top, total = soft(biased(scores, 0, bias), v)
             rows.put(col, mixed)
-            rows.put_stat(head, top, total)
-
-    first, second = Rows(size, a0, a1), Rows(size, b0, b1)
+            rows.put_wide(head, top, total)
+            if base == 0:
+                stat = (head, top, total)
+        return stat
+
+    first, second = Rows(size, a0, a1, aw), Rows(size, b0, b1, bw)
     first.clear()
-    second.clear()
-    each_head(per, size, work)
-
-
-def other_kernel(per, size, asked_at, factor, own, par, two, three, q_two, q_three, b0, b1, s0, s1):
-    second, result = Rows(size, b0, b1), Rows(size, s0, s1)
-    result.clear()
+    each_head(per, size, work, first.put_lanes)
+
+
+def other_kernel(per, size, asked_at, factor, own, par, two, three, q_two, q_three, b0, b1, bw, s0, s1, sw):
+    second, result = Rows(size, b0, b1, bw), Rows(size, s0, s1, sw)
 
     def keep(head, col, mixed, top, total):
         result.put(col, mixed)
-        result.put_stat(head, top, total)
+        result.put_wide(head, top, total)
 
     def on_first(head, col):
         k, v = (rows_of((own, par), size, t, head) for t in (1, 2))
@@ -354,9 +364,11 @@
         each_head(per, size, on_second)
 
 
-def early_kernel(per, size, asked_at, factor, own, par, q_two, q_three, kept, a0, a1, p0, p1, loc0, loc1, part0, part1):
+def early_kernel(
+    per, size, asked_at, factor, own, par, q_two, q_three, kept, a0, a1, aw, s0, s1, sw, loc0, loc1, part0, part1
+):
     heads = size // HD
-    first, partial = Rows(size, a0, a1), Rows(size, p0, p1)
+    first, partial = Rows(size, a0, a1, aw), Rows(size, s0, s1, sw)
     loc, part = Rows(size, loc0, loc1), Rows(size, part0, part1)
 
     def on_first(head, col):
@@ -367,12 +379,12 @@
         scores = logits(rows_of((q_two, q_three), asked_at, 1, head), k, factor)
         mixed, top, total = resume(scores, v, *partial.get(col, head))
         part.put(col, mixed * (1.0 / total))
-        loc.put_stat(head, top, total)
+        return head, top, total
 
     @pl.when(lax.axis_index("head") == 0)
     def _():
         loc.clear()
-        each_head(per, size, on_first)
+        each_head(per, size, on_first, loc.put_lanes)
         for source, into in zip(loc.refs, part.refs):
             left = source[:, size:]
             packed = jnp.zeros_like(left)
@@ -388,7 +400,7 @@
             into[...] = source[...]
 
 
-def late_kernel(per, size, factor, own, par, kept, crossed, b0, b1, s0, s1, out0, out1):
+def late_kernel(per, size, factor, own, par, kept, crossed, b0, b1, bw, s0, s1, sw, out0, out1):
     out = Rows(size, out0, out1)
 
     def run(cache, second):
@@ -401,11 +413,11 @@
 
     @pl.when(lax.axis_index("head") == 0)
     def _():
-        run(crossed, Rows(size, b0, b1))
+        run(crossed, Rows(size, b0, b1, bw))
 
     @pl.when(lax.axis_index("head") == 1)
     def _():
-        run(kept, Rows(size, s0, s1))
+        run(kept, Rows(size, s0, s1, sw))
 
 
 def finish_kernel(width, start, size, count, *refs):
@@ -549,20 +561,22 @@
     result = None
     for i, (start, size) in enumerate(chunks):
         kept, crossed = fetch(i)
-        per = 2 if size // HD % 2 == 0 else 1
+        per = max(p for p in (5, 3, 2, 1) if size // HD % p == 0)
         both = [own[i], par[i]]
         held_f32, held_bf16 = ((rows, size + HD), f32), ((rows, size + HD), bf16)
-        a0, a1, b0, b1 = call(
+        plain = ((rows, size), f32)
+        wide = ((2 * size // HD, 2 * rows, HD), f32)
+        a0, a1, aw, b0, b1, bw = call(
             functools.partial(span_kernel, per, size, factor), [bias] + both,
-            [resident] * 3, [held_f32] * 4,
-        )
-        s0, s1 = call(
+            [resident] * 3, [held_f32] * 2 + [wide] + [plain] * 2 + [wide],
+        )
+        s0, s1, sw = call(
             functools.partial(other_kernel, per, size, start, factor),
-            both + crossing[i] + crossing[0] + [b0, b1], [resident] * 8, [held_f32] * 2,
+            both + crossing[i] + crossing[0] + [b0, b1, bw], [resident] * 9, [plain] * 2 + [wide],
         )
         loc0, loc1, part0, part1 = call(
             functools.partial(early_kernel, per, size, start, factor),
-            both + crossing[0] + [kept, a0, a1, s0, s1], [resident] * 9,
+            both + crossing[0] + [kept, a0, a1, aw, s0, s1, sw], [resident] * 11,
             [held_f32] * 2 + [held_bf16] * 2,
         )
         far0 = move(part0, apart(2, (0, 1)))
@@ -570,7 +584,7 @@
         got_loc = move(loc1, apart(1))
         out0, out1 = call(
             functools.partial(late_kernel, per, size, factor),
-            both + [kept, crossed, b0, b1, s0, s1], [resident] * 8, [((rows, size), bf16)] * 2,
+            both + [kept, crossed, b0, b1, bw, s0, s1, sw], [resident] * 10, [((rows, size), bf16)] * 2,
         )
         got = move(out1, apart(1))
         pieces = [out0, got, loc0, got_loc, far0, far1]

time: 119 us -> 114 us (0.958)
  Pallas kernels: 38.4 us -> 32.6 us
    pallas_call x19, Pallas kernels: 38.4 us -> 32.6 us  [call(): pl.pallas_call(kernel, out_shape=[pltpu.VMEM(*s) for s in shapes] if resu...]
  transfers between devices with their start and end apart: 22 -> 22, of which waited for: 8 -> 8; matrix products, arithmetic and copies ran while one was open for 0% -> 0% of each run, Pallas kernels for 26% -> 22%
where the time goes in v6:
time: 114 us; the launch traced here: 113 us
  waiting for transfers between devices  52.1 us (46%)
  Pallas kernels  32.6 us (29%)
  starting transfers between devices  28.1 us (25%)
    ppermute x22, waiting for transfers between devices, move(): return lax.ppermute(x, axes, list(pairs))  52.1 us
    pallas_call x19, Pallas kernels, call(): pl.pallas_call(kernel, out_shape=[pltpu.VMEM(*s) for s in shapes] if resu...  32.6 us
    ppermute x22, starting transfers between devices, move(): return lax.ppermute(x, axes, list(pairs))  28.1 us
  transfers between devices with their start and end apart: 22, of which 8 were waited for; matrix products, arithmetic and copies ran while one was open for 0% of the time, Pallas kernels for 22%

profile of v6, /device:TPU:0, one launch (start us, length us, event | category | flops | bytes accessed | tf_op | source)
XLA Modules:
  0.0 113.1 jit_solution(9773684531657876289)
XLA Ops:
  0.0 2.5 %shard_map.64 = (bf16[128,1280]{1,0:T(8,128)(2,1)S(1)}, bf16[128,1280]{1,0:T(8,128)(2,1)S(1)}, bf16[128,1280]{1,0:T(8,128)(2,1)S(1)}, bf16[128,1280]{1,0:T(8,128...) custom-call(s32[2,4]{1,0:T(2,128)} %bitcast.1, ...), custom_call_target="tpu_custom_call" | custom-call | tf_op jit(solution)/shard_map/pallas_call | solution.py:488
  2.6 1.4 %shard_map.65 = (bf16[96,2560]{1,0:T(8,128)(2,1)S(1)}, bf16[96,2560]{1,0:T(8,128)(2,1)S(1)}) custom-call(bf16[96,8192]{1,0:T(8,128)(2,1)} %q.11, bf16[96,8192]{1,0:T(8,128)(2,1)} %k.11, bf16[96,8192]{1,0:T(8,128)(2,1)} %v.11, bf16[128,1280]{1,0:T(8,128)(2,1)S(1)} %get-tuple-element.48.after), custom_call_target="tpu_custom_call" | custom-call | tf_op jit(solution)/shard_map/pallas_call | solution.py:488
  3.9 1.2 %shard_map.66 = (bf16[96,1536]{1,0:T(8,128)(2,1)S(1)}, bf16[96,1536]{1,0:T(8,128)(2,1)S(1)}) custom-call(bf16[96,8192]{1,0:T(8,128)(2,1)} %q.11, bf16[96,8192]{1,0:T(8,128)(2,1)} %k.11, bf16[96,8192]{1,0:T(8,128)(2,1)} %v.11, bf16[96,2560]{1,0:T(8,128)(2,1)S(1)} %get-tuple-element.49.after), custom_call_target="tpu_custom_call" | custom-call | tf_op jit(solution)/shard_map/pallas_call | solution.py:488
  5.1 1.5 %shard_map.67.after = bf16[96,7680]{1,0:T(8,128)(2,1)S(1)} custom-call(bf16[96,8192]{1,0:T(8,128)(2,1)} %q.11, bf16[96,8192]{1,0:T(8,128)(2,1)} %k.11, bf16[96,8192]{1,0:T(8,128)(2,1)} %v.11, bf16[96,1536]{1,0:T(8,128)(2,1)S(1)} %get-tuple-element.50.after), custom_call_target="tpu_custom_call" | custom-call | tf_op jit(solution)/shard_map/pallas_call | solution.py:488
  6.6 0.6 collective-permute-start.13
  7.2 2.6 %collective-permute-start.1 = (bf16[128,768]{1,0:T(8,128)(2,1)S(1)}, bf16[128,768]{1,0:T(8,128)(2,1)S(1)}, u32[]{:S(2)}, u32[]{:S(2)}) collective-permute-start(bf16[128,768]{1,0:T(8,128)(2,1)S(1)} %get-tuple-element.52), channel_id=1, source_target_pairs={{0,4},{4,0},{8,12},{12,8},{1,5},{5,1},{9,13},{13,9},{2,6},{6,2},{1... | collective-permute-start | bytes 589832 | tf_op jit(solution)/shard_map/ppermute | solution.py:503
  9.8 2.7 %collective-permute-start.15 = (bf16[128,1280]{1,0:T(8,128)(2,1)S(1)}, bf16[128,1280]{1,0:T(8,128)(2,1)S(1)}, u32[]{:S(2)}, u32[]{:S(2)}) collective-permute-start(bf16[128,1280]{1,0:T(8,128)(2,1)S(1)} %get-tuple-element.74), channel_id=1, source_target_pairs={{0,8},{4,12},{8,0},{12,4},{1,9},{5,13},{9,1},{13,5},{2,10},{6,14},... | collective-permute-start | bytes 983048 | tf_op jit(solution)/shard_map/ppermute | solution.py:503
  12.6 0.0 collective-permute-start.16
  12.6 0.7 collective-permute-start.14
  13.3 6.3 %collective-permute-done.1.refs_1_ = bf16[128,768]{1,0:T(8,128)(2,1)S(1)} collective-permute-done((bf16[128,768]{1,0:T(8,128)(2,1)S(1)}, bf16[128,768]{1,0:T(8,128)(2,1)S(1)}, u32[]{:S(2)}, u32[]{:S(2)}) %collective-permute-start.1) | collective-permute-done | bytes 196640 | tf_op jit(solution)/shard_map/ppermute | solution.py:503
  19.6 1.3 %collective-permute-start.2 = (bf16[128,768]{1,0:T(8,128)(2,1)S(1)}, bf16[128,768]{1,0:T(8,128)(2,1)S(1)}, u32[]{:S(2)}, u32[]{:S(2)}) collective-permute-start(bf16[128,768]{1,0:T(8,128)(2,1)S(1)} %get-tuple-element.53), channel_id=1, source_target_pairs={{0,8},{4,12},{8,0},{12,4},{1,9},{5,13},{9,1},{13,5},{2,10},{6,14},... | collective-permute-start | bytes 589832 | tf_op jit(solution)/shard_map/ppermute | solution.py:503
  20.9 29.3 %collective-permute-done.2.refs_2_ = bf16[128,768]{1,0:T(8,128)(2,1)S(1)} collective-permute-done((bf16[128,768]{1,0:T(8,128)(2,1)S(1)}, bf16[128,768]{1,0:T(8,128)(2,1)S(1)}, u32[]{:S(2)}, u32[]{:S(2)}) %collective-permute-start.2) | collective-permute-done | bytes 196640 | tf_op jit(solution)/shard_map/ppermute | solution.py:503
  50.2 0.0 collective-permute-start.8
  50.2 1.3 %shard_map.68.after = bf16[96,4608]{1,0:T(8,128)(2,1)S(1)} custom-call(bf16[96,8192]{1,0:T(8,128)(2,1)} %q.11, bf16[96,8192]{1,0:T(8,128)(2,1)} %k.11, bf16[96,8192]{1,0:T(8,128)(2,1)} %v.11, bf16[96,7680]{1,0:T(8,128)(2,1)S(1)} %shard_map.67.after), custom_call_target="tpu_custom_call" | custom-call | tf_op jit(solution)/shard_map/pallas_call | solution.py:488
  51.5 0.0 collective-permute-done.15.refs_2_
  51.5 0.5 collective-permute-start
  52.0 0.0 collective-permute-done.16.refs_3_
  52.0 2.4 %collective-permute-start.3 = (bf16[128,768]{1,0:T(8,128)(2,1)S(1)}, bf16[128,768]{1,0:T(8,128)(2,1)S(1)}, u32[]{:S(2)}, u32[]{:S(2)}) collective-permute-start(bf16[128,768]{1,0:T(8,128)(2,1)S(1)} %get-tuple-element.54), channel_id=1, source_target_pairs={{0,12},{4,8},{8,4},{12,0},{1,13},{5,9},{9,5},{13,1},{2,14},{6,10},... | collective-permute-start | bytes 589832 | tf_op jit(solution)/shard_map/ppermute | solution.py:503
  54.3 0.0 collective-permute-done.14.refs_1_
  54.3 1.7 %collective-permute-start.7 = (bf16[96,2560]{1,0:T(8,128)(2,1)S(1)}, bf16[96,2560]{1,0:T(8,128)(2,1)S(1)}, u32[]{:S(2)}, u32[]{:S(2)}) collective-permute-start(bf16[96,2560]{1,0:T(8,128)(2,1)S(1)} %get-tuple-element.49.after), channel_id=1, source_target_pairs={{0,2},{1,3},{2,0},{3,1},{4,6},{5,7},{6,4},{7,5},{8,10},{9,11},{10,... | collective-permute-start | bytes 1474568 | tf_op jit(solution)/shard_map/ppermute | solution.py:503
  56.1 0.8 shard_map.76.kept
  56.9 3.9 %collective-permute-done.3.refs_3_ = bf16[128,768]{1,0:T(8,128)(2,1)S(1)} collective-permute-done((bf16[128,768]{1,0:T(8,128)(2,1)S(1)}, bf16[128,768]{1,0:T(8,128)(2,1)S(1)}, u32[]{:S(2)}, u32[]{:S(2)}) %collective-permute-start.3) | collective-permute-done | bytes 196640 | tf_op jit(solution)/shard_map/ppermute | solution.py:503
  60.8 1.3 %collective-permute-start.17 = (bf16[256,1280]{1,0:T(8,128)(2,1)S(1)}, bf16[256,1280]{1,0:T(8,128)(2,1)S(1)}, u32[]{:S(2)}, u32[]{:S(2)}) collective-permute-start(bf16[256,1280]{1,0:T(8,128)(2,1)S(1)} %shard_map.76.kept), channel_id=1, source_target_pairs={{2,0},{3,1},{6,4},{7,5},{10,8},{11,9},{14,12},{15,13},{18,16},{19,... | collective-permute-start | bytes 1966088 | tf_op jit(solution)/shard_map/ppermute | solution.py:503
  62.1 1.6 %collective-permute-done.8.q_three.three = bf16[96,2560]{1,0:T(8,128)(2,1)S(1)} collective-permute-done((bf16[96,2560]{1,0:T(8,128)(2,1)S(1)}, bf16[96,2560]{1,0:T(8,128)(2,1)S(1)}, u32[]{:S(2)}, u32[]{:S(2)}) %collective-permute-start.8) | collective-permute-done | bytes 491552 | tf_op jit(solution)/shard_map/ppermute | solution.py:503
  63.7 1.9 %collective-permute-start.6 = (bf16[96,1536]{1,0:T(8,128)(2,1)S(1)}, bf16[96,1536]{1,0:T(8,128)(2,1)S(1)}, u32[]{:S(2)}, u32[]{:S(2)}) collective-permute-start(bf16[96,1536]{1,0:T(8,128)(2,1)S(1)} %get-tuple-element.59), channel_id=1, source_target_pairs={{0,3},{1,2},{4,7},{5,6},{8,11},{9,10},{12,15},{13,14},{16,19},{17,... | collective-permute-start | bytes 884744 | tf_op jit(solution)/shard_map/ppermute | solution.py:503
  65.6 0.8 shard_map.71.kept
  66.4 7.0 %collective-permute-done.7.q_two.two = bf16[96,2560]{1,0:T(8,128)(2,1)S(1)} collective-permute-done((bf16[96,2560]{1,0:T(8,128)(2,1)S(1)}, bf16[96,2560]{1,0:T(8,128)(2,1)S(1)}, u32[]{:S(2)}, u32[]{:S(2)}) %collective-permute-start.7) | collective-permute-done | bytes 491552 | tf_op jit(solution)/shard_map/ppermute | solution.py:503
  73.4 1.3 %collective-permute-start.4 = (bf16[256,768]{1,0:T(8,128)(2,1)S(1)}, bf16[256,768]{1,0:T(8,128)(2,1)S(1)}, u32[]{:S(2)}, u32[]{:S(2)}) collective-permute-start(bf16[256,768]{1,0:T(8,128)(2,1)S(1)} %shard_map.71.kept), channel_id=1, source_target_pairs={{2,0},{3,1},{6,4},{7,5},{10,8},{11,9},{14,12},{15,13},{18,16},{19,... | collective-permute-start | bytes 1179656 | tf_op jit(solution)/shard_map/ppermute | solution.py:503
  74.6 0.0 collective-permute-done.13.par
  74.7 4.6 %collective-permute-start.5 = (bf16[96,1536]{1,0:T(8,128)(2,1)S(1)}, bf16[96,1536]{1,0:T(8,128)(2,1)S(1)}, u32[]{:S(2)}, u32[]{:S(2)}) collective-permute-start(bf16[96,1536]{1,0:T(8,128)(2,1)S(1)} %get-tuple-element.50.after), channel_id=1, source_target_pairs={{0,2},{1,3},{4,6},{5,7},{8,10},{9,11},{12,14},{13,15},{16,18},{17,... | collective-permute-start | bytes 884744 | tf_op jit(solution)/shard_map/ppermute | solution.py:503
  79.2 1.5 %shard_map.69.after.own = bf16[96,7680]{1,0:T(8,128)(2,1)S(1)} custom-call(bf16[96,8192]{1,0:T(8,128)(2,1)} %q.11, bf16[96,8192]{1,0:T(8,128)(2,1)} %k.11, bf16[96,8192]{1,0:T(8,128)(2,1)} %v.11, bf16[96,4608]{1,0:T(8,128)(2,1)S(1)} %shard_map.68.after), custom_call_target="tpu_custom_call" | custom-call | tf_op jit(solution)/shard_map/pallas_call | solution.py:488
  80.8 2.2 %shard_map.77 = (f32[96,1408]{1,0:T(8,128)S(1)}, f32[96,1408]{1,0:T(8,128)S(1)}, f32[20,192,128]{2,1,0:T(8,128)S(1)}, f32[96,1280]{1,0:T(8,128)S(1)}, f32[96,128...) custom-call(f32[192,256]{1,0:T(8,128)S(1)} %get-tuple-element.55.bias, bf16[96,7680]{1,0:T(8,128)(2,1)S(1)} %shard_map.69.after.own, ...), custom_call_target="tpu_custom_call" | custom-call | tf_op jit(solution)/shard_map/pallas_call | solution.py:488
  83.0 1.7 %shard_map.78 = (f32[96,1280]{1,0:T(8,128)S(1)}, f32[96,1280]{1,0:T(8,128)S(1)}, f32[20,192,128]{2,1,0:T(8,128)S(1)}) custom-call(bf16[96,7680]{1,0:T(8,128)(2,1)S(1)} %shard_map.69.after.own, bf16[96,7680]{1,0:T(8,128)(2,1)S(1)} %collective-permute-done.13.par, bf16[96,2560]{1,0:T(8,128)(2,1)S(1)} %collective-permute-done.7.q_two.two, ...), custom_call_target="tpu_custom_call" | custom-call | tf_op jit(solution)/shard_map/pallas_call | solution.py:488
  84.7 4.8 %shard_map.80 = (f32[96,1408]{1,0:T(8,128)S(1)}, f32[96,1408]{1,0:T(8,128)S(1)}, bf16[96,1408]{1,0:T(8,128)(2,1)S(1)}, bf16[96,1408]{1,0:T(8,128)(2,1)S(1)}) custom-call(bf16[96,7680]{1,0:T(8,128)(2,1)S(1)} %shard_map.69.after.own, bf16[96,7680]{1,0:T(8,128)(2,1)S(1)} %collective-permute-done.13.par, bf16[96,2560]{1,0:T(8,128)(2,1)S(1)} %collective-permute-done.7.q_two.two, ...), custom_call_target="tpu_custom_call" | custom-call | tf_op jit(solution)/shard_map/pallas_call | solution.py:488
  89.6 0.0 collective-permute-done.6.three
  89.6 0.5 collective-permute-start.19
  90.1 0.0 collective-permute-done.17.crossed
  90.1 1.3 %collective-permute-start.20 = (bf16[96,1408]{1,0:T(8,128)(2,1)S(1)}, bf16[96,1408]{1,0:T(8,128)(2,1)S(1)}, u32[]{:S(2)}, u32[]{:S(2)}) collective-permute-start(bf16[96,1408]{1,0:T(8,128)(2,1)S(1)} %get-tuple-element.89), channel_id=1, source_target_pairs={{0,2},{1,3},{4,6},{5,7},{8,10},{9,11},{12,14},{13,15},{16,18},{17,... | collective-permute-start | bytes 811016 | tf_op jit(solution)/shard_map/ppermute | solution.py:503
  91.4 2.3 %shard_map.79 = (bf16[96,1280]{1,0:T(8,128)(2,1)S(1)}, bf16[96,1280]{1,0:T(8,128)(2,1)S(1)}) custom-call(bf16[96,7680]{1,0:T(8,128)(2,1)S(1)} %shard_map.69.after.own, bf16[96,7680]{1,0:T(8,128)(2,1)S(1)} %collective-permute-done.13.par, bf16[256,1280]{1,0:T(8,128)(2,1)S(1)} %shard_map.76.kept, bf16[256,1280]{1,0:T(8,128)(2,1)S(1)} %collective-permute-done.17.crossed, ...), custom_call_target="tpu_custom_call" | custom-call | tf_op jit(solution)/shard_map/pallas_call | solution.py:488
  93.7 0.0 collective-permute-done.5.two
  93.7 0.1 collective-permute-start.18
  93.8 0.0 collective-permute-done.par
  93.8 1.3 %collective-permute-start.21 = (bf16[96,1408]{1,0:T(8,128)(2,1)S(1)}, bf16[96,1408]{1,0:T(8,128)(2,1)S(1)}, u32[]{:S(2)}, u32[]{:S(2)}) collective-permute-start(bf16[96,1408]{1,0:T(8,128)(2,1)S(1)} %get-tuple-element.90), channel_id=1, source_target_pairs={{0,3},{1,2},{4,7},{5,6},{8,11},{9,10},{12,15},{13,14},{16,19},{17,... | collective-permute-start | bytes 811016 | tf_op jit(solution)/shard_map/ppermute | solution.py:503
  95.1 1.3 %shard_map.70.own = bf16[96,4608]{1,0:T(8,128)(2,1)S(1)} custom-call(bf16[96,8192]{1,0:T(8,128)(2,1)} %q.11, bf16[96,8192]{1,0:T(8,128)(2,1)} %k.11, bf16[96,8192]{1,0:T(8,128)(2,1)} %v.11, bf16[96,7680]{1,0:T(8,128)(2,1)S(1)} %shard_map.69.after.own), custom_call_target="tpu_custom_call" | custom-call | tf_op jit(solution)/shard_map/pallas_call | solution.py:488
  96.5 1.8 %shard_map.72 = (f32[96,896]{1,0:T(8,128)S(1)}, f32[96,896]{1,0:T(8,128)S(1)}, f32[12,192,128]{2,1,0:T(8,128)S(1)}, f32[96,768]{1,0:T(8,128)S(1)}, f32[96,768]{1,0:T(8,128)S(1)}, /*index=5*/f32[12,192,128]{2,1,0:T(8,128)S(1)}) custom-call(f32[192,256]{1,0:T(8,128)S(1)} %get-tuple-element.55.bias, bf16[96,4608]{1,0:T(8,128)(2,1)S(1)} %shard_map.70.own, ...), custom_call_target="tpu_custom_call" | custom-call | tf_op jit(solution)/shard_map/pallas_call | solution.py:488
  98.3 1.5 %shard_map.73 = (f32[96,768]{1,0:T(8,128)S(1)}, f32[96,768]{1,0:T(8,128)S(1)}, f32[12,192,128]{2,1,0:T(8,128)S(1)}) custom-call(bf16[96,4608]{1,0:T(8,128)(2,1)S(1)} %shard_map.70.own, bf16[96,4608]{1,0:T(8,128)(2,1)S(1)} %collective-permute-done.par, bf16[96,1536]{1,0:T(8,128)(2,1)S(1)} %collective-permute-done.5.two, ...), custom_call_target="tpu_custom_call" | custom-call | tf_op jit(solution)/shard_map/pallas_call | solution.py:488
  99.7 2.9 %shard_map.75 = (f32[96,896]{1,0:T(8,128)S(1)}, f32[96,896]{1,0:T(8,128)S(1)}, bf16[96,896]{1,0:T(8,128)(2,1)S(1)}, bf16[96,896]{1,0:T(8,128)(2,1)S(1)}) custom-call(bf16[96,4608]{1,0:T(8,128)(2,1)S(1)} %shard_map.70.own, bf16[96,4608]{1,0:T(8,128)(2,1)S(1)} %collective-permute-done.par, bf16[96,2560]{1,0:T(8,128)(2,1)S(1)} %collective-permute-done.7.q_two.two, ...), custom_call_target="tpu_custom_call" | custom-call | tf_op jit(solution)/shard_map/pallas_call | solution.py:488
  102.6 0.0 collective-permute-done.4.crossed
  102.7 0.5 collective-permute-start.10
  103.1 0.0 collective-permute-done.18.refs_1_
  103.2 1.3 %collective-permute-start.11 = (bf16[96,896]{1,0:T(8,128)(2,1)S(1)}, bf16[96,896]{1,0:T(8,128)(2,1)S(1)}, u32[]{:S(2)}, u32[]{:S(2)}) collective-permute-start(bf16[96,896]{1,0:T(8,128)(2,1)S(1)} %get-tuple-element.71), channel_id=1, source_target_pairs={{0,2},{1,3},{4,6},{5,7},{8,10},{9,11},{12,14},{13,15},{16,18},{17,... | collective-permute-start | bytes 516104 | tf_op jit(solution)/shard_map/ppermute | solution.py:503
  104.4 0.0 collective-permute-done.20.refs_4_
  104.5 1.3 %collective-permute-start.12 = (bf16[96,896]{1,0:T(8,128)(2,1)S(1)}, bf16[96,896]{1,0:T(8,128)(2,1)S(1)}, u32[]{:S(2)}, u32[]{:S(2)}) collective-permute-start(bf16[96,896]{1,0:T(8,128)(2,1)S(1)} %get-tuple-element.72), channel_id=1, source_target_pairs={{0,3},{1,2},{4,7},{5,6},{8,11},{9,10},{12,15},{13,14},{16,19},{17,... | collective-permute-start | bytes 516104 | tf_op jit(solution)/shard_map/ppermute | solution.py:503
  105.8 1.3 %shard_map.74 = (bf16[96,768]{1,0:T(8,128)(2,1)S(1)}, bf16[96,768]{1,0:T(8,128)(2,1)S(1)}) custom-call(bf16[96,4608]{1,0:T(8,128)(2,1)S(1)} %shard_map.70.own, bf16[96,4608]{1,0:T(8,128)(2,1)S(1)} %collective-permute-done.par, bf16[256,768]{1,0:T(8,128)(2,1)S(1)} %shard_map.71.kept, bf16[256,768]{1,0:T(8,128)(2,1)S(1)} %collective-permute-done.4.crossed, ...), custom_call_target="tpu_custom_call" | custom-call | tf_op jit(solution)/shard_map/pallas_call | solution.py:488
  107.1 0.0 collective-permute-done.21.refs_5_
  107.1 0.2 collective-permute-start.9
  107.3 0.0 collective-permute-done.19.refs_3_
  107.3 1.0 shard_map.81.refs_6_
  108.2 0.3 collective-permute-done.9.refs_1_
  108.6 0.6 collective-permute-done.11.refs_4_
  109.2 3.1 %collective-permute-done.12.refs_5_ = bf16[96,896]{1,0:T(8,128)(2,1)S(1)} collective-permute-done((bf16[96,896]{1,0:T(8,128)(2,1)S(1)}, bf16[96,896]{1,0:T(8,128)(2,1)S(1)}, u32[]{:S(2)}, u32[]{:S(2)}) %collective-permute-start.12) | collective-permute-done | bytes 172064 | tf_op jit(solution)/shard_map/ppermute | solution.py:503
  112.3 0.0 collective-permute-done.10.refs_3_
  112.3 0.8 shard_map.82
Async XLA Ops:
  6.6 68.0 %collective-permute-start.13 = (bf16[96,7680]{1,0:T(8,128)(2,1)S(1)}, bf16[96,7680]{1,0:T(8,128)(2,1)S(1)}, u32[]{:S(2)}, u32[]{:S(2)}) collective-permute-start(bf16[96,7680]{1,0:T(8,128)(2,1)S(1)} %shard_map.67.after), channel_id=1, source_target_pairs={{0,1},{1,0},{2,3},{3,2},{4,5},{5,4},{6,7},{7,6},{8,9},{9,8},{10,11... | collective-permute-start | bytes 4423688 | tf_op jit(solution)/shard_map/ppermute | solution.py:503
  7.2 12.4 %collective-permute-start.1 = (bf16[128,768]{1,0:T(8,128)(2,1)S(1)}, bf16[128,768]{1,0:T(8,128)(2,1)S(1)}, u32[]{:S(2)}, u32[]{:S(2)}) collective-permute-start(bf16[128,768]{1,0:T(8,128)(2,1)S(1)} %get-tuple-element.52), channel_id=1, source_target_pairs={{0,4},{4,0},{8,12},{12,8},{1,5},{5,1},{9,13},{13,9},{2,6},{6,2},{1... | collective-permute-start | bytes 589832 | tf_op jit(solution)/shard_map/ppermute | solution.py:503
  9.8 41.7 %collective-permute-start.15 = (bf16[128,1280]{1,0:T(8,128)(2,1)S(1)}, bf16[128,1280]{1,0:T(8,128)(2,1)S(1)}, u32[]{:S(2)}, u32[]{:S(2)}) collective-permute-start(bf16[128,1280]{1,0:T(8,128)(2,1)S(1)} %get-tuple-element.74), channel_id=1, source_target_pairs={{0,8},{4,12},{8,0},{12,4},{1,9},{5,13},{9,1},{13,5},{2,10},{6,14},... | collective-permute-start | bytes 983048 | tf_op jit(solution)/shard_map/ppermute | solution.py:503
  12.6 39.4 %collective-permute-start.16 = (bf16[128,1280]{1,0:T(8,128)(2,1)S(1)}, bf16[128,1280]{1,0:T(8,128)(2,1)S(1)}, u32[]{:S(2)}, u32[]{:S(2)}) collective-permute-start(bf16[128,1280]{1,0:T(8,128)(2,1)S(1)} %get-tuple-element.75), channel_id=1, source_target_pairs={{0,12},{4,8},{8,4},{12,0},{1,13},{5,9},{9,5},{13,1},{2,14},{6,10},... | collective-permute-start | bytes 983048 | tf_op jit(solution)/shard_map/ppermute | solution.py:503
  12.6 41.8 %collective-permute-start.14 = (bf16[128,1280]{1,0:T(8,128)(2,1)S(1)}, bf16[128,1280]{1,0:T(8,128)(2,1)S(1)}, u32[]{:S(2)}, u32[]{:S(2)}) collective-permute-start(bf16[128,1280]{1,0:T(8,128)(2,1)S(1)} %get-tuple-element.48.after), channel_id=1, source_target_pairs={{0,4},{4,0},{8,12},{12,8},{1,5},{5,1},{9,13},{13,9},{2,6},{6,2},{1... | collective-permute-start | bytes 983048 | tf_op jit(solution)/shard_map/ppermute | solution.py:503
  19.6 30.6 %collective-permute-start.2 = (bf16[128,768]{1,0:T(8,128)(2,1)S(1)}, bf16[128,768]{1,0:T(8,128)(2,1)S(1)}, u32[]{:S(2)}, u32[]{:S(2)}) collective-permute-start(bf16[128,768]{1,0:T(8,128)(2,1)S(1)} %get-tuple-element.53), channel_id=1, source_target_pairs={{0,8},{4,12},{8,0},{12,4},{1,9},{5,13},{9,1},{13,5},{2,10},{6,14},... | collective-permute-start | bytes 589832 | tf_op jit(solution)/shard_map/ppermute | solution.py:503
  50.2 13.5 %collective-permute-start.8 = (bf16[96,2560]{1,0:T(8,128)(2,1)S(1)}, bf16[96,2560]{1,0:T(8,128)(2,1)S(1)}, u32[]{:S(2)}, u32[]{:S(2)}) collective-permute-start(bf16[96,2560]{1,0:T(8,128)(2,1)S(1)} %get-tuple-element.60), channel_id=1, source_target_pairs={{0,3},{1,2},{2,1},{3,0},{4,7},{5,6},{6,5},{7,4},{8,11},{9,10},{10,... | collective-permute-start | bytes 1474568 | tf_op jit(solution)/shard_map/ppermute | solution.py:503
  51.5 42.3 %collective-permute-start = (bf16[96,4608]{1,0:T(8,128)(2,1)S(1)}, bf16[96,4608]{1,0:T(8,128)(2,1)S(1)}, u32[]{:S(2)}, u32[]{:S(2)}) collective-permute-start(bf16[96,4608]{1,0:T(8,128)(2,1)S(1)} %shard_map.68.after), channel_id=1, source_target_pairs={{0,1},{1,0},{2,3},{3,2},{4,5},{5,4},{6,7},{7,6},{8,9},{9,8},{10,11... | collective-permute-start | bytes 2654216 | tf_op jit(solution)/shard_map/ppermute | solution.py:503
  52.0 8.8 %collective-permute-start.3 = (bf16[128,768]{1,0:T(8,128)(2,1)S(1)}, bf16[128,768]{1,0:T(8,128)(2,1)S(1)}, u32[]{:S(2)}, u32[]{:S(2)}) collective-permute-start(bf16[128,768]{1,0:T(8,128)(2,1)S(1)} %get-tuple-element.54), channel_id=1, source_target_pairs={{0,12},{4,8},{8,4},{12,0},{1,13},{5,9},{9,5},{13,1},{2,14},{6,10},... | collective-permute-start | bytes 589832 | tf_op jit(solution)/shard_map/ppermute | solution.py:503
  54.3 19.0 %collective-permute-start.7 = (bf16[96,2560]{1,0:T(8,128)(2,1)S(1)}, bf16[96,2560]{1,0:T(8,128)(2,1)S(1)}, u32[]{:S(2)}, u32[]{:S(2)}) collective-permute-start(bf16[96,2560]{1,0:T(8,128)(2,1)S(1)} %get-tuple-element.49.after), channel_id=1, source_target_pairs={{0,2},{1,3},{2,0},{3,1},{4,6},{5,7},{6,4},{7,5},{8,10},{9,11},{10,... | collective-permute-start | bytes 1474568 | tf_op jit(solution)/shard_map/ppermute | solution.py:503
  60.8 29.3 %collective-permute-start.17 = (bf16[256,1280]{1,0:T(8,128)(2,1)S(1)}, bf16[256,1280]{1,0:T(8,128)(2,1)S(1)}, u32[]{:S(2)}, u32[]{:S(2)}) collective-permute-start(bf16[256,1280]{1,0:T(8,128)(2,1)S(1)} %shard_map.76.kept), channel_id=1, source_target_pairs={{2,0},{3,1},{6,4},{7,5},{10,8},{11,9},{14,12},{15,13},{18,16},{19,... | collective-permute-start | bytes 1966088 | tf_op jit(solution)/shard_map/ppermute | solution.py:503
  63.7 25.9 %collective-permute-start.6 = (bf16[96,1536]{1,0:T(8,128)(2,1)S(1)}, bf16[96,1536]{1,0:T(8,128)(2,1)S(1)}, u32[]{:S(2)}, u32[]{:S(2)}) collective-permute-start(bf16[96,1536]{1,0:T(8,128)(2,1)S(1)} %get-tuple-element.59), channel_id=1, source_target_pairs={{0,3},{1,2},{4,7},{5,6},{8,11},{9,10},{12,15},{13,14},{16,19},{17,... | collective-permute-start | bytes 884744 | tf_op jit(solution)/shard_map/ppermute | solution.py:503
  73.4 29.3 %collective-permute-start.4 = (bf16[256,768]{1,0:T(8,128)(2,1)S(1)}, bf16[256,768]{1,0:T(8,128)(2,1)S(1)}, u32[]{:S(2)}, u32[]{:S(2)}) collective-permute-start(bf16[256,768]{1,0:T(8,128)(2,1)S(1)} %shard_map.71.kept), channel_id=1, source_target_pairs={{2,0},{3,1},{6,4},{7,5},{10,8},{11,9},{14,12},{15,13},{18,16},{19,... | collective-permute-start | bytes 1179656 | tf_op jit(solution)/shard_map/ppermute | solution.py:503
  74.7 19.0 %collective-permute-start.5 = (bf16[96,1536]{1,0:T(8,128)(2,1)S(1)}, bf16[96,1536]{1,0:T(8,128)(2,1)S(1)}, u32[]{:S(2)}, u32[]{:S(2)}) collective-permute-start(bf16[96,1536]{1,0:T(8,128)(2,1)S(1)} %get-tuple-element.50.after), channel_id=1, source_target_pairs={{0,2},{1,3},{4,6},{5,7},{8,10},{9,11},{12,14},{13,15},{16,18},{17,... | collective-permute-start | bytes 884744 | tf_op jit(solution)/shard_map/ppermute | solution.py:503
  89.6 17.7 %collective-permute-start.19 = (f32[96,1408]{1,0:T(8,128)S(1)}, f32[96,1408]{1,0:T(8,128)S(1)}, u32[]{:S(2)}, u32[]{:S(2)}) collective-permute-start(f32[96,1408]{1,0:T(8,128)S(1)} %get-tuple-element.88), channel_id=1, source_target_pairs={{0,1},{1,0},{2,3},{3,2},{4,5},{5,4},{6,7},{7,6},{8,9},{9,8},{10,11... | collective-permute-start | bytes 1622024 | tf_op jit(solution)/shard_map/ppermute | solution.py:503
  90.1 14.4 %collective-permute-start.20 = (bf16[96,1408]{1,0:T(8,128)(2,1)S(1)}, bf16[96,1408]{1,0:T(8,128)(2,1)S(1)}, u32[]{:S(2)}, u32[]{:S(2)}) collective-permute-start(bf16[96,1408]{1,0:T(8,128)(2,1)S(1)} %get-tuple-element.89), channel_id=1, source_target_pairs={{0,2},{1,3},{4,6},{5,7},{8,10},{9,11},{12,14},{13,15},{16,18},{17,... | collective-permute-start | bytes 811016 | tf_op jit(solution)/shard_map/ppermute | solution.py:503
  93.7 9.5 %collective-permute-start.18 = (bf16[96,1280]{1,0:T(8,128)(2,1)S(1)}, bf16[96,1280]{1,0:T(8,128)(2,1)S(1)}, u32[]{:S(2)}, u32[]{:S(2)}) collective-permute-start(bf16[96,1280]{1,0:T(8,128)(2,1)S(1)} %get-tuple-element.83), channel_id=1, source_target_pairs={{0,1},{1,0},{2,3},{3,2},{4,5},{5,4},{6,7},{7,6},{8,9},{9,8},{10,11... | collective-permute-start | bytes 737288 | tf_op jit(solution)/shard_map/ppermute | solution.py:503
  93.8 13.3 %collective-permute-start.21 = (bf16[96,1408]{1,0:T(8,128)(2,1)S(1)}, bf16[96,1408]{1,0:T(8,128)(2,1)S(1)}, u32[]{:S(2)}, u32[]{:S(2)}) collective-permute-start(bf16[96,1408]{1,0:T(8,128)(2,1)S(1)} %get-tuple-element.90), channel_id=1, source_target_pairs={{0,3},{1,2},{4,7},{5,6},{8,11},{9,10},{12,15},{13,14},{16,19},{17,... | collective-permute-start | bytes 811016 | tf_op jit(solution)/shard_map/ppermute | solution.py:503
  102.7 9.6 %collective-permute-start.10 = (f32[96,896]{1,0:T(8,128)S(1)}, f32[96,896]{1,0:T(8,128)S(1)}, u32[]{:S(2)}, u32[]{:S(2)}) collective-permute-start(f32[96,896]{1,0:T(8,128)S(1)} %get-tuple-element.70), channel_id=1, source_target_pairs={{0,1},{1,0},{2,3},{3,2},{4,5},{5,4},{6,7},{7,6},{8,9},{9,8},{10,11... | collective-permute-start | bytes 1032200 | tf_op jit(solution)/shard_map/ppermute | solution.py:503
  103.2 6.0 %collective-permute-start.11 = (bf16[96,896]{1,0:T(8,128)(2,1)S(1)}, bf16[96,896]{1,0:T(8,128)(2,1)S(1)}, u32[]{:S(2)}, u32[]{:S(2)}) collective-permute-start(bf16[96,896]{1,0:T(8,128)(2,1)S(1)} %get-tuple-element.71), channel_id=1, source_target_pairs={{0,2},{1,3},{4,6},{5,7},{8,10},{9,11},{12,14},{13,15},{16,18},{17,... | collective-permute-start | bytes 516104 | tf_op jit(solution)/shard_map/ppermute | solution.py:503
  104.5 7.8 %collective-permute-start.12 = (bf16[96,896]{1,0:T(8,128)(2,1)S(1)}, bf16[96,896]{1,0:T(8,128)(2,1)S(1)}, u32[]{:S(2)}, u32[]{:S(2)}) collective-permute-start(bf16[96,896]{1,0:T(8,128)(2,1)S(1)} %get-tuple-element.72), channel_id=1, source_target_pairs={{0,3},{1,2},{4,7},{5,6},{8,11},{9,10},{12,15},{13,14},{16,19},{17,... | collective-permute-start | bytes 516104 | tf_op jit(solution)/shard_map/ppermute | solution.py:503
  107.1 1.4 %collective-permute-start.9 = (bf16[96,768]{1,0:T(8,128)(2,1)S(1)}, bf16[96,768]{1,0:T(8,128)(2,1)S(1)}, u32[]{:S(2)}, u32[]{:S(2)}) collective-permute-start(bf16[96,768]{1,0:T(8,128)(2,1)S(1)} %get-tuple-element.65), channel_id=1, source_target_pairs={{0,1},{1,0},{2,3},{3,2},{4,5},{5,4},{6,7},{7,6},{8,9},{9,8},{10,11... | collective-permute-start | bytes 442376 | tf_op jit(solution)/shard_map/ppermute | solution.py:503
